TPU v7x, 512 devices: a whole 4x4x16 slice. The times are simulated.
512 devices in a mesh: seq: 64 (over y, z), head: 8 (over x, core).
Axes of the slice: x: 4, y: 4, z: 16, core: 2. Of those that a mesh axis runs over, the one named last changes fastest.
Arguments:
- lengths: int32 [2], replicated, may hold values from 1 to 3571, 5952 in all
- step_index: int32 [2], replicated, may hold values from 20 to 999
- query_act: bfloat16 [6144, 3072], P('seq', 'head'), may hold values from -24 to 24
- key_act: bfloat16 [6144, 3072], P('seq', 'head'), may hold values from -24 to 24
- value_act: bfloat16 [6144, 3072], P('seq', 'head'), may hold values from -6 to 6
- hidden: bfloat16 [6144, 3072], P('seq', 'head'), may hold values from -64 to 64
- attn_weight: bfloat16 [3072, 3072], P('head'), may hold values from -0.4375 to 0.4375
- gate_mod: bfloat16 [2, 3072], P(None, 'head'), may hold values from 0.5 to 2
- shift_mod: bfloat16 [2, 3072], P(None, 'head'), may hold values from -3 to 3
- scale_mod: bfloat16 [2, 3072], P(None, 'head'), may hold values from -0.5 to 0.5
- proj_weight: bfloat16 [3072, 64], P('head'), may hold values from -0.109375 to 0.109375
- latent: float32 [6144, 64], P('seq'), may hold values from -6 to 6
Outputs:
- hidden_out: bfloat16 [6144, 3072], P('seq', 'head')
- clean_estimate: float32 [6144, 64], P('seq')
- latent_prev: float32 [6144, 64], P('seq')
- latent_rim: float32 [5760, 64], P('seq')
Inputs may be any that keep to these rules, and one draw needn't show every extreme that they name: lengths[0] and lengths[1] are laid end to end from slot 0; they sum to 5952 and the larger is at most 3571.
All inputs are finite; a program needn't handle non-finite values.
Results may differ from a plain program's by a relative error of at most 0.008.
Values may be sent and summed in bfloat16 or wider, within the bound.
No kernel may reach another device: no remote copies, remote signals or barrier semaphores. Data moves between devices by JAX's collectives and lax.ppermute only.
A program may use at most 64 MiB of HBM per device.

v0:
```python
import math

import jax
import jax.numpy as jnp
from jax import lax
from jax.sharding import PartitionSpec as P

D = 3072
HD = 64
RIM = 45
TRAIN_STEPS = 1000
STEP_GAP = 20


NEG_BIG = -1e30
EPSILON = 1e-06


def with_halo(value, sides, width):
    for axis, dim in sides:
        size, length = (lax.axis_size(axis), value.shape[dim])
        up = [(i, (i + 1) % size) for i in range(size - 1)]
        down = [(j, i) for i, j in up]
        last = lax.slice_in_dim(value, length - width, length, axis=dim)
        first = lax.slice_in_dim(value, 0, width, axis=dim)
        before = lax.ppermute(last, axis, up)
        after = lax.ppermute(first, axis, down)
        value = jnp.concatenate([before, value, after], axis=dim)
    return value


def alpha_table():
    betas = jnp.linspace(0.00085**0.5, 0.012**0.5, TRAIN_STEPS, dtype=jnp.float32) ** 2
    return jnp.cumprod(1.0 - betas)


def request_of(position, lengths):
    first_len = lengths[0]
    total_len = lengths[0] + lengths[1]
    return jnp.where(
        position < 0, -1, jnp.where(position < first_len, 0, jnp.where(position < total_len, 1, 2))
    ).astype(jnp.int32)


def absorb(carry, queries, query_req, key_rows, value_rows, key_start, lengths):
    key_count = key_rows.shape[0]
    head_count = queries.shape[0]
    head_width = queries.shape[2]
    key_req = request_of(key_start + jnp.arange(key_count, dtype=jnp.int32), lengths)
    allowed = (query_req[:, None] == key_req[None, :]) & (query_req[:, None] < 2)

    def attend(current):
        run_max, run_sum, run_acc = current
        keys_h = key_rows.reshape(key_count, head_count, head_width)
        values_h = value_rows.reshape(key_count, head_count, head_width)
        scores = jnp.einsum(
            "hqd,khd->hqk", queries, keys_h, preferred_element_type=jnp.float32
        ) / math.sqrt(head_width)
        scores = jnp.where(allowed[None], scores, NEG_BIG)
        new_max = jnp.maximum(run_max, jnp.max(scores, axis=2))
        weights = jnp.where(allowed[None], jnp.exp(scores - new_max[:, :, None]), 0.0)
        factor = jnp.exp(run_max - new_max)
        new_sum = run_sum * factor + jnp.sum(weights, axis=2)
        new_acc = run_acc * factor[:, :, None] + jnp.einsum(
            "hqk,khd->hqd",
            weights.astype(jnp.bfloat16),
            values_h,
            preferred_element_type=jnp.float32,
        )
        return (new_max, new_sum, new_acc)

    return lax.cond(jnp.any(allowed), attend, lambda current: current, carry)


def shards(
    lengths,
    step_index,
    query_act,
    key_act,
    value_act,
    hidden,
    attn_weight,
    gate_mod,
    shift_mod,
    scale_mod,
    proj_weight,
    latent,
):
    rows_dev = query_act.shape[0]
    head_count = query_act.shape[1] // HD
    my_index = lax.axis_index("seq")
    positions = my_index * rows_dev + jnp.arange(rows_dev, dtype=jnp.int32)
    query_req = request_of(positions, lengths)
    queries_h = jnp.transpose(query_act.reshape(rows_dev, head_count, HD), (1, 0, 2))
    initial = (
        jnp.full((head_count, rows_dev), NEG_BIG, jnp.float32),
        jnp.zeros((head_count, rows_dev), jnp.float32),
        jnp.zeros((head_count, rows_dev, HD), jnp.float32),
    )
    key_piece = lax.all_gather(key_act, "seq", axis=0, tiled=True)
    value_piece = lax.all_gather(value_act, "seq", axis=0, tiled=True)
    blocks = key_piece.shape[0] // rows_dev

    def one_block(number, current):
        key_rows = lax.dynamic_slice_in_dim(key_piece, number * rows_dev, rows_dev, 0)
        value_rows = lax.dynamic_slice_in_dim(value_piece, number * rows_dev, rows_dev, 0)
        return absorb(
            current, queries_h, query_req, key_rows, value_rows, number * rows_dev, lengths
        )

    final = lax.fori_loop(0, blocks, one_block, initial)
    run_max, run_sum, run_acc = final
    divisor = jnp.where(query_req < 2, run_sum, 1.0)
    attended = run_acc / divisor[:, :, None]
    attended = (
        jnp.transpose(attended, (1, 0, 2)).reshape(rows_dev, head_count * HD).astype(jnp.bfloat16)
    )
    term = jnp.dot(attended, attn_weight, preferred_element_type=jnp.float32)
    projected = lax.psum_scatter(
        term.astype(jnp.bfloat16), "head", scatter_dimension=1, tiled=True
    ).astype(jnp.float32)

    def per_row(table):
        first_row = table[0].astype(jnp.float32)
        second_row = table[1].astype(jnp.float32)
        return jnp.where(
            (query_req == 0)[:, None],
            first_row[None],
            jnp.where((query_req == 1)[:, None], second_row[None], 0.0),
        )

    hidden_out = (hidden.astype(jnp.float32) + per_row(gate_mod) * projected).astype(jnp.bfloat16)
    values_f = hidden_out.astype(jnp.float32)
    total_sum, square_sum = lax.psum(
        (jnp.sum(values_f, axis=1), jnp.sum(values_f * values_f, axis=1)), "head"
    )
    row_mean = total_sum / D
    variance = square_sum / D - row_mean * row_mean
    normed = (values_f - row_mean[:, None]) * lax.rsqrt(variance[:, None] + EPSILON)
    modulated = (normed * (1.0 + per_row(scale_mod)) + per_row(shift_mod)).astype(jnp.bfloat16)
    velocity = lax.psum(jnp.dot(modulated, proj_weight, preferred_element_type=jnp.float32), "head")
    table = alpha_table()
    alpha_now = table[step_index]
    alpha_prev = table[step_index - STEP_GAP]
    now_rows = jnp.where(query_req == 0, alpha_now[0], alpha_now[1])[:, None]
    prev_rows = jnp.where(query_req == 0, alpha_prev[0], alpha_prev[1])[:, None]
    clean = jnp.sqrt(now_rows) * latent - jnp.sqrt(1.0 - now_rows) * velocity
    noise = jnp.sqrt(1.0 - now_rows) * latent + jnp.sqrt(now_rows) * velocity
    stepped = jnp.sqrt(prev_rows) * clean + jnp.sqrt(1.0 - prev_rows) * noise
    live = (query_req < 2)[:, None]
    clean = jnp.where(live, clean, 0.0)
    stepped = jnp.where(live, stepped, 0.0)
    padded = with_halo(stepped, (("seq", 0),), RIM)
    offsets = jnp.arange(RIM, dtype=jnp.int32)
    lower_ok = request_of(my_index * rows_dev - RIM + offsets, lengths) == query_req[0]
    upper_ok = request_of((my_index + 1) * rows_dev + offsets, lengths) == query_req[rows_dev - 1]
    lower_rows = jnp.where(lower_ok[:, None], padded[:RIM], 0.0)
    upper_rows = jnp.where(upper_ok[:, None], padded[RIM + rows_dev :], 0.0)
    rim_rows = jnp.concatenate([lower_rows, upper_rows], axis=0)
    return (hidden_out, clean, stepped, rim_rows)


def solution(mesh):
    in_specs = (
        P(),
        P(),
        P("seq", "head"),
        P("seq", "head"),
        P("seq", "head"),
        P("seq", "head"),
        P("head", None),
        P(None, "head"),
        P(None, "head"),
        P(None, "head"),
        P("head", None),
        P("seq", None),
    )
    out_specs = (P("seq", "head"), P("seq", None), P("seq", None), P("seq", None))
    return jax.shard_map(shards, mesh=mesh, in_specs=in_specs, out_specs=out_specs, check_vma=False)
```

profile of v0, /device:TPU:25, one launch (start us, length us, event | category | flops | bytes accessed | tf_op | source)
XLA Modules:
  0.0 649.6 jit_solution(12525048440479406488)
XLA Ops:
  10.2 1.3 fusion.35
  14.9 1.9 select_sqrt_fusion
  16.8 136.2 %all-gather.3.cloned.1.call-done = bf16[6144,384]{1,0:T(8,128)(2,1)} async-done(((bf16[96,384]{1,0:T(8,128)(2,1)}), bf16[6144,384]{1,0:T(8,128)(2,1)}) %all-gather.3.cloned.1.call-update) | async-done | bytes 4718608 | tf_op jit(solution)/shard_map/all_gather | solution.py:100
  153.0 6.7 %copy.26 = bf16[6144,384]{0,1:T(8,128)(2,1)} copy(bf16[6144,384]{1,0:T(8,128)(2,1)} %all-gather.3.cloned.1.call-done) | data formatting | bytes 9437184
  159.7 138.8 %all-gather.5.cloned.1.call-done = bf16[6144,384]{1,0:T(8,128)(2,1)} async-done(((bf16[96,384]{1,0:T(8,128)(2,1)}), bf16[6144,384]{1,0:T(8,128)(2,1)}) %all-gather.5.cloned.1.call-update) | async-done | bytes 4718608 | tf_op jit(solution)/shard_map/all_gather | solution.py:101
  298.6 6.7 %copy.27 = bf16[6144,384]{0,1:T(8,128)(2,1)} copy(bf16[6144,384]{1,0:T(8,128)(2,1)} %all-gather.5.cloned.1.call-done) | data formatting | bytes 9437184
  305.3 201.6 %while.20 = (s32[]{:T(128)}, f32[6,96]{1,0:T(8,128)S(1)}, f32[6,96]{1,0:T(8,128)S(1)}, f32[6,96,64]{1,2,0:T(8,128)S(1)}, s32[2]{0:T(128)S(1)}, /*index=5*/s32[]{...) while((s32[]{:T(128)}, f32[6,96]{1,0:T(8,128)S(1)}, ...), condition=%wide.region_6.7_spmd.clone.clone, body=%wide.region_0.6_spmd.clone.clone.sunk | while | flops 14757414 | bytes 1550341 | solution.py:111
  363.5 1.8 conditional.4
  363.5 1.2 constant_dynamic-slice_fusion
  367.4 1.8 conditional.4
  367.4 1.2 constant_dynamic-slice_fusion
  371.3 1.8 conditional.4
  371.4 1.2 constant_dynamic-slice_fusion
  375.3 1.8 conditional.4
  375.3 1.2 constant_dynamic-slice_fusion
  379.2 1.8 conditional.4
  379.2 1.2 constant_dynamic-slice_fusion
  383.1 1.8 conditional.4
  387.0 1.8 conditional.4
  391.0 1.8 conditional.4
  394.9 1.8 conditional.4
  394.9 1.2 constant_dynamic-slice_fusion
  398.8 1.8 conditional.4
  402.7 1.8 conditional.4
  402.7 1.2 constant_dynamic-slice_fusion
  406.6 1.8 conditional.4
  410.6 1.8 conditional.4
  414.5 1.8 conditional.4
  414.5 1.2 constant_dynamic-slice_fusion
  418.4 1.8 conditional.4
  418.4 1.2 constant_dynamic-slice_fusion
  422.3 1.8 conditional.4
  422.4 1.2 constant_dynamic-slice_fusion
  426.3 1.8 conditional.4
  426.3 1.2 constant_dynamic-slice_fusion
  430.2 1.8 conditional.4
  430.2 1.2 constant_dynamic-slice_fusion
  434.1 1.8 conditional.4
  434.1 1.2 constant_dynamic-slice_fusion
  438.0 1.8 conditional.4
  441.9 1.8 conditional.4
  445.9 1.8 conditional.4
  449.8 1.8 conditional.4
  453.7 1.8 conditional.4
  457.6 1.8 conditional.4
  461.6 1.8 conditional.4
  465.5 1.8 conditional.4
  469.4 1.8 conditional.4
  473.3 1.8 conditional.4
  477.2 1.8 conditional.4
  481.2 1.8 conditional.4
  485.1 1.8 conditional.4
  489.0 1.8 conditional.4
  492.9 1.8 conditional.4
  496.9 1.8 conditional.4
  500.8 1.8 conditional.4
  507.6 1.2 copy.29
  510.7 2.6 subtract_sqrt_fusion
  513.3 79.8 %reduce-scatter.4.cloned.1.call-done = bf16[384,96]{1,0:T(8,128)(2,1)} async-done(((bf16[3072,96]{1,0:T(8,128)(2,1)}), bf16[384,96]{1,0:T(8,128)(2,1)}) %reduce-scatter.4.cloned.1.call-update) | async-done | bytes 73744
  594.3 15.1 %all-reduce.1 = (f32[96]{0:T(128)S(1)}, f32[96]{0:T(128)S(1)}) all-reduce(f32[96]{0:T(128)S(1)} %get-tuple-element.387, f32[96]{0:T(128)S(1)} %get-tuple-element.386), channel_id=1, replica_groups=mesh['seq'=64,'head'=8] {'head'}, use_global_device_ids=true, to_apply=%region_13.14 | all-reduce | flops 192 | bytes 1536 | tf_op jit(solution)/shard_map/psum | solution.py:134
  609.7 21.1 %psum.23 = f32[96,64]{0,1:T(8,128)S(1)} all-reduce(f32[96,64]{0,1:T(8,128)S(1)} %fusion.17), channel_id=1, replica_groups=mesh['seq'=64,'head'=8] {'head'}, use_global_device_ids=true, to_apply=%region_14.15 | all-reduce | flops 6144 | bytes 49152 | tf_op jit(solution)/shard_map/psum | solution.py:141
  631.5 3.2 collective-permute-start
  634.8 1.9 fusion.26
  636.6 4.7 collective-permute-start.1
  (522 shorter events, 152.1 us)
Async XLA Ops:
  7.2 499.9 %copy-start = (bf16[384,3072]{1,0:T(8,128)(2,1)S(1)}, bf16[384,3072]{1,0:T(8,128)(2,1)}, u32[]{:S(2)}) copy-start(bf16[384,3072]{1,0:T(8,128)(2,1)} %param.22) | copy-start | bytes 7077892
  7.2 145.8 %all-gather.3.cloned.1.call-start = ((), (), s32[]{:S(2)}) async-start(), calls=%async_computation.1 | async-start | bytes 4792320 | tf_op jit(solution)/shard_map/all_gather | solution.py:100
  7.9 290.6 %all-gather.5.cloned.1.call-start = ((), (), s32[]{:S(2)}) async-start(), calls=%async_computation.2 | async-start | bytes 4792320 | tf_op jit(solution)/shard_map/all_gather | solution.py:101
  8.7 584.4 %reduce-scatter.4.cloned.1.call-start = ((), (), s32[]{:S(2)}) async-start(), calls=%async_computation.3 | async-start | bytes 884736
  159.7 145.5 %copy-start.5 = (s32[2]{0:T(128)S(1)}, s32[2]{0:T(128)}, u32[]{:S(2)}) copy-start(s32[2]{0:T(128)} %param.16) | copy-start | bytes 28
  506.9 3.8 copy-start.6
  506.9 3.8 copy-start.7
  506.9 3.8 copy-start.8
  506.9 87.2 %copy-start.2 = (bf16[96,384]{1,0:T(8,128)(2,1)S(1)}, bf16[96,384]{1,0:T(8,128)(2,1)}, u32[]{:S(2)}) copy-start(bf16[96,384]{1,0:T(8,128)(2,1)} %param.21) | copy-start | bytes 221188
  506.9 102.5 %copy-start.9 = (bf16[384,64]{0,1:T(8,128)(2,1)S(1)}, bf16[384,64]{0,1:T(8,128)(2,1)}, u32[]{:S(2)}) copy-start(bf16[384,64]{0,1:T(8,128)(2,1)} %param.26) | copy-start | bytes 147460
  507.0 123.9 %copy-start.4 = (f32[96,64]{0,1:T(8,128)S(1)}, f32[96,64]{0,1:T(8,128)}, u32[]{:S(2)}) copy-start(f32[96,64]{0,1:T(8,128)} %param.27) | copy-start | bytes 73732
  594.3 48.7 %copy-start.3 = (bf16[96,384]{1,0:T(8,128)(2,1)}, bf16[96,384]{1,0:T(8,128)(2,1)S(1)}, u32[]{:S(2)}) copy-start(bf16[96,384]{1,0:T(8,128)(2,1)S(1)} %get-tuple-element.424) | copy-start | bytes 221188
  631.4 11.6 %copy-start.1 = (f32[96,64]{0,1:T(8,128)}, f32[96,64]{0,1:T(8,128)S(1)}, u32[]{:S(2)}) copy-start(f32[96,64]{0,1:T(8,128)S(1)} %get-tuple-element.431) | copy-start | bytes 73732
  631.5 9.8 %collective-permute-start = (f32[45,64]{0,1:T(8,128)S(1)}, f32[45,64]{0,1:T(8,128)S(1)}, u32[]{:S(2)}, u32[]{:S(2)}) collective-permute-start(f32[45,64]{0,1:T(8,128)S(1)} %get-tuple-element.433), channel_id=1, source_target_pairs={{0,8},{8,16},{16,24},{24,32},{32,40},{40,48},{48,56},{56,64},{64,7... | collective-permute-start | bytes 34568 | tf_op jit(solution)/shard_map/ppermute | solution.py:26
  636.6 5.7 collective-permute-start.1
Sparse Core Ops, SparseCore 0:
  11.0 142.0 all-gather.2
  156.0 142.5 all-gather.4
  508.9 84.1 reduce-scatter.3
where the time goes:
time: 657 us; the launch traced here: 650 us
  waiting for transfers between devices  357 us (54%)
  other arithmetic  106 us (16%)
  local copies, waits for them, and re-layouts  62.8 us (10%)
  loops' own time  46.5 us (7%)
  blocking collectives  36.2 us (6%)
  matrix products  17.4 us (3%)
  between operations  15.3 us (2%)
  starting transfers between devices  8.03 us (1%)
    all_gather x1, waiting for transfers between devices, shards(): value_piece = lax.all_gather(value_act, 'seq', axis=0, tiled=True)  139 us
    all_gather x1, waiting for transfers between devices, shards(): key_piece = lax.all_gather(key_act, 'seq', axis=0, tiled=True)  136 us
    unnamed x4, waiting for transfers between devices  81.2 us
    and x64, other arithmetic, absorb(): (query_req[:, None] == key_req[None, :]) & (query_req[:, None] < 2)  50.2 us
    another operation x1, loops' own time, shards(): final = lax.fori_loop(0, blocks, one_block, initial)  43.5 us
    dynamic_slice x36, local copies, waits for them, and re-layouts, one_block(): lax.dynamic_slice_in_dim(value_piece, number * rows_dev, rows_dev, 0)  41.5 us
    lt x64, other arithmetic, absorb(): query_req[:, None] < 2  41 us
    psum x1, blocking collectives, shards(): lax.psum(jnp.dot(modulated, proj_weight, preferred_element_type=jnp.float...  21.1 us
  transfers between devices with their start and end apart: 5, of which 4 were waited for; matrix products, arithmetic and copies ran while one was open for 3% of the time, Pallas kernels for 0%

commit v1 on v0

v1 whole, which is shorter than its diff:
```python
import jax
import jax.numpy as jnp
import numpy as np
from jax import lax
from jax.experimental import pallas as pl
from jax.experimental.pallas import tpu as pltpu
from jax.sharding import Mesh
from jax.sharding import PartitionSpec as P

D = 3072
HD = 64
RIM = 45
TOK = 96
HALF = 48
LEN_ALL = 5952
TRAIN_STEPS = 1000
STEP_GAP = 20
NY, NZ, NX, NC = 4, 16, 4, 2
NHEAD = 8
EPSILON = 1e-06
MASKED = -1e30
FLOOR = -0.5e30
HEAD_OF = (0, 0, 0, 1, 1, 1, 2, 2, 2, 3, 3, 3, 4, 4, 5, 5)
PART_OF = (0, 1, 2, 0, 1, 2, 0, 1, 2, 0, 1, 2, 0, 1, 0, 1)
SIZE_OF = (32,) * 12 + (48,) * 4
BF = jnp.bfloat16
F32 = jnp.float32
SMEM = pltpu.SMEM
VMEM = pltpu.VMEM


def low_lanes(rows):
    return lax.broadcasted_iota(jnp.int32, (rows, 128), 1) < HD


def swap(x):
    return pltpu.roll(x, HD, 1)


def pack_kernel(q_ref, k_ref, v_ref, out_ref):
    low_h, low_t = low_lanes(HALF), low_lanes(TOK)
    for pair in range(3):
        lanes = slice(128 * pair, 128 * pair + 128)
        q = q_ref[:, lanes].astype(F32) * 0.125
        k = k_ref[:, lanes].astype(F32)
        v = v_ref[:, lanes].astype(F32)
        top, bottom = q[:HALF], q[HALF:]
        queries = (jnp.where(low_h, top, swap(bottom)), jnp.where(low_h, swap(top), bottom))
        keyvals = (jnp.where(low_t, k, swap(v)), jnp.where(low_t, swap(k), v))
        for side in range(2):
            qh = queries[side].astype(BF)
            kvh = keyvals[side].astype(BF)
            for d in range(NZ):
                if HEAD_OF[d] != 2 * pair + side:
                    continue
                size = SIZE_OF[d]
                start = PART_OF[d] * size
                out_ref[d, :HALF, :] = qh
                out_ref[d, HALF : HALF + size, :] = kvh[start : start + size]
                if size < HALF:
                    out_ref[d, HALF + size :, :] = jnp.zeros((HALF - size, 128), BF)


def pieces(x):
    hi = x.astype(BF).astype(F32)
    rest = x - hi
    mid = rest.astype(BF).astype(F32)
    return (hi, mid, rest - mid)


QT = 192
KT = 768


def attend_kernel(scal_ref, q_ref, kv_ref, out_ref, klo_ref, khi_ref, vlo_ref, vhi_ref):
    first_len, row, size, offset = scal_ref[0], scal_ref[1], scal_ref[2], scal_ref[3]
    low = low_lanes(KT)
    lane = lax.broadcasted_iota(jnp.int32, (KT, 128), 1)
    for j in range(NY):
        kv = kv_ref[j * KT : (j + 1) * KT, :].astype(F32)
        other = swap(kv)
        shape = (NZ, HALF, 128)
        slot = lax.broadcasted_iota(jnp.int32, shape, 1)
        pos = (lax.broadcasted_iota(jnp.int32, shape, 0) + j * NZ) * TOK + slot + offset
        pos = jnp.where(slot < size, pos, LEN_ALL).reshape(KT, 128)
        own = jnp.where(pos < first_len, 0, jnp.where(pos < LEN_ALL, 1, -1))
        lo_mask = jnp.where((lane < 3) & (lane != own), MASKED, 0.0).astype(BF)
        hi_mask = jnp.where((lane >= 3) & (lane < 6) & (lane - 3 != own), MASKED, 0.0).astype(BF)
        rows = slice(j * KT, (j + 1) * KT)
        klo_ref[rows, :128] = jnp.where(low, kv, 0.0).astype(BF)
        khi_ref[rows, :128] = jnp.where(low, 0.0, other).astype(BF)
        klo_ref[rows, 128:] = lo_mask
        khi_ref[rows, 128:] = hi_mask
        vlo_ref[rows, :] = jnp.where(low, other, 0.0).astype(BF)
        vhi_ref[rows, :] = jnp.where(low, 0.0, kv).astype(BF)

    low_q = low_lanes(QT)
    lane_q = lax.broadcasted_iota(jnp.int32, (QT, 128), 1)
    blocks = QT // HALF
    eye = (
        lax.broadcasted_iota(jnp.int32, (HALF, 128), 0)
        == lax.broadcasted_iota(jnp.int32, (HALF, 128), 1)
    ).astype(BF)

    def tile(t, carry):
        q = q_ref[pl.ds(t * blocks, blocks), :HALF, :].reshape(QT, 128)
        shape = (blocks, HALF, 128)
        base = (lax.broadcasted_iota(jnp.int32, shape, 0) + row * NZ + t * blocks) * TOK
        pos = (base + lax.broadcasted_iota(jnp.int32, shape, 1)).reshape(QT, 128)
        pos = jnp.where(lane_q < 3, pos, pos + HALF)
        own = jnp.where(pos < first_len, 0, jnp.where(pos < LEN_ALL, 1, 2))
        own = jnp.where(lane_q < 3, own, own + 3)
        q_all = jnp.concatenate([q, jnp.where(lane_q == own, 1.0, 0.0).astype(BF)], axis=1)

        def scores(keys):
            return lax.dot_general(
                q_all, keys, (((1,), (1,)), ((), ())), preferred_element_type=F32
            )

        def soft(k_ref):
            s = scores(k_ref[...])
            m = jnp.maximum(jnp.max(s, axis=1, keepdims=True), FLOOR)
            p = jnp.exp(s - m)
            return m, jnp.sum(p, axis=1, keepdims=True), p.astype(BF)

        m_lo, l_lo, p_lo = soft(klo_ref)
        acc = jnp.dot(p_lo, vlo_ref[...], preferred_element_type=F32)
        m_hi, l_hi, p_hi = soft(khi_ref)
        acc += jnp.dot(p_hi, vhi_ref[...], preferred_element_type=F32)
        div_lo = jnp.where(l_lo > 0.0, l_lo, 1.0)
        div_hi = jnp.where(l_hi > 0.0, l_hi, 1.0)
        out = (acc / jnp.where(low_q, div_lo, div_hi)).astype(BF)
        stats = jnp.zeros((QT, 128), F32)
        number = 0
        for value in (m_lo, l_lo, m_hi, l_hi):
            for piece in pieces(value):
                stats = jnp.where(lane_q == number, piece, stats)
                number += 1
        stats = stats.astype(BF)
        for b in range(blocks):
            rows = slice(b * HALF, (b + 1) * HALF)
            out_ref[t * blocks + b, :HALF, :] = out[rows]
            turned = lax.dot_general(
                stats[rows], eye, (((0,), (0,)), ((), ())), preferred_element_type=F32
            )
            out_ref[t * blocks + b, HALF:, :] = turned[:16].astype(BF)
        return carry

    lax.fori_loop(0, NZ * HALF // QT, tile, 0)


def merge_kernel(part_ref, w_ref, out_ref, att_ref):
    @pl.when(pl.program_id(0) == 0)
    def _():
        low = low_lanes(HALF)
        rows16 = lax.broadcasted_iota(jnp.int32, (16, 128), 0)
        lanes16 = lax.broadcasted_iota(jnp.int32, (16, 128), 1)
        eye = (rows16 == lanes16).astype(BF)
        stats = []
        for d in range(NZ):
            turned = lax.dot_general(
                part_ref[d, HALF:, :], eye, (((0,), (0,)), ((), ())), preferred_element_type=F32
            )[:HALF]
            cols = [turned[:, i : i + 1] for i in range(12)]
            stats.append([cols[3 * i] + cols[3 * i + 1] + cols[3 * i + 2] for i in range(4)])
        heads = []
        for h in range(6):
            devices = [d for d in range(NZ) if HEAD_OF[d] == h]
            shares = []
            for side in range(2):
                tops = [stats[d][2 * side] for d in devices]
                sums = [stats[d][2 * side + 1] for d in devices]
                top = tops[0]
                for m in tops[1:]:
                    top = jnp.maximum(top, m)
                scaled = [jnp.exp(m - top) * s for m, s in zip(tops, sums)]
                total = scaled[0]
                for s in scaled[1:]:
                    total = total + s
                total = jnp.where(total > 0.0, total, 1.0)
                shares.append([s / total for s in scaled])
            mixed = jnp.zeros((HALF, 128), F32)
            for i, d in enumerate(devices):
                weight = jnp.where(low, shares[0][i], shares[1][i])
                mixed += weight * part_ref[d, :HALF, :].astype(F32)
            heads.append(mixed)
        for pair in range(3):
            even, odd = heads[2 * pair], heads[2 * pair + 1]
            lanes = slice(128 * pair, 128 * pair + 128)
            att_ref[:HALF, lanes] = jnp.where(low, even, swap(odd)).astype(BF)
            att_ref[HALF:, lanes] = jnp.where(low, swap(even), odd).astype(BF)

    out_ref[0] = jnp.dot(att_ref[...], w_ref[...], preferred_element_type=F32).astype(BF)


def split2(x):
    hi = x.astype(BF)
    return hi, (x - hi.astype(F32)).astype(BF)


def stream_kernel(
    scal_ref, term_ref, hid_ref, gate_ref, shift_ref, scale_ref, w_ref, hid_out, msg_ref
):
    first_len, base = scal_ref[0], scal_ref[4]
    projected = term_ref[0].astype(F32)
    for j in range(1, NHEAD):
        projected += term_ref[j].astype(F32)
    pos = base + lax.broadcasted_iota(jnp.int32, (TOK, 384), 0)
    first, second = pos < first_len, pos < LEN_ALL

    def per_row(table_ref):
        table = table_ref[...].astype(F32)
        return jnp.where(first, table[0:1], jnp.where(second, table[1:2], 0.0))

    x = (hid_ref[...].astype(F32) + per_row(gate_ref) * projected).astype(BF)
    hid_out[...] = x
    xf = x.astype(F32)
    total = jnp.sum(xf, axis=1, keepdims=True)
    squares = jnp.sum(xf * xf, axis=1, keepdims=True)
    x_hi, x_lo = split2(xf * (1.0 + per_row(scale_ref)))
    factor = 1.0 + scale_ref[...].astype(F32)
    f_hi, f_lo = split2(factor)
    small = jnp.concatenate(
        [f_hi.astype(F32), f_lo.astype(F32), shift_ref[...].astype(F32), jnp.zeros((10, 384), F32)], axis=0
    ).astype(BF)
    w = jnp.concatenate([w_ref[...], jnp.zeros((384, 64), BF)], axis=1)
    a = jnp.dot(x_hi, w, preferred_element_type=F32) + jnp.dot(x_lo, w, preferred_element_type=F32)
    lane = lax.broadcasted_iota(jnp.int32, (TOK, 128), 1)
    a = jnp.where(lane == 64, total, jnp.where(lane == 65, squares, a))
    b = jnp.dot(small, w, preferred_element_type=F32)
    rows8 = lax.broadcasted_iota(jnp.int32, (8, 128), 0)
    tail = jnp.where(
        rows8 == 0,
        b[0:1] + b[2:3],
        jnp.where(
            rows8 == 1,
            b[1:2] + b[3:4],
            jnp.where(rows8 == 2, b[4:5], jnp.where(rows8 == 3, b[5:6], 0.0)),
        ),
    )
    for j in range(NHEAD):
        msg_ref[j, :TOK, :] = a
        msg_ref[j, TOK:, :] = tail


def step_kernel(scal_ref, coef_ref, msg_ref, lat_ref, clean_ref, prev_ref, rim_ref):
    first_len, base, core = scal_ref[0], scal_ref[4], scal_ref[5]
    total = msg_ref[0]
    for j in range(1, NHEAD):
        total += msg_ref[j]
    pos = base + lax.broadcasted_iota(jnp.int32, (TOK, 128), 0)
    first, live = pos < first_len, pos < LEN_ALL
    mean = total[:TOK, 64:65] * (1.0 / D)
    var = total[:TOK, 65:66] * (1.0 / D) - mean * mean
    scale_w = jnp.where(first, total[TOK : TOK + 1], total[TOK + 1 : TOK + 2])
    shift_w = jnp.where(first, total[TOK + 2 : TOK + 3], total[TOK + 3 : TOK + 4])
    velocity = lax.rsqrt(var + EPSILON) * (total[:TOK] - mean * scale_w) + shift_w
    velocity = velocity[:, :64]
    first, live = first[:, :64], live[:, :64]
    latent = lat_ref[...]

    def row_coef(i):
        return jnp.where(first, coef_ref[2 * i], coef_ref[2 * i + 1])

    root_a, root_1a, root_q, root_1q = (row_coef(i) for i in range(4))
    clean = root_a * latent - root_1a * velocity
    noise = root_1a * latent + root_a * velocity
    stepped = root_q * clean + root_1q * noise
    stepped = jnp.where(live, stepped, 0.0)
    clean_ref[...] = jnp.where(live, clean, 0.0)
    prev_ref[...] = stepped
    rim_ref[...] = jnp.where(core == 0, stepped[HALF:], stepped[:HALF])


def alpha_table():
    betas = np.linspace(0.00085**0.5, 0.012**0.5, TRAIN_STEPS) ** 2
    return np.cumprod(1.0 - betas).astype(np.float32)


def request_of(position, first_len):
    return jnp.where(
        position < 0, -1, jnp.where(position < first_len, 0, jnp.where(position < LEN_ALL, 1, 2))
    )


def whole(*shape):
    return pl.BlockSpec(shape, lambda *_: (0,) * len(shape))


def shards(
    lengths,
    step_index,
    query_act,
    key_act,
    value_act,
    hidden,
    attn_weight,
    gate_mod,
    shift_mod,
    scale_mod,
    proj_weight,
    latent,
):
    z = lax.axis_index("z")
    y = lax.axis_index("y")
    core = lax.axis_index("core")
    seq = y * NZ + z
    first_len = lengths[0]
    size = jnp.where(z < 12, 32, 48)
    part = jnp.where(z < 12, z % 3, z % 2)
    scal = jnp.stack(
        [first_len, y, size, part * size, seq * TOK, core, z, seq * 0]
    ).astype(jnp.int32)
    in_smem = pl.BlockSpec(memory_space=SMEM)
    big = pltpu.CompilerParams(vmem_limit_bytes=48 * 1024 * 1024)

    packed = pl.pallas_call(
        pack_kernel, out_shape=jax.ShapeDtypeStruct((NZ, TOK, 128), BF), name="pack"
    )(query_act, key_act, value_act)
    mine = lax.all_to_all(packed, "z", 0, 0, tiled=True)
    kv = lax.all_gather(mine[:, HALF:, :].reshape(NZ * HALF, 128), "y", axis=0, tiled=True)
    partial = pl.pallas_call(
        attend_kernel,
        out_shape=jax.ShapeDtypeStruct((NZ, 64, 128), BF),
        in_specs=[in_smem, pl.BlockSpec(memory_space=VMEM), pl.BlockSpec(memory_space=VMEM)],
        out_specs=pl.BlockSpec(memory_space=VMEM),
        scratch_shapes=[
            VMEM((NY * KT, 256), BF),
            VMEM((NY * KT, 256), BF),
            VMEM((NY * KT, 128), BF),
            VMEM((NY * KT, 128), BF),
        ],
        compiler_params=big,
        name="attend",
    )(scal, mine, kv)
    parts = lax.all_to_all(partial, "z", 0, 0, tiled=True)
    term = pl.pallas_call(
        merge_kernel,
        grid=(NHEAD,),
        out_shape=jax.ShapeDtypeStruct((NHEAD, TOK, 384), BF),
        in_specs=[whole(NZ, 64, 128), pl.BlockSpec((384, 384), lambda j: (0, j))],
        out_specs=pl.BlockSpec((1, TOK, 384), lambda j: (j, 0, 0)),
        scratch_shapes=[VMEM((TOK, 384), BF)],
        name="merge",
    )(parts, attn_weight)
    terms = lax.all_to_all(term, ("x", "core"), 0, 0, tiled=True)
    hidden_out, message = pl.pallas_call(
        stream_kernel,
        out_shape=(
            jax.ShapeDtypeStruct((TOK, 384), BF),
            jax.ShapeDtypeStruct((NHEAD, TOK + 8, 128), F32),
        ),
        in_specs=[in_smem] + [pl.BlockSpec(memory_space=VMEM)] * 6,
        name="stream",
    )(scal, terms, hidden, gate_mod, shift_mod, scale_mod, proj_weight)
    message = lax.all_to_all(message, ("x", "core"), 0, 0, tiled=True)
    table = jnp.asarray(alpha_table())
    alpha_now = table[step_index]
    alpha_prev = table[step_index - STEP_GAP]
    coef = jnp.concatenate(
        [
            jnp.sqrt(alpha_now),
            jnp.sqrt(1.0 - alpha_now),
            jnp.sqrt(alpha_prev),
            jnp.sqrt(1.0 - alpha_prev),
        ]
    )
    clean, stepped, rim = pl.pallas_call(
        step_kernel,
        out_shape=(
            jax.ShapeDtypeStruct((TOK, 64), F32),
            jax.ShapeDtypeStruct((TOK, 64), F32),
            jax.ShapeDtypeStruct((HALF, 64), F32),
        ),
        in_specs=[in_smem, in_smem] + [pl.BlockSpec(memory_space=VMEM)] * 2,
        name="ddim",
    )(scal, coef, message, latent)
    pairs = []
    for s in range(NY * NZ):
        for x in range(NX):
            up, down = (s * NX + x) * NC, (s * NX + x) * NC + 1
            if s + 1 < NY * NZ:
                pairs.append((up, up + NX * NC))
            if s > 0:
                pairs.append((down, down - NX * NC))
    got = lax.ppermute(rim, ("y", "z", "x", "core"), pairs)
    both = lax.all_gather(got, "core")
    offsets = jnp.arange(RIM, dtype=jnp.int32)
    start = seq * TOK
    lower_ok = request_of(start - RIM + offsets, first_len) == request_of(start, first_len)
    upper_ok = request_of(start + TOK + offsets, first_len) == request_of(
        start + TOK - 1, first_len
    )
    lower_ok &= start > 0
    upper_ok &= start + TOK < NY * NZ * TOK
    rims = jnp.concatenate(
        [
            jnp.where(lower_ok[:, None], both[0, HALF - RIM :], 0.0),
            jnp.where(upper_ok[:, None], both[1, :RIM], 0.0),
        ],
        axis=0,
    )
    return hidden_out, clean, stepped, rims


def solution(mesh):
    grid = Mesh(mesh.devices.reshape(NY, NZ, NX, NC), ("y", "z", "x", "core"))
    seq, head = ("y", "z"), ("x", "core")
    in_specs = (
        P(),
        P(),
        P(seq, head),
        P(seq, head),
        P(seq, head),
        P(seq, head),
        P(head, None),
        P(None, head),
        P(None, head),
        P(None, head),
        P(head, None),
        P(seq, None),
    )
    out_specs = (P(seq, head), P(seq, None), P(seq, None), P(seq, None))
    return jax.shard_map(shards, mesh=grid, in_specs=in_specs, out_specs=out_specs, check_vma=False)
```

time: 657 us -> 145 us (0.22)
  waiting for transfers between devices: 357 us -> 32.4 us
  other arithmetic: 106 us -> 1.37 us
  local copies, waits for them, and re-layouts: 62.8 us -> 8.23 us
  loops' own time: 46.5 us -> 0 us
  starting transfers between devices: 8.03 us -> 34.9 us
  Pallas kernels: 0 us -> 26.3 us
  matrix products: 17.4 us -> 0 us
  between operations: 15.3 us -> 0.85 us
    all_gather x2 -> x0, waiting for transfers between devices: 275 us -> none  [the longest x1 139 us: shards(): value_piece = lax.all_gather(value_act, 'seq', axis=0, tiled=True)]
    unnamed x4 -> x0, waiting for transfers between devices: 81.2 us -> none
    and x64 -> x1, other arithmetic: 50.2 us -> 0.04 us  [shards(): upper_ok &= start + TOK < NY * NZ * TOK]
    another operation x65 -> x0, loops' own time: 46.5 us -> none  [the longest x1 43.5 us: shards(): final = lax.fori_loop(0, blocks, one_block, initial)]
    dynamic_slice x36 -> x0, local copies, waits for them, and re-layouts: 41.5 us -> none  [one_block(): lax.dynamic_slice_in_dim(value_piece, number * rows_dev, rows_dev, 0)]
    lt x64 -> x0, other arithmetic: 41 us -> none  [absorb(): query_req[:, None] < 2]
    psum x2 -> x0, blocking collectives: 36.2 us -> none  [the longest x1 21.1 us: shards(): lax.psum(jnp.dot(modulated, proj_weight, preferred_element_type=jnp.float...]
    all_to_all x0 -> x3, waiting for transfers between devices: none -> 32.4 us  [the longest x1 17.2 us: shards(): mine = lax.all_to_all(packed, 'z', 0, 0, tiled=True)]
  transfers between devices with their start and end apart: 5 -> 4, of which waited for: 4 -> 3; matrix products, arithmetic and copies ran while one was open for 3% -> 5% of each run, Pallas kernels for 0% -> 0%
where the time goes in v1:
time: 145 us; the launch traced here: 143 us
  blocking collectives  39.4 us (27%)
  starting transfers between devices  34.9 us (24%)
  waiting for transfers between devices  32.4 us (22%)
  Pallas kernels  26.3 us (18%)
  local copies, waits for them, and re-layouts  8.23 us (6%)
    all_to_all x1, blocking collectives, shards(): parts = lax.all_to_all(partial, 'z', 0, 0, tiled=True)  24.1 us
    all_to_all x1, waiting for transfers between devices, shards(): mine = lax.all_to_all(packed, 'z', 0, 0, tiled=True)  17.2 us
    all_to_all x1, starting transfers between devices, shards(): mine = lax.all_to_all(packed, 'z', 0, 0, tiled=True)  14.9 us
    all_to_all x1, starting transfers between devices, shards(): terms = lax.all_to_all(term, ('x', 'core'), 0, 0, tiled=True)  12.9 us
    pallas_call x1, Pallas kernels, shards(): pl.pallas_call(attend_kernel, out_shape=jax.ShapeDtypeStruct((NZ, 64, 128...  12.7 us
    all_gather x1, blocking collectives, shards(): lax.all_gather(mine[:, HALF:, :].reshape(NZ * HALF, 128), 'y', axis=0, ti...  10.7 us
    all_to_all x1, waiting for transfers between devices, shards(): terms = lax.all_to_all(term, ('x', 'core'), 0, 0, tiled=True)  8.77 us
    pallas_call x1, Pallas kernels, shards(): pl.pallas_call(merge_kernel, grid=(NHEAD,), out_shape=jax.ShapeDtypeStruc...  7.58 us
  transfers between devices with their start and end apart: 4, of which 3 were waited for; matrix products, arithmetic and copies ran while one was open for 5% of the time, Pallas kernels for 0%

profile of v1, /device:TPU:25, one launch (start us, length us, event | category | flops | bytes accessed | tf_op | source)
XLA Modules:
  0.0 143.4 jit_solution(6786254115124803150)
XLA Ops:
  0.6 1.8 %pack.1 = bf16[16,96,128]{2,1,0:T(8,128)(2,1)} custom-call(bf16[96,384]{1,0:T(8,128)(2,1)} %q_ref.1, bf16[96,384]{1,0:T(8,128)(2,1)} %k_ref.1, bf16[96,384]{1,0:T(8,128)(2,1)} %v_ref.1), custom_call_target="tpu_custom_call" | custom-call | tf_op jit(solution)/shard_map/pack/pallas_call | solution.py:317
  2.5 14.9 %all-to-all-start = ((bf16[16,96,128]{2,1,0:T(8,128)(2,1)}), bf16[16,96,128]{2,1,0:T(8,128)(2,1)S(1)}, u32[]{:S(2)}, u32[]{:S(2)}) async-start(bf16[16,96,128]{2,1,0:T(8,128)(2,1)} %pack.1), calls=%async_computation | async-start | bytes 786432 | tf_op jit(solution)/shard_map/all_to_all | solution.py:320
  17.4 0.7 stack.27.scal_ref
  18.2 0.0 copy-start
  18.2 17.2 %all-to-all-done.q_ref = bf16[16,96,128]{2,1,0:T(8,128)(2,1)S(1)} async-done(((bf16[16,96,128]{2,1,0:T(8,128)(2,1)}), bf16[16,96,128]{2,1,0:T(8,128)(2,1)S(1)}, u32[]{:S(2)}, u32[]{:S(2)}) %all-to-all-start) | async-done | bytes 393248 | tf_op jit(solution)/shard_map/all_to_all | solution.py:320
  35.4 10.7 %all_gather.9.kv_ref = bf16[3072,128]{1,0:T(8,128)(2,1)S(1)} all-gather(bf16[768,128]{1,0:T(8,128)(2,1)S(1)} %bitcast.14), channel_id=1, replica_groups=mesh['y'=4,'z'=16,'x'=4,'core'=2] {'y'}, dimensions={0}, use_global_device_ids=true | all-gather | bytes 983040 | tf_op jit(solution)/shard_map/all_gather | solution.py:321
  46.1 12.7 %attend.1 = bf16[16,64,128]{2,1,0:T(8,128)(2,1)S(1)} custom-call(s32[8]{0:T(128)S(1)} %stack.27.scal_ref, bf16[16,96,128]{2,1,0:T(8,128)(2,1)S(1)} %all-to-all-done.q_ref, bf16[3072,128]{1,0:T(8,128)(2,1)S(1)} %all_gather.9.kv_ref), custom_call_target="tpu_custom_call" | custom-call | tf_op jit(solution)/shard_map/attend/pallas_call | solution.py:322
  58.9 0.0 copy-start.4
  58.9 24.1 %all_to_all.20.part_ref = bf16[16,64,128]{2,1,0:T(8,128)(2,1)} all-to-all(bf16[16,64,128]{2,1,0:T(8,128)(2,1)S(1)} %attend.1), channel_id=1, replica_groups=mesh['y'=4,'z'=16,'x'=4,'core'=2] {'z'}, dimensions={0} | all-to-all | bytes 524288 | tf_op jit(solution)/shard_map/all_to_all | solution.py:336
  83.0 0.0 copy-start.7
  83.0 0.0 copy-start.1
  83.0 7.6 %merge.1 = bf16[8,96,384]{2,1,0:T(8,128)(2,1)} custom-call(bf16[16,64,128]{2,1,0:T(8,128)(2,1)} %all_to_all.20.part_ref, bf16[384,3072]{1,0:T(8,128)(2,1)} %w_ref.2), custom_call_target="tpu_custom_call" | custom-call | tf_op jit(solution)/shard_map/merge/pallas_call | solution.py:337
  90.6 0.0 copy-done
  90.6 0.0 copy-start.6
  90.6 0.0 copy-start.5
  90.6 12.9 %all-to-all-start.2 = ((bf16[8,96,384]{2,1,0:T(8,128)(2,1)}), bf16[8,96,384]{2,1,0:T(8,128)(2,1)S(1)}, u32[]{:S(2)}, u32[]{:S(2)}) async-start(bf16[8,96,384]{2,1,0:T(8,128)(2,1)} %merge.1), calls=%async_computation.2 | async-start | bytes 1179648 | tf_op jit(solution)/shard_map/all_to_all | solution.py:346
  103.5 0.0 copy-done.4
  103.5 0.8 copy.23.w_ref
  104.3 0.0 copy-done.7
  104.3 0.0 copy-done.1
  104.3 0.6 gather_fusion
  105.0 8.8 %all-to-all-done.2.term_ref = bf16[8,96,384]{2,1,0:T(8,128)(2,1)S(1)} async-done(((bf16[8,96,384]{2,1,0:T(8,128)(2,1)}), bf16[8,96,384]{2,1,0:T(8,128)(2,1)S(1)}, u32[]{:S(2)}, u32[]{:S(2)}) %all-to-all-start.2) | async-done | bytes 589856 | tf_op jit(solution)/shard_map/all_to_all | solution.py:346
  113.7 0.0 copy-start.2
  113.7 0.8 copy-done.2
  114.5 2.3 %stream.1 = (bf16[96,384]{1,0:T(8,128)(2,1)}, f32[8,104,128]{2,1,0:T(8,128)}) custom-call(s32[8]{0:T(128)} %copy-done, bf16[8,96,384]{2,1,0:T(8,128)(2,1)} %copy-done.2, bf16[96,384]{1,0:T(8,128)(2,1)} %hid_ref.1, bf16[2,384]{1,0:T(2,128)(2,1)} %gate_ref.1, bf16[2,384]{1,0:T(2,128)(2,1)} %shift_ref.1, bf16[2,384]{1,0:T(2,128)(2,1)} %scale_ref.1, ...), custom_call_target="tpu_custom_call" | custom-call | tf_op jit(solution)/shard_map/stream/pallas_call | solution.py:347
  116.8 4.2 %all-to-all-start.3 = ((f32[8,104,128]{2,1,0:T(8,128)}), f32[8,104,128]{2,1,0:T(8,128)S(1)}, u32[]{:S(2)}, u32[]{:S(2)}) async-start(f32[8,104,128]{2,1,0:T(8,128)} %get-tuple-element.10), calls=%async_computation.3 | async-start | bytes 851968 | tf_op jit(solution)/shard_map/all_to_all | solution.py:356
  121.0 0.0 copy-done.6
  121.1 0.6 gather_fusion.1
  121.8 0.0 copy-done.5
  121.8 0.7 copy.24.lat_ref
  122.5 0.6 pad_maximum_fusion.1.coef_ref
  123.1 6.4 %all-to-all-done.3.msg_ref = f32[8,104,128]{2,1,0:T(8,128)S(1)} async-done(((f32[8,104,128]{2,1,0:T(8,128)}), f32[8,104,128]{2,1,0:T(8,128)S(1)}, u32[]{:S(2)}, u32[]{:S(2)}) %all-to-all-start.3) | async-done | bytes 426016 | tf_op jit(solution)/shard_map/all_to_all | solution.py:356
  129.5 0.0 copy-start.3
  129.5 0.8 copy-done.3
  130.2 1.8 %ddim.1 = (f32[96,64]{1,0:T(8,128)}, f32[96,64]{1,0:T(8,128)}, f32[48,64]{1,0:T(8,128)}) custom-call(s32[8]{0:T(128)} %copy-done, f32[8]{0:T(128)} %pad_maximum_fusion.1.coef_ref, f32[8,104,128]{2,1,0:T(8,128)} %copy-done.3, f32[96,64]{1,0:T(8,128)} %copy.24.lat_ref), custom_call_target="tpu_custom_call" | custom-call | tf_op jit(solution)/shard_map/ddim/pallas_call | solution.py:368
  132.1 2.8 %collective-permute-start = (f32[48,64]{1,0:T(8,128)}, f32[48,64]{1,0:T(8,128)S(1)}, u32[]{:S(2)}, u32[]{:S(2)}) collective-permute-start(f32[48,64]{1,0:T(8,128)} %get-tuple-element.13), channel_id=1, source_target_pairs={{0,8},{2,10},{4,12},{6,14},{8,16},{9,1},{10,18},{11,3},{12,20},{13... | collective-permute-start | bytes 36872 | tf_op jit(solution)/shard_map/ppermute | solution.py:386
  134.9 1.5 %copy.27 = f32[96,64]{0,1:T(8,128)} copy(f32[96,64]{1,0:T(8,128)} %get-tuple-element.19) | data formatting | bytes 49152
  136.4 1.5 %copy.28 = f32[96,64]{0,1:T(8,128)} copy(f32[96,64]{1,0:T(8,128)} %get-tuple-element.20) | data formatting | bytes 49152
  137.9 0.0 collective-permute-done
  137.9 4.5 %all-gather = f32[96,64]{1,0:T(8,128)S(1)} all-gather(f32[48,64]{1,0:T(8,128)S(1)} %collective-permute-done), channel_id=2, replica_groups=mesh['y'=4,'z'=16,'x'=4,'core'=2] {'core'}, dimensions={0}, use_global_device_ids=true | all-gather | bytes 36864 | tf_op jit(solution)/shard_map/all_gather | solution.py:387
  142.5 0.1 copy.30
  142.6 0.1 copy.29
  142.7 0.7 pad_maximum_fusion
  (9 shorter events, 0.1 us)
Async XLA Ops:
  2.5 32.9 %all-to-all-start = ((bf16[16,96,128]{2,1,0:T(8,128)(2,1)}), bf16[16,96,128]{2,1,0:T(8,128)(2,1)S(1)}, u32[]{:S(2)}, u32[]{:S(2)}) async-start(bf16[16,96,128]{2,1,0:T(8,128)(2,1)} %pack.1), calls=%async_computation | async-start | bytes 786432 | tf_op jit(solution)/shard_map/all_to_all | solution.py:320
  18.2 72.4 %copy-start = (s32[8]{0:T(128)}, s32[8]{0:T(128)S(1)}, u32[]{:S(2)}) copy-start(s32[8]{0:T(128)S(1)} %stack.27.scal_ref) | copy-start | bytes 100
  58.9 44.7 %copy-start.4 = (bf16[384,64]{0,1:T(8,128)(2,1)S(1)}, bf16[384,64]{0,1:T(8,128)(2,1)}, u32[]{:S(2)}) copy-start(bf16[384,64]{0,1:T(8,128)(2,1)} %param.23) | copy-start | bytes 147460
  83.0 21.3 %copy-start.7 = (s32[2]{0:T(128)S(1)}, s32[2]{0:T(128)}, u32[]{:S(2)}) copy-start(s32[2]{0:T(128)} %param.14) | copy-start | bytes 28
  83.0 21.3 %copy-start.1 = (f32[1000]{0:T(1024)S(1)}, f32[1000]{0:T(1024)}, u32[]{:S(2)}) copy-start(f32[1000]{0:T(1024)} %constant.77.clone) | copy-start | bytes 12004
  90.6 30.5 %copy-start.6 = (s32[2]{0:T(128)S(1)}, s32[2]{0:T(128)}, u32[]{:S(2)}) copy-start(s32[2]{0:T(128)} %param.13) | copy-start | bytes 28
  90.6 31.2 %copy-start.5 = (f32[96,64]{0,1:T(8,128)S(1)}, f32[96,64]{0,1:T(8,128)}, u32[]{:S(2)}) copy-start(f32[96,64]{0,1:T(8,128)} %param.24) | copy-start | bytes 73732
  90.6 23.1 %all-to-all-start.2 = ((bf16[8,96,384]{2,1,0:T(8,128)(2,1)}), bf16[8,96,384]{2,1,0:T(8,128)(2,1)S(1)}, u32[]{:S(2)}, u32[]{:S(2)}) async-start(bf16[8,96,384]{2,1,0:T(8,128)(2,1)} %merge.1), calls=%async_computation.2 | async-start | bytes 1179648 | tf_op jit(solution)/shard_map/all_to_all | solution.py:346
  113.7 0.8 copy-start.2
  116.8 12.7 %all-to-all-start.3 = ((f32[8,104,128]{2,1,0:T(8,128)}), f32[8,104,128]{2,1,0:T(8,128)S(1)}, u32[]{:S(2)}, u32[]{:S(2)}) async-start(f32[8,104,128]{2,1,0:T(8,128)} %get-tuple-element.10), calls=%async_computation.3 | async-start | bytes 851968 | tf_op jit(solution)/shard_map/all_to_all | solution.py:356
  129.5 0.8 copy-start.3
  132.1 5.8 %collective-permute-start = (f32[48,64]{1,0:T(8,128)}, f32[48,64]{1,0:T(8,128)S(1)}, u32[]{:S(2)}, u32[]{:S(2)}) collective-permute-start(f32[48,64]{1,0:T(8,128)} %get-tuple-element.13), channel_id=1, source_target_pairs={{0,8},{2,10},{4,12},{6,14},{8,16},{9,1},{10,18},{11,3},{12,20},{13... | collective-permute-start | bytes 36872 | tf_op jit(solution)/shard_map/ppermute | solution.py:386

commit v2 on v1

v2 whole, which is shorter than its diff:
```python
import jax
import jax.numpy as jnp
import numpy as np
from jax import lax
from jax.experimental import pallas as pl
from jax.experimental.pallas import tpu as pltpu
from jax.sharding import Mesh
from jax.sharding import PartitionSpec as P

D = 3072
HD = 64
RIM = 45
TOK = 96
HALF = 48
LEN_ALL = 5952
TRAIN_STEPS = 1000
STEP_GAP = 20
NY, NZ, NX, NC = 4, 16, 4, 2
NHEAD = 8
EPSILON = 1e-06
MASKED = -1e30
FLOOR = -0.5e30
HEAD_OF = (0, 0, 0, 1, 1, 1, 2, 2, 2, 3, 3, 3, 4, 4, 5, 5)
PART_OF = (0, 1, 2, 0, 1, 2, 0, 1, 2, 0, 1, 2, 0, 1, 0, 1)
SIZE_OF = (32,) * 12 + (48,) * 4
BF = jnp.bfloat16
F32 = jnp.float32
SMEM = pltpu.SMEM
VMEM = pltpu.VMEM


def low_lanes(rows):
    return lax.broadcasted_iota(jnp.int32, (rows, 128), 1) < HD


def swap(x):
    return pltpu.roll(x, HD, 1)


def pack_kernel(q_ref, k_ref, v_ref, queries_ref, keyvals_ref):
    low_h, low_t = low_lanes(HALF), low_lanes(TOK)
    for pair in range(3):
        lanes = slice(128 * pair, 128 * pair + 128)
        q = q_ref[:, lanes].astype(F32) * 0.125
        k = k_ref[:, lanes].astype(F32)
        v = v_ref[:, lanes].astype(F32)
        top, bottom = q[:HALF], q[HALF:]
        queries = (jnp.where(low_h, top, swap(bottom)), jnp.where(low_h, swap(top), bottom))
        keyvals = (jnp.where(low_t, k, swap(v)), jnp.where(low_t, swap(k), v))
        for side in range(2):
            qh = queries[side].astype(BF)
            kvh = keyvals[side].astype(BF)
            for d in range(NZ):
                if HEAD_OF[d] != 2 * pair + side:
                    continue
                size = SIZE_OF[d]
                start = PART_OF[d] * size
                queries_ref[d] = qh
                keyvals_ref[d, :size, :] = kvh[start : start + size]
                if size < HALF:
                    keyvals_ref[d, size:, :] = jnp.zeros((HALF - size, 128), BF)


def pieces(x):
    hi = x.astype(BF).astype(F32)
    rest = x - hi
    mid = rest.astype(BF).astype(F32)
    return (hi, mid, rest - mid)


QT = 384
KT = 768
HALVES = NZ * HALF
TILES = 2 * HALVES // QT
ONES = 131


def attend_kernel(scal_ref, q_ref, kv_ref, out_ref, key_ref, query_ref, top_ref, acc_ref):
    first_len, row, size, offset = scal_ref[0], scal_ref[1], scal_ref[2], scal_ref[3]
    lane3 = lax.broadcasted_iota(jnp.int32, (NZ, HALF, 128), 2)
    slot = lax.broadcasted_iota(jnp.int32, (NZ, HALF, 128), 1)
    block = lax.broadcasted_iota(jnp.int32, (NZ, HALF, 128), 0) * TOK + slot
    for j in range(NY):
        pos = jnp.where(slot < size, block + (j * NZ * TOK + offset), LEN_ALL)
        own = jnp.where(pos < first_len, 0, jnp.where(pos < LEN_ALL, 1, -1))
        extra = jnp.where((lane3 < 3) & (lane3 != own), MASKED, 0.0)
        extra = jnp.where(lane3 == ONES - 128, 1.0, extra)
        key_ref[j, :, :128] = kv_ref[j * KT : (j + 1) * KT, :]
        key_ref[j, :, 128:] = extra.reshape(KT, 128).astype(BF)

    low = low_lanes(HALVES)
    q = q_ref[...].astype(F32).reshape(HALVES, 128)
    for side in range(2):
        pos = block + (row * NZ * TOK + side * HALF)
        own = jnp.where(pos < first_len, 0, jnp.where(pos < LEN_ALL, 1, 2))
        extra = jnp.where(lane3 == own, 1.0, 0.0).reshape(HALVES, 128)
        rows = slice(side * HALVES, (side + 1) * HALVES)
        query_ref[rows, :128] = jnp.where(low, swap(q) if side else q, 0.0).astype(BF)
        query_ref[rows, 128:] = extra.astype(BF)
    top_ref[...] = jnp.full_like(top_ref, FLOOR)
    acc_ref[...] = jnp.zeros_like(acc_ref)

    def holds(start, stop):
        stop = jnp.minimum(stop, LEN_ALL)
        return start < first_len, (stop > first_len) & (start < stop)

    def visit(number, carry):
        j, tile = number // TILES, number % TILES
        start = row * (NZ * TOK) + (tile % (TILES // 2)) * (QT // HALF * TOK)
        q_first, q_second = holds(start, start + QT // HALF * TOK)
        k_first, k_second = holds(j * (NZ * TOK), (j + 1) * (NZ * TOK))

        @pl.when((q_first & k_first) | (q_second & k_second))
        def _():
            rows = pl.ds(tile * QT, QT)
            keys = key_ref[j]
            scores = lax.dot_general(
                query_ref[rows, :], keys, (((1,), (1,)), ((), ())), preferred_element_type=F32
            )
            old = top_ref[rows, :1]
            new = jnp.maximum(jnp.max(scores, axis=1, keepdims=True), old)
            weights = jnp.exp(scores - new).astype(BF)
            acc_ref[rows, :] = acc_ref[rows, :] * jnp.exp(old - new) + jnp.dot(
                weights, keys, preferred_element_type=F32
            )
            top_ref[rows, :] = jnp.broadcast_to(new, (QT, 128))

        return carry

    lax.fori_loop(0, NY * TILES, visit, 0)

    lane = lax.broadcasted_iota(jnp.int32, (HALVES, 128), 1)
    eye = (
        lax.broadcasted_iota(jnp.int32, (TOK, 128), 0)
        == lax.broadcasted_iota(jnp.int32, (TOK, 128), 1)
    ).astype(BF)
    outs, stats = [], []
    for side in range(2):
        rows = slice(side * HALVES, (side + 1) * HALVES)
        sums = acc_ref[rows, ONES : ONES + 1]
        outs.append(acc_ref[rows, :128] / jnp.where(sums > 0.0, sums, 1.0))
        stat = jnp.zeros((HALVES, 128), F32)
        for number, piece in enumerate(pieces(top_ref[rows, :1]) + pieces(sums)):
            stat = jnp.where(lane == number, piece, stat)
        stats.append(stat.astype(BF))
    mixed = jnp.where(low, swap(outs[0]), outs[1]).astype(BF)
    for b in range(NZ):
        rows = slice(b * HALF, (b + 1) * HALF)
        out_ref[b, :HALF, :] = mixed[rows]
        both = jnp.concatenate([stats[0][rows], stats[1][rows]], axis=0)
        turned = lax.dot_general(
            both, eye, (((0,), (0,)), ((), ())), preferred_element_type=F32
        )
        out_ref[b, HALF:, :] = turned[:8].astype(BF)


def merge_kernel(part_ref, w_ref, out_ref, att_ref, copy_ref, sem):
    copy = pltpu.make_async_copy(w_ref, copy_ref, sem)
    copy.start()
    low = low_lanes(HALF)
    stat = part_ref[:, HALF:, :].astype(F32)
    tops = stat[:, 0] + stat[:, 1] + stat[:, 2]
    sums = stat[:, 3] + stat[:, 4] + stat[:, 5]
    shares = []
    for h in range(6):
        own = [d for d in range(NZ) if HEAD_OF[d] == h]
        rows = slice(own[0], own[-1] + 1)
        top = jnp.max(tops[rows], axis=0, keepdims=True)
        scaled = jnp.exp(tops[rows] - top) * sums[rows]
        total = jnp.sum(scaled, axis=0, keepdims=True)
        shares.append(scaled / jnp.where(total > 0.0, total, 1.0))
    shares = jnp.concatenate(shares + [jnp.zeros((128 - NZ, 128), F32)], axis=0).T
    heads = []
    for h in range(6):
        mixed = jnp.zeros((HALF, 128), F32)
        for d in range(NZ):
            if HEAD_OF[d] == h:
                weight = jnp.where(
                    low, shares[:HALF, d : d + 1], shares[HALF : 2 * HALF, d : d + 1]
                )
                mixed += weight * part_ref[d, :HALF, :].astype(F32)
        heads.append(mixed)
    for pair in range(3):
        even, odd = heads[2 * pair], heads[2 * pair + 1]
        lanes = slice(128 * pair, 128 * pair + 128)
        att_ref[:HALF, lanes] = jnp.where(low, even, swap(odd)).astype(BF)
        att_ref[HALF:, lanes] = jnp.where(low, swap(even), odd).astype(BF)
    copy.wait()
    for j in range(NHEAD):
        out_ref[j] = jnp.dot(
            att_ref[...], copy_ref[:, 384 * j : 384 * j + 384], preferred_element_type=F32
        ).astype(BF)


def split2(x):
    hi = x.astype(BF)
    return hi, (x - hi.astype(F32)).astype(BF)


def stream_kernel(
    scal_ref, term_ref, hid_ref, gate_ref, shift_ref, scale_ref, w_ref, hid_out, msg_ref
):
    first_len, base = scal_ref[0], scal_ref[4]
    projected = term_ref[0].astype(F32)
    for j in range(1, NHEAD):
        projected += term_ref[j].astype(F32)
    pos = base + lax.broadcasted_iota(jnp.int32, (TOK, 384), 0)
    first, second = pos < first_len, pos < LEN_ALL

    def per_row(table):
        return jnp.where(first, table[0:1], jnp.where(second, table[1:2], 0.0))

    gate, shift = gate_ref[...].astype(F32), shift_ref[...].astype(F32)
    factor = 1.0 + scale_ref[...].astype(F32)
    x = (hid_ref[...].astype(F32) + per_row(gate) * projected).astype(BF)
    hid_out[...] = x
    xf = x.astype(F32)
    scaled = jnp.concatenate(
        [xf * per_row(factor), factor, shift, jnp.zeros((28, 384), F32)], axis=0
    )
    sq_hi, sq_lo = split2(xf * xf)
    ones = jnp.ones((8, 384), BF)

    def turn(left, right):
        return lax.dot_general(left, right, (((1,), (1,)), ((), ())), preferred_element_type=F32)

    high, rest = split2(scaled)
    w = w_ref[...]
    a = turn(w, high) + turn(w, rest)
    total = turn(ones, x)
    squares = turn(ones, sq_hi) + turn(ones, sq_lo)
    rows8 = lax.broadcasted_iota(jnp.int32, (8, TOK), 0)
    tail = jnp.where(rows8 == 0, total, squares)
    for j in range(NHEAD):
        msg_ref[j, :64, :] = a
        msg_ref[j, 64:, :TOK] = tail
        msg_ref[j, 64:, TOK:] = jnp.zeros((8, 128 - TOK), F32)


def step_kernel(scal_ref, coef_ref, msg_ref, lat_ref, clean_ref, prev_ref):
    first_len, base = scal_ref[0], scal_ref[4]
    total = msg_ref[0]
    for j in range(1, NHEAD):
        total += msg_ref[j]
    pos = base + lax.broadcasted_iota(jnp.int32, (64, TOK), 1)
    first, live = pos < first_len, pos < LEN_ALL
    mean = total[64:65, :TOK] * (1.0 / D)
    var = total[65:66, :TOK] * (1.0 / D) - mean * mean
    scale_w = jnp.where(first, total[:64, TOK : TOK + 1], total[:64, TOK + 1 : TOK + 2])
    shift_w = jnp.where(first, total[:64, TOK + 2 : TOK + 3], total[:64, TOK + 3 : TOK + 4])
    velocity = lax.rsqrt(var + EPSILON) * (total[:64, :TOK] - mean * scale_w) + shift_w
    latent = lat_ref[...]

    def row_coef(i):
        return jnp.where(first, coef_ref[2 * i], coef_ref[2 * i + 1])

    root_a, root_1a, root_q, root_1q = (row_coef(i) for i in range(4))
    clean = root_a * latent - root_1a * velocity
    noise = root_1a * latent + root_a * velocity
    stepped = root_q * clean + root_1q * noise
    clean_ref[...] = jnp.where(live, clean, 0.0)
    prev_ref[...] = jnp.where(live, stepped, 0.0)


def alpha_table():
    betas = np.linspace(0.00085**0.5, 0.012**0.5, TRAIN_STEPS) ** 2
    return np.cumprod(1.0 - betas).astype(np.float32)


def request_of(position, first_len):
    return jnp.where(
        position < 0, -1, jnp.where(position < first_len, 0, jnp.where(position < LEN_ALL, 1, 2))
    )


def shards(
    lengths,
    step_index,
    query_act,
    key_act,
    value_act,
    hidden,
    attn_weight,
    gate_mod,
    shift_mod,
    scale_mod,
    proj_weight,
    latent,
):
    z = lax.axis_index("z")
    y = lax.axis_index("y")
    seq = y * NZ + z
    first_len = lengths[0]
    size = jnp.where(z < 12, 32, 48)
    part = jnp.where(z < 12, z % 3, z % 2)
    scal = jnp.stack([first_len, y, size, part * size, seq * TOK]).astype(jnp.int32)
    in_smem = pl.BlockSpec(memory_space=SMEM)
    big = pltpu.CompilerParams(vmem_limit_bytes=48 * 1024 * 1024)

    any_vmem = pl.BlockSpec(memory_space=VMEM)

    queries, keyvals = pl.pallas_call(
        pack_kernel,
        out_shape=(jax.ShapeDtypeStruct((NZ, HALF, 128), BF),) * 2,
        name="pack",
    )(query_act, key_act, value_act)
    keyvals = lax.all_to_all(keyvals, "z", 0, 0, tiled=True)
    keyvals, queries = lax.optimization_barrier((keyvals, queries))
    queries = lax.all_to_all(queries, "z", 0, 0, tiled=True)
    keyvals = lax.all_gather(keyvals.reshape(NZ * HALF, 128), "y", axis=0, tiled=True)
    partial = pl.pallas_call(
        attend_kernel,
        out_shape=jax.ShapeDtypeStruct((NZ, HALF + 8, 128), BF),
        in_specs=[in_smem, any_vmem, any_vmem],
        out_specs=any_vmem,
        scratch_shapes=[
            VMEM((NY, KT, 256), BF),
            VMEM((2 * HALVES, 256), BF),
            VMEM((2 * HALVES, 128), F32),
            VMEM((2 * HALVES, 256), F32),
        ],
        compiler_params=big,
        name="attend",
    )(scal, queries, keyvals)
    parts = lax.all_to_all(partial, "z", 0, 0, tiled=True)
    term = pl.pallas_call(
        merge_kernel,
        out_shape=jax.ShapeDtypeStruct((NHEAD, TOK, 384), BF),
        in_specs=[any_vmem, pl.BlockSpec(memory_space=pl.ANY)],
        out_specs=any_vmem,
        scratch_shapes=[VMEM((TOK, 384), BF), VMEM((384, D), BF), pltpu.SemaphoreType.DMA],
        compiler_params=big,
        name="merge",
    )(parts, attn_weight)
    terms = lax.all_to_all(term, ("x", "core"), 0, 0, tiled=True)
    hidden_out, message = pl.pallas_call(
        stream_kernel,
        out_shape=(
            jax.ShapeDtypeStruct((TOK, 384), BF),
            jax.ShapeDtypeStruct((NHEAD, 72, 128), F32),
        ),
        in_specs=[in_smem] + [any_vmem] * 6,
        name="stream",
    )(scal, terms, hidden, gate_mod, shift_mod, scale_mod, proj_weight.T)
    message = lax.all_to_all(message, ("x", "core"), 0, 0, tiled=True)
    table = jnp.asarray(alpha_table())
    alpha_now = table[step_index]
    alpha_prev = table[step_index - STEP_GAP]
    coef = jnp.concatenate(
        [
            jnp.sqrt(alpha_now),
            jnp.sqrt(1.0 - alpha_now),
            jnp.sqrt(alpha_prev),
            jnp.sqrt(1.0 - alpha_prev),
        ]
    )
    clean, stepped = pl.pallas_call(
        step_kernel,
        out_shape=(jax.ShapeDtypeStruct((64, TOK), F32),) * 2,
        in_specs=[in_smem, in_smem, any_vmem, any_vmem],
        name="ddim",
    )(scal, coef, message, latent.T)
    pairs = []
    for s in range(NY * NZ):
        for x in range(NX):
            up, down = (s * NX + x) * NC, (s * NX + x) * NC + 1
            if s + 1 < NY * NZ:
                pairs.append((up, up + NX * NC))
            if s > 0:
                pairs.append((down, down - NX * NC))
    got = lax.ppermute(stepped, ("y", "z", "x", "core"), pairs)
    both = lax.all_gather(got, "core")
    offsets = jnp.arange(RIM, dtype=jnp.int32)
    start = seq * TOK
    lower_ok = request_of(start - RIM + offsets, first_len) == request_of(start, first_len)
    upper_ok = request_of(start + TOK + offsets, first_len) == request_of(
        start + TOK - 1, first_len
    )
    lower_ok &= start > 0
    upper_ok &= start + TOK < NY * NZ * TOK
    rims = jnp.concatenate(
        [
            jnp.where(lower_ok[None], both[0, :, TOK - RIM :], 0.0),
            jnp.where(upper_ok[None], both[1, :, :RIM], 0.0),
        ],
        axis=1,
    )
    return hidden_out, clean.T, stepped.T, rims.T


def solution(mesh):
    grid = Mesh(mesh.devices.reshape(NY, NZ, NX, NC), ("y", "z", "x", "core"))
    seq, head = ("y", "z"), ("x", "core")
    in_specs = (
        P(),
        P(),
        P(seq, head),
        P(seq, head),
        P(seq, head),
        P(seq, head),
        P(head, None),
        P(None, head),
        P(None, head),
        P(None, head),
        P(head, None),
        P(seq, None),
    )
    out_specs = (P(seq, head), P(seq, None), P(seq, None), P(seq, None))
    return jax.shard_map(shards, mesh=grid, in_specs=in_specs, out_specs=out_specs, check_vma=False)
```

time: 145 us -> 145 us (level)
  blocking collectives: 39.4 us -> 44.1 us
  local copies, waits for them, and re-layouts: 8.23 us -> 3.55 us
  starting transfers between devices: 34.9 us -> 38.1 us
  waiting for transfers between devices: 32.4 us -> 29.7 us
    all_to_all x1 -> x2, starting transfers between devices: 14.9 us -> 19.6 us  [the longest x1 10.8 us: shards(): parts = lax.all_to_all(partial, 'z', 0, 0, tiled=True)]
    unnamed x22 -> x14, local copies, waits for them, and re-layouts: 6.22 us -> 1.56 us
    all_to_all x1 -> x2, waiting for transfers between devices: 17.2 us -> 13.1 us  [the longest x1 12.5 us: shards(): parts = lax.all_to_all(partial, 'z', 0, 0, tiled=True)]
    all_to_all x1, blocking collectives: 24.1 us -> 27.5 us  [shards(): keyvals = lax.all_to_all(keyvals, 'z', 0, 0, tiled=True)]
    all_to_all x1, starting transfers between devices: 12.9 us -> 10.7 us  [shards(): terms = lax.all_to_all(term, ('x', 'core'), 0, 0, tiled=True)]
    ppermute x1, waiting for transfers between devices: 0.01 us -> 1.51 us  [shards(): got = lax.ppermute(stepped, ('y', 'z', 'x', 'core'), pairs)]
  transfers between devices with their start and end apart: 4 -> 5, of which waited for: 3 -> 5; matrix products, arithmetic and copies ran while one was open for 5% -> 2% of each run, Pallas kernels for 0% -> 0%
where the time goes in v2:
time: 145 us; the launch traced here: 144 us
  blocking collectives  44.1 us (30%)
  starting transfers between devices  38.1 us (26%)
  waiting for transfers between devices  29.7 us (20%)
  Pallas kernels  26.6 us (18%)
  local copies, waits for them, and re-layouts  3.55 us (2%)
    all_to_all x1, blocking collectives, shards(): keyvals = lax.all_to_all(keyvals, 'z', 0, 0, tiled=True)  27.5 us
    pallas_call x1, Pallas kernels, shards(): pl.pallas_call(attend_kernel, out_shape=jax.ShapeDtypeStruct((NZ, HALF +...  18.5 us
    all_to_all x1, waiting for transfers between devices, shards(): parts = lax.all_to_all(partial, 'z', 0, 0, tiled=True)  12.5 us
    all_gather x1, blocking collectives, shards(): lax.all_gather(keyvals.reshape(NZ * HALF, 128), 'y', axis=0, tiled=True)  11.1 us
    all_to_all x1, starting transfers between devices, shards(): parts = lax.all_to_all(partial, 'z', 0, 0, tiled=True)  10.8 us
    all_to_all x1, starting transfers between devices, shards(): terms = lax.all_to_all(term, ('x', 'core'), 0, 0, tiled=True)  10.7 us
    all_to_all x1, waiting for transfers between devices, shards(): terms = lax.all_to_all(term, ('x', 'core'), 0, 0, tiled=True)  8.89 us
    all_to_all x1, starting transfers between devices, shards(): queries = lax.all_to_all(queries, 'z', 0, 0, tiled=True)  8.81 us
  transfers between devices with their start and end apart: 5, of which 5 were waited for; matrix products, arithmetic and copies ran while one was open for 2% of the time, Pallas kernels for 0%

profile of v2, /device:TPU:25, one launch (start us, length us, event | category | flops | bytes accessed | tf_op | source)
XLA Modules:
  0.0 144.3 jit_solution(12733854870605198187)
XLA Ops:
  0.6 0.0 copy-start.5
  0.6 0.0 copy-start
  0.7 2.0 %pack.1 = (bf16[16,48,128]{2,1,0:T(8,128)(2,1)}, bf16[16,48,128]{2,1,0:T(8,128)(2,1)}) custom-call(bf16[96,384]{1,0:T(8,128)(2,1)} %q_ref.1, bf16[96,384]{1,0:T(8,128)(2,1)} %k_ref.1, bf16[96,384]{1,0:T(8,128)(2,1)} %v_ref.1), custom_call_target="tpu_custom_call" | custom-call | tf_op jit(solution)/shard_map/pack/pallas_call | solution.py:302
  2.6 27.5 %all_to_all.25 = bf16[16,48,128]{2,1,0:T(8,128)(2,1)S(1)} all-to-all(bf16[16,48,128]{2,1,0:T(8,128)(2,1)} %get-tuple-element.12), channel_id=1, replica_groups=mesh['y'=4,'z'=16,'x'=4,'core'=2] {'z'}, dimensions={0} | all-to-all | bytes 393216 | tf_op jit(solution)/shard_map/all_to_all | solution.py:307
  30.1 8.8 %all-to-all-start.1 = ((bf16[16,48,128]{2,1,0:T(8,128)(2,1)}), bf16[16,48,128]{2,1,0:T(8,128)(2,1)S(1)}, u32[]{:S(2)}, u32[]{:S(2)}) async-start(bf16[16,48,128]{2,1,0:T(8,128)(2,1)} %get-tuple-element.14), calls=%async_computation.1 | async-start | bytes 393216 | tf_op jit(solution)/shard_map/all_to_all | solution.py:309
  38.9 0.7 stack.19.scal_ref
  39.7 0.0 copy-start.1
  39.7 11.1 %all_gather.9.kv_ref = bf16[3072,128]{1,0:T(8,128)(2,1)S(1)} all-gather(bf16[768,128]{1,0:T(8,128)(2,1)S(1)} %bitcast.22), channel_id=1, replica_groups=mesh['y'=4,'z'=16,'x'=4,'core'=2] {'y'}, dimensions={0}, use_global_device_ids=true | all-gather | bytes 983040 | tf_op jit(solution)/shard_map/all_gather | solution.py:310
  50.8 0.7 all-to-all-done.1.q_ref
  51.5 18.5 %attend.1 = bf16[16,56,128]{2,1,0:T(8,128)(2,1)} custom-call(s32[5]{0:T(128)S(1)} %stack.19.scal_ref, bf16[16,48,128]{2,1,0:T(8,128)(2,1)S(1)} %all-to-all-done.1.q_ref, bf16[3072,128]{1,0:T(8,128)(2,1)S(1)} %all_gather.9.kv_ref), custom_call_target="tpu_custom_call" | custom-call | tf_op jit(solution)/shard_map/attend/pallas_call | solution.py:311
  70.0 0.0 copy-start.6
  70.0 0.0 copy-start.2
  70.0 10.8 %all-to-all-start.2 = ((bf16[16,56,128]{2,1,0:T(8,128)(2,1)}), bf16[16,56,128]{2,1,0:T(8,128)(2,1)S(1)}, u32[]{:S(2)}, u32[]{:S(2)}) async-start(bf16[16,56,128]{2,1,0:T(8,128)(2,1)} %attend.1), calls=%async_computation.2 | async-start | bytes 458752 | tf_op jit(solution)/shard_map/all_to_all | solution.py:325
  80.7 0.0 copy-done.5
  80.8 12.5 %all-to-all-done.2.part_ref = bf16[16,56,128]{2,1,0:T(8,128)(2,1)S(1)} async-done(((bf16[16,56,128]{2,1,0:T(8,128)(2,1)}), bf16[16,56,128]{2,1,0:T(8,128)(2,1)S(1)}, u32[]{:S(2)}, u32[]{:S(2)}) %all-to-all-start.2) | async-done | bytes 229408 | tf_op jit(solution)/shard_map/all_to_all | solution.py:325
  93.3 0.0 copy-done
  93.3 2.1 %merge.1 = bf16[8,96,384]{2,1,0:T(8,128)(2,1)} custom-call(bf16[16,56,128]{2,1,0:T(8,128)(2,1)S(1)} %all-to-all-done.2.part_ref, bf16[384,3072]{1,0:T(8,128)(2,1)S(1)} %copy-done), custom_call_target="tpu_custom_call" | custom-call | tf_op jit(solution)/shard_map/merge/pallas_call | solution.py:326
  95.4 0.0 copy-done.1
  95.4 10.7 %all-to-all-start.3 = ((bf16[8,96,384]{2,1,0:T(8,128)(2,1)}), bf16[8,96,384]{2,1,0:T(8,128)(2,1)S(1)}, u32[]{:S(2)}, u32[]{:S(2)}) async-start(bf16[8,96,384]{2,1,0:T(8,128)(2,1)} %merge.1), calls=%async_computation.3 | async-start | bytes 1179648 | tf_op jit(solution)/shard_map/all_to_all | solution.py:335
  106.1 0.0 copy-done.6
  106.2 0.0 copy-done.2
  106.2 0.6 gather_fusion
  106.8 0.6 gather_fusion.1
  107.4 8.9 %all-to-all-done.3.term_ref = bf16[8,96,384]{2,1,0:T(8,128)(2,1)S(1)} async-done(((bf16[8,96,384]{2,1,0:T(8,128)(2,1)}), bf16[8,96,384]{2,1,0:T(8,128)(2,1)S(1)}, u32[]{:S(2)}, u32[]{:S(2)}) %all-to-all-start.3) | async-done | bytes 589856 | tf_op jit(solution)/shard_map/all_to_all | solution.py:335
  116.3 0.0 copy-start.3
  116.3 0.8 copy-done.3
  117.1 2.3 %stream.1 = (bf16[96,384]{1,0:T(8,128)(2,1)}, f32[8,72,128]{2,1,0:T(8,128)}) custom-call(s32[5]{0:T(128)} %copy-done.1, bf16[8,96,384]{2,1,0:T(8,128)(2,1)} %copy-done.3, bf16[96,384]{1,0:T(8,128)(2,1)} %hid_ref.1, bf16[2,384]{1,0:T(2,128)(2,1)} %gate_ref.1, bf16[2,384]{1,0:T(2,128)(2,1)} %shift_ref.1, bf16[2,384]{1,0:T(2,128)(2,1)} %scale_ref.1, ...), custom_call_target="tpu_custom_call" | custom-call | tf_op jit(solution)/shard_map/stream/pallas_call | solution.py:336
  119.4 4.2 %all-to-all-start.4 = ((f32[8,72,128]{2,1,0:T(8,128)}), f32[8,72,128]{2,1,0:T(8,128)S(1)}, u32[]{:S(2)}, u32[]{:S(2)}) async-start(f32[8,72,128]{2,1,0:T(8,128)} %get-tuple-element.17), calls=%async_computation.4 | async-start | bytes 589824 | tf_op jit(solution)/shard_map/all_to_all | solution.py:345
  123.6 0.6 pad_maximum_fusion.coef_ref
  124.2 6.2 %all-to-all-done.4.msg_ref = f32[8,72,128]{2,1,0:T(8,128)S(1)} async-done(((f32[8,72,128]{2,1,0:T(8,128)}), f32[8,72,128]{2,1,0:T(8,128)S(1)}, u32[]{:S(2)}, u32[]{:S(2)}) %all-to-all-start.4) | async-done | bytes 294944 | tf_op jit(solution)/shard_map/all_to_all | solution.py:345
  130.4 0.0 copy-start.4
  130.4 0.7 copy-done.4
  131.2 1.7 %ddim.1 = (f32[64,96]{1,0:T(8,128)}, f32[64,96]{1,0:T(8,128)}) custom-call(s32[5]{0:T(128)} %copy-done.1, f32[8]{0:T(128)} %pad_maximum_fusion.coef_ref, f32[8,72,128]{2,1,0:T(8,128)} %copy-done.4, f32[64,96]{1,0:T(8,128)} %bitcast.25), custom_call_target="tpu_custom_call" | custom-call | tf_op jit(solution)/shard_map/ddim/pallas_call | solution.py:357
  132.9 3.6 %collective-permute-start = (f32[64,96]{1,0:T(8,128)}, f32[64,96]{1,0:T(8,128)S(1)}, u32[]{:S(2)}, u32[]{:S(2)}) collective-permute-start(f32[64,96]{1,0:T(8,128)} %get-tuple-element.19), channel_id=1, source_target_pairs={{0,8},{2,10},{4,12},{6,14},{8,16},{9,1},{10,18},{11,3},{12,20},{13... | collective-permute-start | bytes 73736 | tf_op jit(solution)/shard_map/ppermute | solution.py:371
  136.6 1.5 %collective-permute-done = f32[64,96]{1,0:T(8,128)S(1)} collective-permute-done((f32[64,96]{1,0:T(8,128)}, f32[64,96]{1,0:T(8,128)S(1)}, u32[]{:S(2)}, u32[]{:S(2)}) %collective-permute-start) | collective-permute-done | bytes 24608 | tf_op jit(solution)/shard_map/ppermute | solution.py:371
  138.1 5.5 %all-gather = f32[128,96]{1,0:T(8,128)S(1)} all-gather(f32[64,96]{1,0:T(8,128)S(1)} %collective-permute-done), channel_id=2, replica_groups=mesh['y'=4,'z'=16,'x'=4,'core'=2] {'core'}, dimensions={0}, use_global_device_ids=true | all-gather | bytes 73728 | tf_op jit(solution)/shard_map/all_gather | solution.py:372
  143.6 0.1 fusion.1
  143.6 0.7 maximum_bitcast_fusion
  (5 shorter events, 0.1 us)
Async XLA Ops:
  0.6 80.1 %copy-start.5 = (s32[2]{0:T(128)S(1)}, s32[2]{0:T(128)}, u32[]{:S(2)}) copy-start(s32[2]{0:T(128)} %param.13) | copy-start | bytes 28
  0.6 92.7 %copy-start = (bf16[384,3072]{1,0:T(8,128)(2,1)S(1)}, bf16[384,3072]{1,0:T(8,128)(2,1)}, u32[]{:S(2)}) copy-start(bf16[384,3072]{1,0:T(8,128)(2,1)} %w_ref.1) | copy-start | bytes 7077892
  30.1 21.4 %all-to-all-start.1 = ((bf16[16,48,128]{2,1,0:T(8,128)(2,1)}), bf16[16,48,128]{2,1,0:T(8,128)(2,1)S(1)}, u32[]{:S(2)}, u32[]{:S(2)}) async-start(bf16[16,48,128]{2,1,0:T(8,128)(2,1)} %get-tuple-element.14), calls=%async_computation.1 | async-start | bytes 393216 | tf_op jit(solution)/shard_map/all_to_all | solution.py:309
  39.7 55.8 %copy-start.1 = (s32[5]{0:T(128)}, s32[5]{0:T(128)S(1)}, u32[]{:S(2)}) copy-start(s32[5]{0:T(128)S(1)} %stack.19.scal_ref) | copy-start | bytes 64
  70.0 36.2 %copy-start.6 = (s32[2]{0:T(128)S(1)}, s32[2]{0:T(128)}, u32[]{:S(2)}) copy-start(s32[2]{0:T(128)} %param.14) | copy-start | bytes 28
  70.0 36.2 %copy-start.2 = (f32[1000]{0:T(1024)S(1)}, f32[1000]{0:T(1024)}, u32[]{:S(2)}) copy-start(f32[1000]{0:T(1024)} %constant.71.clone) | copy-start | bytes 12004
  70.0 23.3 %all-to-all-start.2 = ((bf16[16,56,128]{2,1,0:T(8,128)(2,1)}), bf16[16,56,128]{2,1,0:T(8,128)(2,1)S(1)}, u32[]{:S(2)}, u32[]{:S(2)}) async-start(bf16[16,56,128]{2,1,0:T(8,128)(2,1)} %attend.1), calls=%async_computation.2 | async-start | bytes 458752 | tf_op jit(solution)/shard_map/all_to_all | solution.py:325
  95.4 20.9 %all-to-all-start.3 = ((bf16[8,96,384]{2,1,0:T(8,128)(2,1)}), bf16[8,96,384]{2,1,0:T(8,128)(2,1)S(1)}, u32[]{:S(2)}, u32[]{:S(2)}) async-start(bf16[8,96,384]{2,1,0:T(8,128)(2,1)} %merge.1), calls=%async_computation.3 | async-start | bytes 1179648 | tf_op jit(solution)/shard_map/all_to_all | solution.py:335
  116.3 0.8 copy-start.3
  119.4 11.0 %all-to-all-start.4 = ((f32[8,72,128]{2,1,0:T(8,128)}), f32[8,72,128]{2,1,0:T(8,128)S(1)}, u32[]{:S(2)}, u32[]{:S(2)}) async-start(f32[8,72,128]{2,1,0:T(8,128)} %get-tuple-element.17), calls=%async_computation.4 | async-start | bytes 589824 | tf_op jit(solution)/shard_map/all_to_all | solution.py:345
  130.4 0.7 copy-start.4
  132.9 5.2 %collective-permute-start = (f32[64,96]{1,0:T(8,128)}, f32[64,96]{1,0:T(8,128)S(1)}, u32[]{:S(2)}, u32[]{:S(2)}) collective-permute-start(f32[64,96]{1,0:T(8,128)} %get-tuple-element.19), channel_id=1, source_target_pairs={{0,8},{2,10},{4,12},{6,14},{8,16},{9,1},{10,18},{11,3},{12,20},{13... | collective-permute-start | bytes 73736 | tf_op jit(solution)/shard_map/ppermute | solution.py:371

commit v3 on v2

v3 whole, which is shorter than its diff:
```python
import jax
import jax.numpy as jnp
import numpy as np
from jax import lax
from jax.experimental import pallas as pl
from jax.experimental.pallas import tpu as pltpu
from jax.sharding import Mesh
from jax.sharding import PartitionSpec as P

D = 3072
HD = 64
RIM = 45
TOK = 96
HALF = 48
LEN_ALL = 5952
TRAIN_STEPS = 1000
STEP_GAP = 20
NY, NA, NB, NX, NC = 4, 4, 4, 4, 2
NG = NY * NB
NHEAD = 8
EPSILON = 1e-06
MASKED = -1e30
FLOOR = -0.5e30
HEAD_OF = (0, 0, 0, 1, 1, 1, 2, 2, 2, 3, 3, 3, 4, 4, 5, 5)
PART_OF = (0, 1, 2, 0, 1, 2, 0, 1, 2, 0, 1, 2, 0, 1, 0, 1)
SIZE_OF = (32,) * 12 + (48,) * 4
BF = jnp.bfloat16
F32 = jnp.float32
SMEM = pltpu.SMEM
VMEM = pltpu.VMEM


def low_lanes(rows):
    return lax.broadcasted_iota(jnp.int32, (rows, 128), 1) < HD


def swap(x):
    return pltpu.roll(x, HD, 1)


def pack_kernel(q_ref, k_ref, v_ref, out_ref):
    low_h, low_t = low_lanes(HALF), low_lanes(TOK)
    for pair in range(3):
        lanes = slice(128 * pair, 128 * pair + 128)
        q = q_ref[:, lanes].astype(F32) * 0.125
        k = k_ref[:, lanes].astype(F32)
        v = v_ref[:, lanes].astype(F32)
        top, bottom = q[:HALF], q[HALF:]
        queries = (jnp.where(low_h, top, swap(bottom)), jnp.where(low_h, swap(top), bottom))
        keyvals = (jnp.where(low_t, k, swap(v)), jnp.where(low_t, swap(k), v))
        for side in range(2):
            qh = queries[side].astype(BF)
            kvh = keyvals[side].astype(BF)
            for d in range(NG):
                if HEAD_OF[d] != 2 * pair + side:
                    continue
                size = SIZE_OF[d]
                start = PART_OF[d] * size
                out_ref[d, :HALF, :] = qh
                out_ref[d, HALF : HALF + size, :] = kvh[start : start + size]
                if size < HALF:
                    out_ref[d, HALF + size :, :] = jnp.zeros((HALF - size, 128), BF)


def pieces(x):
    hi = x.astype(BF).astype(F32)
    rest = x - hi
    mid = rest.astype(BF).astype(F32)
    return (hi, mid, rest - mid)


QT = NB * TOK
KT = NA * NB * HALF
ROWS = 80


def attend_kernel(scal_ref, q_ref, kv_ref, out_ref, key_ref, val_ref, query_ref, top_ref, acc_ref):
    first_len, column, size, offset = scal_ref[0], scal_ref[1], scal_ref[2], scal_ref[3]
    row_tok = NA * NB * TOK
    lane3 = lax.broadcasted_iota(jnp.int32, (NA * NB, HALF, 128), 2)
    slot = lax.broadcasted_iota(jnp.int32, (NA * NB, HALF, 128), 1)
    block = lax.broadcasted_iota(jnp.int32, (NA * NB, HALF, 128), 0) * TOK + slot
    low = low_lanes(HALF)
    lane_q = lax.broadcasted_iota(jnp.int32, (16, QT), 1)
    row_q = lax.broadcasted_iota(jnp.int32, (16, QT), 0)
    part = NB * HALF
    ones = (lax.broadcasted_iota(jnp.int32, (ROWS - HD, KT), 0) == 0).astype(F32)
    for j in range(NY):
        pos = jnp.where(slot < size, block + (j * row_tok + offset), LEN_ALL)
        own = jnp.where(pos < first_len, 0, jnp.where(pos < LEN_ALL, 1, -1))
        extra = jnp.where((lane3 < 3) & (lane3 != own), MASKED, 0.0)
        key_ref[j, :, 128:] = extra.reshape(KT, 128).astype(BF)
        for i in range(NA):
            rows = slice(i * part, (i + 1) * part)
            start = (i * NY + j) * part
            key_ref[j, rows, :128] = kv_ref[start : start + part, :]
        turned = key_ref[j, :, :128].astype(F32).T
        val_ref[j] = jnp.concatenate([turned[HD:], ones], axis=0).astype(BF)

        stack = []
        for c in range(NB):
            q = q_ref[j * NB + c, :HALF, :].astype(F32)
            stack += [jnp.where(low, q, 0.0), jnp.where(low, swap(q), 0.0)]
        query_ref[j, :128, :] = jnp.concatenate(stack, axis=0).T.astype(BF)
        pos = lane_q + (j * row_tok + column * QT)
        own = jnp.where(pos < first_len, 0, jnp.where(pos < LEN_ALL, 1, 2))
        query_ref[j, 128:144, :] = jnp.where(row_q == own, 1.0, 0.0).astype(BF)
        query_ref[j, 144:, :] = jnp.zeros((112, QT), BF)
    top_ref[...] = jnp.full_like(top_ref, FLOOR)
    acc_ref[...] = jnp.zeros_like(acc_ref)

    def holds(start, stop):
        stop = jnp.minimum(stop, LEN_ALL)
        return start < first_len, (stop > first_len) & (start < stop)

    def visit(number, carry):
        j, t = number // NY, number % NY
        start = t * row_tok + column * QT
        q_first, q_second = holds(start, start + QT)
        k_first, k_second = holds(j * row_tok, (j + 1) * row_tok)

        @pl.when((q_first & k_first) | (q_second & k_second))
        def _():
            scores = jnp.dot(key_ref[j], query_ref[t], preferred_element_type=F32)
            old = top_ref[t, :1, :]
            new = jnp.maximum(jnp.max(scores, axis=0, keepdims=True), old)
            weights = jnp.exp(scores - new).astype(BF)
            acc_ref[t] = acc_ref[t] * jnp.exp(old - new) + jnp.dot(
                val_ref[j], weights, preferred_element_type=F32
            )
            top_ref[t] = jnp.broadcast_to(new, (8, QT))

        return carry

    lax.fori_loop(0, NY * NY, visit, 0)

    row8 = lax.broadcasted_iota(jnp.int32, (8, QT), 0)
    for t in range(NY):
        sums = acc_ref[t, HD : HD + 1, :]
        stats = jnp.zeros((8, QT), F32)
        for number, piece in enumerate(pieces(top_ref[t, :1, :]) + pieces(sums)):
            stats = jnp.where(row8 == number, piece, stats)
        whole = jnp.concatenate(
            [acc_ref[t, :HD, :] * (1.0 / jnp.where(sums > 0.0, sums, 1.0)), stats], axis=0
        )
        for c in range(NB):
            moved = pltpu.roll(whole, QT - c * TOK, 1) if c else whole
            out_ref[t * NB + c] = moved[:, :128].astype(BF)


def merge_kernel(part_ref, w_ref, out_ref, att_ref, copy_ref, sem):
    copy = pltpu.make_async_copy(w_ref, copy_ref, sem)
    copy.start()
    stat = part_ref[:, HD:, :].astype(F32)
    tops = stat[:, 0] + stat[:, 1] + stat[:, 2]
    sums = stat[:, 3] + stat[:, 4] + stat[:, 5]
    for h in range(6):
        own = [d for d in range(NG) if HEAD_OF[d] == h]
        rows = slice(own[0], own[-1] + 1)
        top = jnp.max(tops[rows], axis=0, keepdims=True)
        scaled = jnp.exp(tops[rows] - top) * sums[rows]
        total = jnp.sum(scaled, axis=0, keepdims=True)
        shares = scaled / jnp.where(total > 0.0, total, 1.0)
        mixed = jnp.zeros((HD, 128), F32)
        for i, d in enumerate(own):
            mixed += shares[i : i + 1] * part_ref[d, :HD, :].astype(F32)
        att_ref[HD * h : HD * h + HD, :] = mixed
    attended = att_ref[...].T[:TOK].astype(BF)
    copy.wait()
    for j in range(NHEAD):
        out_ref[j] = jnp.dot(
            attended, copy_ref[:, 384 * j : 384 * j + 384], preferred_element_type=F32
        ).astype(BF)


def split2(x):
    hi = x.astype(BF)
    return hi, (x - hi.astype(F32)).astype(BF)


def stream_kernel(
    scal_ref, term_ref, hid_ref, gate_ref, shift_ref, scale_ref, w_ref, hid_out, msg_ref
):
    first_len, base = scal_ref[0], scal_ref[4]
    projected = term_ref[0].astype(F32)
    for j in range(1, NHEAD):
        projected += term_ref[j].astype(F32)
    pos = base + lax.broadcasted_iota(jnp.int32, (TOK, 384), 0)
    first, second = pos < first_len, pos < LEN_ALL

    def per_row(table):
        return jnp.where(first, table[0:1], jnp.where(second, table[1:2], 0.0))

    gate, shift = gate_ref[...].astype(F32), shift_ref[...].astype(F32)
    factor = 1.0 + scale_ref[...].astype(F32)
    x = (hid_ref[...].astype(F32) + per_row(gate) * projected).astype(BF)
    hid_out[...] = x
    xf = x.astype(F32)
    scaled = jnp.concatenate(
        [xf * per_row(factor), factor, shift, jnp.zeros((28, 384), F32)], axis=0
    )
    sq_hi, sq_lo = split2(xf * xf)
    ones = jnp.ones((8, 384), BF)

    def turn(left, right):
        return lax.dot_general(left, right, (((1,), (1,)), ((), ())), preferred_element_type=F32)

    high, rest = split2(scaled)
    w = w_ref[...]
    a = turn(w, high) + turn(w, rest)
    total = turn(ones, x)
    squares = turn(ones, sq_hi) + turn(ones, sq_lo)
    rows8 = lax.broadcasted_iota(jnp.int32, (8, TOK), 0)
    tail = jnp.where(rows8 == 0, total, squares)
    for j in range(NHEAD):
        msg_ref[j, :64, :] = a
        msg_ref[j, 64:, :TOK] = tail
        msg_ref[j, 64:, TOK:] = jnp.zeros((8, 128 - TOK), F32)


def step_kernel(scal_ref, coef_ref, msg_ref, lat_ref, clean_ref, prev_ref):
    first_len, base = scal_ref[0], scal_ref[4]
    total = msg_ref[0]
    for j in range(1, NHEAD):
        total += msg_ref[j]
    pos = base + lax.broadcasted_iota(jnp.int32, (64, TOK), 1)
    first, live = pos < first_len, pos < LEN_ALL
    mean = total[64:65, :TOK] * (1.0 / D)
    var = total[65:66, :TOK] * (1.0 / D) - mean * mean
    scale_w = jnp.where(first, total[:64, TOK : TOK + 1], total[:64, TOK + 1 : TOK + 2])
    shift_w = jnp.where(first, total[:64, TOK + 2 : TOK + 3], total[:64, TOK + 3 : TOK + 4])
    velocity = lax.rsqrt(var + EPSILON) * (total[:64, :TOK] - mean * scale_w) + shift_w
    latent = lat_ref[...]

    def row_coef(i):
        return jnp.where(first, coef_ref[2 * i], coef_ref[2 * i + 1])

    root_a, root_1a, root_q, root_1q = (row_coef(i) for i in range(4))
    clean = root_a * latent - root_1a * velocity
    noise = root_1a * latent + root_a * velocity
    stepped = root_q * clean + root_1q * noise
    clean_ref[...] = jnp.where(live, clean, 0.0)
    prev_ref[...] = jnp.where(live, stepped, 0.0)


def alpha_table():
    betas = np.linspace(0.00085**0.5, 0.012**0.5, TRAIN_STEPS) ** 2
    return np.cumprod(1.0 - betas).astype(np.float32)


def request_of(position, first_len):
    return jnp.where(
        position < 0, -1, jnp.where(position < first_len, 0, jnp.where(position < LEN_ALL, 1, 2))
    )


def shards(
    lengths,
    step_index,
    query_act,
    key_act,
    value_act,
    hidden,
    attn_weight,
    gate_mod,
    shift_mod,
    scale_mod,
    proj_weight,
    latent,
):
    y, column, c = lax.axis_index("y"), lax.axis_index("a"), lax.axis_index("c")
    seq = (y * NA + column) * NB + c
    member = y * NB + c
    first_len = lengths[0]
    size = jnp.where(member < 12, 32, 48)
    part = jnp.where(member < 12, member % 3, member % 2)
    scal = jnp.stack([first_len, column, size, part * size, seq * TOK]).astype(jnp.int32)
    in_smem = pl.BlockSpec(memory_space=SMEM)
    big = pltpu.CompilerParams(vmem_limit_bytes=48 * 1024 * 1024)

    any_vmem = pl.BlockSpec(memory_space=VMEM)

    packed = pl.pallas_call(
        pack_kernel, out_shape=jax.ShapeDtypeStruct((NG, TOK, 128), BF), name="pack"
    )(query_act, key_act, value_act)
    mine = lax.all_to_all(packed, ("y", "c"), 0, 0, tiled=True)
    keyvals = lax.all_gather(mine[:, HALF:].reshape(NG * HALF, 128), "a", axis=0, tiled=True)
    partial = pl.pallas_call(
        attend_kernel,
        out_shape=jax.ShapeDtypeStruct((NG, HD + 8, 128), BF),
        in_specs=[in_smem, any_vmem, any_vmem],
        out_specs=any_vmem,
        scratch_shapes=[
            VMEM((NY, KT, 256), BF),
            VMEM((NY, ROWS, KT), BF),
            VMEM((NY, 256, QT), BF),
            VMEM((NY, 8, QT), F32),
            VMEM((NY, ROWS, QT), F32),
        ],
        compiler_params=big,
        name="attend",
    )(scal, mine, keyvals)
    parts = lax.all_to_all(partial, ("y", "c"), 0, 0, tiled=True)
    term = pl.pallas_call(
        merge_kernel,
        out_shape=jax.ShapeDtypeStruct((NHEAD, TOK, 384), BF),
        in_specs=[any_vmem, pl.BlockSpec(memory_space=pl.ANY)],
        out_specs=any_vmem,
        scratch_shapes=[VMEM((384, 128), F32), VMEM((384, D), BF), pltpu.SemaphoreType.DMA],
        compiler_params=big,
        name="merge",
    )(parts, attn_weight)
    terms = lax.all_to_all(term, ("x", "core"), 0, 0, tiled=True)
    hidden_out, message = pl.pallas_call(
        stream_kernel,
        out_shape=(
            jax.ShapeDtypeStruct((TOK, 384), BF),
            jax.ShapeDtypeStruct((NHEAD, 72, 128), F32),
        ),
        in_specs=[in_smem] + [any_vmem] * 6,
        name="stream",
    )(scal, terms, hidden, gate_mod, shift_mod, scale_mod, proj_weight.T)
    message = lax.all_to_all(message, ("x", "core"), 0, 0, tiled=True)
    table = jnp.asarray(alpha_table())
    alpha_now = table[step_index]
    alpha_prev = table[step_index - STEP_GAP]
    coef = jnp.concatenate(
        [
            jnp.sqrt(alpha_now),
            jnp.sqrt(1.0 - alpha_now),
            jnp.sqrt(alpha_prev),
            jnp.sqrt(1.0 - alpha_prev),
        ]
    )
    clean, stepped = pl.pallas_call(
        step_kernel,
        out_shape=(jax.ShapeDtypeStruct((64, TOK), F32),) * 2,
        in_specs=[in_smem, in_smem, any_vmem, any_vmem],
        name="ddim",
    )(scal, coef, message, latent.T)
    pairs = []
    for s in range(NY * NA * NB):
        for x in range(NX):
            up, down = (s * NX + x) * NC, (s * NX + x) * NC + 1
            if s + 1 < NY * NA * NB:
                pairs.append((up, up + NX * NC))
            if s > 0:
                pairs.append((down, down - NX * NC))
    got = lax.ppermute(stepped, ("y", "a", "c", "x", "core"), pairs)
    both = lax.all_gather(got, "core")
    offsets = jnp.arange(RIM, dtype=jnp.int32)
    start = seq * TOK
    lower_ok = request_of(start - RIM + offsets, first_len) == request_of(start, first_len)
    upper_ok = request_of(start + TOK + offsets, first_len) == request_of(
        start + TOK - 1, first_len
    )
    lower_ok &= start > 0
    upper_ok &= start + TOK < NY * NA * NB * TOK
    rims = jnp.concatenate(
        [
            jnp.where(lower_ok[None], both[0, :, TOK - RIM :], 0.0),
            jnp.where(upper_ok[None], both[1, :, :RIM], 0.0),
        ],
        axis=1,
    )
    return hidden_out, clean.T, stepped.T, rims.T


def solution(mesh):
    grid = Mesh(mesh.devices.reshape(NY, NA, NB, NX, NC), ("y", "a", "c", "x", "core"))
    seq, head = ("y", "a", "c"), ("x", "core")
    in_specs = (
        P(),
        P(),
        P(seq, head),
        P(seq, head),
        P(seq, head),
        P(seq, head),
        P(head, None),
        P(None, head),
        P(None, head),
        P(None, head),
        P(head, None),
        P(seq, None),
    )
    out_specs = (P(seq, head), P(seq, None), P(seq, None), P(seq, None))
    return jax.shard_map(shards, mesh=grid, in_specs=in_specs, out_specs=out_specs, check_vma=False)
```

time: 145 us -> 132 us (0.910)
  Pallas kernels: 26.6 us -> 18.3 us
  starting transfers between devices: 38.1 us -> 30.7 us
  waiting for transfers between devices: 29.7 us -> 35.1 us
  blocking collectives: 44.1 us -> 41.7 us
    all_to_all x1 -> x0, blocking collectives: 27.5 us -> none  [shards(): keyvals = lax.all_to_all(keyvals, 'z', 0, 0, tiled=True)]
    all_gather x1, blocking collectives: 11.1 us -> 36.6 us  [shards(): lax.all_gather(mine[:, HALF:].reshape(NG * HALF, 128), 'a', axis=0, tiled...]
    pallas_call x2, Pallas kernels: 20.5 us -> 12.6 us  [the longest x1 10.6 us: shards(): pl.pallas_call(attend_kernel, out_shape=jax.ShapeDtypeStruct((NG, HD + 8,...]
    all_to_all x2, waiting for transfers between devices: 13.1 us -> 18.7 us  [the longest x1 10.2 us: shards(): mine = lax.all_to_all(packed, ('y', 'c'), 0, 0, tiled=True)]
    all_to_all x1, starting transfers between devices: 10.7 us -> 6.15 us  [shards(): terms = lax.all_to_all(term, ('x', 'core'), 0, 0, tiled=True)]
    all_to_all x2, starting transfers between devices: 19.6 us -> 16.2 us  [the longest x1 8.21 us: shards(): mine = lax.all_to_all(packed, ('y', 'c'), 0, 0, tiled=True)]
where the time goes in v3:
time: 132 us
  blocking collectives  41.7 us (32%)
  waiting for transfers between devices  35.1 us (27%)
  starting transfers between devices  30.7 us (23%)
  Pallas kernels  18.3 us (14%)
  local copies, waits for them, and re-layouts  3.57 us (3%)
  other arithmetic  1.46 us (1%)
    all_gather x1, blocking collectives, shards(): lax.all_gather(mine[:, HALF:].reshape(NG * HALF, 128), 'a', axis=0, tiled...  36.6 us
    pallas_call x1, Pallas kernels, shards(): pl.pallas_call(attend_kernel, out_shape=jax.ShapeDtypeStruct((NG, HD + 8,...  10.6 us
    all_to_all x1, waiting for transfers between devices, shards(): mine = lax.all_to_all(packed, ('y', 'c'), 0, 0, tiled=True)  10.2 us
    all_to_all x1, waiting for transfers between devices, shards(): terms = lax.all_to_all(term, ('x', 'core'), 0, 0, tiled=True)  8.89 us
    all_to_all x1, waiting for transfers between devices, shards(): parts = lax.all_to_all(partial, ('y', 'c'), 0, 0, tiled=True)  8.58 us
    all_to_all x1, starting transfers between devices, shards(): mine = lax.all_to_all(packed, ('y', 'c'), 0, 0, tiled=True)  8.21 us
    all_to_all x1, starting transfers between devices, shards(): parts = lax.all_to_all(partial, ('y', 'c'), 0, 0, tiled=True)  7.97 us
    all_to_all x1, waiting for transfers between devices, shards(): message = lax.all_to_all(message, ('x', 'core'), 0, 0, tiled=True)  6.2 us
  transfers between devices with their start and end apart: 5, of which 5 were waited for; matrix products, arithmetic and copies ran while one was open for 2% of the time, Pallas kernels for 0%

profile of v3, /device:TPU:25, one launch (start us, length us, event | category | flops | bytes accessed | tf_op | source)
XLA Modules:
  0.0 131.7 jit_solution(665948926524559196)
XLA Ops:
  0.6 0.0 copy-start.5
  0.6 0.0 copy-start
  0.7 2.0 %pack.1 = bf16[16,96,128]{2,1,0:T(8,128)(2,1)} custom-call(bf16[96,384]{1,0:T(8,128)(2,1)} %q_ref.1, bf16[96,384]{1,0:T(8,128)(2,1)} %k_ref.1, bf16[96,384]{1,0:T(8,128)(2,1)} %v_ref.1), custom_call_target="tpu_custom_call" | custom-call | tf_op jit(solution)/shard_map/pack/pallas_call | solution.py:283
  2.6 8.2 %all-to-all-start = ((bf16[16,96,128]{2,1,0:T(8,128)(2,1)}), bf16[16,96,128]{2,1,0:T(8,128)(2,1)S(1)}, u32[]{:S(2)}, u32[]{:S(2)}) async-start(bf16[16,96,128]{2,1,0:T(8,128)(2,1)} %pack.1), calls=%async_computation | async-start | bytes 786432 | tf_op jit(solution)/shard_map/all_to_all | solution.py:286
  10.8 0.7 stack.19.scal_ref
  11.6 0.0 copy-start.1
  11.6 10.2 %all-to-all-done.q_ref = bf16[16,96,128]{2,1,0:T(8,128)(2,1)S(1)} async-done(((bf16[16,96,128]{2,1,0:T(8,128)(2,1)}), bf16[16,96,128]{2,1,0:T(8,128)(2,1)S(1)}, u32[]{:S(2)}, u32[]{:S(2)}) %all-to-all-start) | async-done | bytes 393248 | tf_op jit(solution)/shard_map/all_to_all | solution.py:286
  21.8 36.6 %all_gather.9.kv_ref = bf16[3072,128]{1,0:T(8,128)(2,1)S(1)} all-gather(bf16[768,128]{1,0:T(8,128)(2,1)S(1)} %bitcast.22), channel_id=1, replica_groups=mesh['y'=4,'a'=4,'c'=4,'x'=4,'core'=2] {'a'}, dimensions={0}, use_global_device_ids=true | all-gather | bytes 983040 | tf_op jit(solution)/shard_map/all_gather | solution.py:287
  58.3 10.6 %attend.1 = bf16[16,72,128]{2,1,0:T(8,128)(2,1)} custom-call(s32[5]{0:T(128)S(1)} %stack.19.scal_ref, bf16[16,96,128]{2,1,0:T(8,128)(2,1)S(1)} %all-to-all-done.q_ref, bf16[3072,128]{1,0:T(8,128)(2,1)S(1)} %all_gather.9.kv_ref), custom_call_target="tpu_custom_call" | custom-call | tf_op jit(solution)/shard_map/attend/pallas_call | solution.py:288
  68.9 8.0 %all-to-all-start.1 = ((bf16[16,72,128]{2,1,0:T(8,128)(2,1)}), bf16[16,72,128]{2,1,0:T(8,128)(2,1)S(1)}, u32[]{:S(2)}, u32[]{:S(2)}) async-start(bf16[16,72,128]{2,1,0:T(8,128)(2,1)} %attend.1), calls=%async_computation.1 | async-start | bytes 589824 | tf_op jit(solution)/shard_map/all_to_all | solution.py:303
  76.9 0.0 copy-start.6
  76.9 0.0 copy-start.2
  76.9 0.0 copy-done.5
  77.0 8.6 %all-to-all-done.1.part_ref = bf16[16,72,128]{2,1,0:T(8,128)(2,1)S(1)} async-done(((bf16[16,72,128]{2,1,0:T(8,128)(2,1)}), bf16[16,72,128]{2,1,0:T(8,128)(2,1)S(1)}, u32[]{:S(2)}, u32[]{:S(2)}) %all-to-all-start.1) | async-done | bytes 294944 | tf_op jit(solution)/shard_map/all_to_all | solution.py:303
  85.6 0.0 copy-done
  85.6 1.8 %merge.1 = bf16[8,96,384]{2,1,0:T(8,128)(2,1)} custom-call(bf16[16,72,128]{2,1,0:T(8,128)(2,1)S(1)} %all-to-all-done.1.part_ref, bf16[384,3072]{1,0:T(8,128)(2,1)S(1)} %copy-done), custom_call_target="tpu_custom_call" | custom-call | tf_op jit(solution)/shard_map/merge/pallas_call | solution.py:304
  87.4 0.0 copy-done.1
  87.4 6.2 %all-to-all-start.2 = ((bf16[8,96,384]{2,1,0:T(8,128)(2,1)}), bf16[8,96,384]{2,1,0:T(8,128)(2,1)S(1)}, u32[]{:S(2)}, u32[]{:S(2)}) async-start(bf16[8,96,384]{2,1,0:T(8,128)(2,1)} %merge.1), calls=%async_computation.2 | async-start | bytes 1179648 | tf_op jit(solution)/shard_map/all_to_all | solution.py:313
  93.5 0.0 copy-done.6
  93.6 0.0 copy-done.2
  93.6 0.6 gather_fusion
  94.2 0.6 gather_fusion.1
  94.8 8.9 %all-to-all-done.2.term_ref = bf16[8,96,384]{2,1,0:T(8,128)(2,1)S(1)} async-done(((bf16[8,96,384]{2,1,0:T(8,128)(2,1)}), bf16[8,96,384]{2,1,0:T(8,128)(2,1)S(1)}, u32[]{:S(2)}, u32[]{:S(2)}) %all-to-all-start.2) | async-done | bytes 589856 | tf_op jit(solution)/shard_map/all_to_all | solution.py:313
  103.7 0.0 copy-start.3
  103.7 0.8 copy-done.3
  104.5 2.3 %stream.1 = (bf16[96,384]{1,0:T(8,128)(2,1)}, f32[8,72,128]{2,1,0:T(8,128)}) custom-call(s32[5]{0:T(128)} %copy-done.1, bf16[8,96,384]{2,1,0:T(8,128)(2,1)} %copy-done.3, bf16[96,384]{1,0:T(8,128)(2,1)} %hid_ref.1, bf16[2,384]{1,0:T(2,128)(2,1)} %gate_ref.1, bf16[2,384]{1,0:T(2,128)(2,1)} %shift_ref.1, bf16[2,384]{1,0:T(2,128)(2,1)} %scale_ref.1, ...), custom_call_target="tpu_custom_call" | custom-call | tf_op jit(solution)/shard_map/stream/pallas_call | solution.py:314
  106.8 4.2 %all-to-all-start.3 = ((f32[8,72,128]{2,1,0:T(8,128)}), f32[8,72,128]{2,1,0:T(8,128)S(1)}, u32[]{:S(2)}, u32[]{:S(2)}) async-start(f32[8,72,128]{2,1,0:T(8,128)} %get-tuple-element.9), calls=%async_computation.3 | async-start | bytes 589824 | tf_op jit(solution)/shard_map/all_to_all | solution.py:323
  111.0 0.6 pad_maximum_fusion.coef_ref
  111.6 6.2 %all-to-all-done.3.msg_ref = f32[8,72,128]{2,1,0:T(8,128)S(1)} async-done(((f32[8,72,128]{2,1,0:T(8,128)}), f32[8,72,128]{2,1,0:T(8,128)S(1)}, u32[]{:S(2)}, u32[]{:S(2)}) %all-to-all-start.3) | async-done | bytes 294944 | tf_op jit(solution)/shard_map/all_to_all | solution.py:323
  117.8 0.0 copy-start.4
  117.8 0.7 copy-done.4
  118.5 1.7 %ddim.1 = (f32[64,96]{1,0:T(8,128)}, f32[64,96]{1,0:T(8,128)}) custom-call(s32[5]{0:T(128)} %copy-done.1, f32[8]{0:T(128)} %pad_maximum_fusion.coef_ref, f32[8,72,128]{2,1,0:T(8,128)} %copy-done.4, f32[64,96]{1,0:T(8,128)} %bitcast.25), custom_call_target="tpu_custom_call" | custom-call | tf_op jit(solution)/shard_map/ddim/pallas_call | solution.py:335
  120.3 4.2 %collective-permute-start = (f32[64,96]{1,0:T(8,128)}, f32[64,96]{1,0:T(8,128)S(1)}, u32[]{:S(2)}, u32[]{:S(2)}) collective-permute-start(f32[64,96]{1,0:T(8,128)} %get-tuple-element.11), channel_id=1, source_target_pairs={{0,8},{2,10},{4,12},{6,14},{8,16},{9,1},{10,18},{11,3},{12,20},{13... | collective-permute-start | bytes 73736 | tf_op jit(solution)/shard_map/ppermute | solution.py:349
  124.5 1.3 collective-permute-done
  125.8 5.1 %all-gather = f32[128,96]{1,0:T(8,128)S(1)} all-gather(f32[64,96]{1,0:T(8,128)S(1)} %collective-permute-done), channel_id=2, replica_groups=mesh['y'=4,'a'=4,'c'=4,'x'=4,'core'=2] {'core'}, dimensions={0}, use_global_device_ids=true | all-gather | bytes 73728 | tf_op jit(solution)/shard_map/all_gather | solution.py:350
  131.0 0.1 fusion.1
  131.0 0.7 maximum_bitcast_fusion
  (6 shorter events, 0.1 us)
Async XLA Ops:
  0.6 76.3 %copy-start.5 = (s32[2]{0:T(128)S(1)}, s32[2]{0:T(128)}, u32[]{:S(2)}) copy-start(s32[2]{0:T(128)} %param.13) | copy-start | bytes 28
  0.6 84.9 %copy-start = (bf16[384,3072]{1,0:T(8,128)(2,1)S(1)}, bf16[384,3072]{1,0:T(8,128)(2,1)}, u32[]{:S(2)}) copy-start(bf16[384,3072]{1,0:T(8,128)(2,1)} %w_ref.1) | copy-start | bytes 7077892
  2.6 19.1 %all-to-all-start = ((bf16[16,96,128]{2,1,0:T(8,128)(2,1)}), bf16[16,96,128]{2,1,0:T(8,128)(2,1)S(1)}, u32[]{:S(2)}, u32[]{:S(2)}) async-start(bf16[16,96,128]{2,1,0:T(8,128)(2,1)} %pack.1), calls=%async_computation | async-start | bytes 786432 | tf_op jit(solution)/shard_map/all_to_all | solution.py:286
  11.6 75.8 %copy-start.1 = (s32[5]{0:T(128)}, s32[5]{0:T(128)S(1)}, u32[]{:S(2)}) copy-start(s32[5]{0:T(128)S(1)} %stack.19.scal_ref) | copy-start | bytes 64
  68.9 16.7 %all-to-all-start.1 = ((bf16[16,72,128]{2,1,0:T(8,128)(2,1)}), bf16[16,72,128]{2,1,0:T(8,128)(2,1)S(1)}, u32[]{:S(2)}, u32[]{:S(2)}) async-start(bf16[16,72,128]{2,1,0:T(8,128)(2,1)} %attend.1), calls=%async_computation.1 | async-start | bytes 589824 | tf_op jit(solution)/shard_map/all_to_all | solution.py:303
  76.9 16.6 %copy-start.6 = (s32[2]{0:T(128)S(1)}, s32[2]{0:T(128)}, u32[]{:S(2)}) copy-start(s32[2]{0:T(128)} %param.14) | copy-start | bytes 28
  76.9 16.6 %copy-start.2 = (f32[1000]{0:T(1024)S(1)}, f32[1000]{0:T(1024)}, u32[]{:S(2)}) copy-start(f32[1000]{0:T(1024)} %constant.73.clone) | copy-start | bytes 12004
  87.4 16.3 %all-to-all-start.2 = ((bf16[8,96,384]{2,1,0:T(8,128)(2,1)}), bf16[8,96,384]{2,1,0:T(8,128)(2,1)S(1)}, u32[]{:S(2)}, u32[]{:S(2)}) async-start(bf16[8,96,384]{2,1,0:T(8,128)(2,1)} %merge.1), calls=%async_computation.2 | async-start | bytes 1179648 | tf_op jit(solution)/shard_map/all_to_all | solution.py:313
  103.7 0.8 copy-start.3
  106.8 11.0 %all-to-all-start.3 = ((f32[8,72,128]{2,1,0:T(8,128)}), f32[8,72,128]{2,1,0:T(8,128)S(1)}, u32[]{:S(2)}, u32[]{:S(2)}) async-start(f32[8,72,128]{2,1,0:T(8,128)} %get-tuple-element.9), calls=%async_computation.3 | async-start | bytes 589824 | tf_op jit(solution)/shard_map/all_to_all | solution.py:323
  117.8 0.7 copy-start.4
  120.3 5.6 %collective-permute-start = (f32[64,96]{1,0:T(8,128)}, f32[64,96]{1,0:T(8,128)S(1)}, u32[]{:S(2)}, u32[]{:S(2)}) collective-permute-start(f32[64,96]{1,0:T(8,128)} %get-tuple-element.11), channel_id=1, source_target_pairs={{0,8},{2,10},{4,12},{6,14},{8,16},{9,1},{10,18},{11,3},{12,20},{13... | collective-permute-start | bytes 73736 | tf_op jit(solution)/shard_map/ppermute | solution.py:349

commit v4 on v3

--- a/solution.py
+++ b/solution.py
@@ -70,8 +70,11 @@
 
 
 QT = NB * TOK
+QP = 2 * QT
 KT = NA * NB * HALF
+KC = 384
 ROWS = 80
+KEPT = 48
 
 
 def attend_kernel(scal_ref, q_ref, kv_ref, out_ref, key_ref, val_ref, query_ref, top_ref, acc_ref):
@@ -84,28 +87,34 @@
     lane_q = lax.broadcasted_iota(jnp.int32, (16, QT), 1)
     row_q = lax.broadcasted_iota(jnp.int32, (16, QT), 0)
     part = NB * HALF
-    ones = (lax.broadcasted_iota(jnp.int32, (ROWS - HD, KT), 0) == 0).astype(F32)
+    ones = (lax.broadcasted_iota(jnp.int32, (ROWS - HD, KC), 0) == 0).astype(F32)
     for j in range(NY):
         pos = jnp.where(slot < size, block + (j * row_tok + offset), LEN_ALL)
         own = jnp.where(pos < first_len, 0, jnp.where(pos < LEN_ALL, 1, -1))
         extra = jnp.where((lane3 < 3) & (lane3 != own), MASKED, 0.0)
-        key_ref[j, :, 128:] = extra.reshape(KT, 128).astype(BF)
-        for i in range(NA):
-            rows = slice(i * part, (i + 1) * part)
-            start = (i * NY + j) * part
-            key_ref[j, rows, :128] = kv_ref[start : start + part, :]
-        turned = key_ref[j, :, :128].astype(F32).T
-        val_ref[j] = jnp.concatenate([turned[HD:], ones], axis=0).astype(BF)
+        extra = extra.reshape(KT, 128).astype(BF)
+        keyvals = jnp.concatenate(
+            [kv_ref[(i * NY + j) * part : (i * NY + j + 1) * part, :] for i in range(NA)], axis=0
+        )
+        turned = keyvals.astype(F32).T
+        for i in range(KT // KC):
+            rows = slice(i * KC, (i + 1) * KC)
+            key_ref[j * (KT // KC) + i, :, :128] = keyvals[rows]
+            key_ref[j * (KT // KC) + i, :, 128:] = extra[rows]
+            val_ref[j * (KT // KC) + i] = jnp.concatenate(
+                [turned[HD:, i * KC : (i + 1) * KC], ones], axis=0
+            ).astype(BF)
 
         stack = []
         for c in range(NB):
             q = q_ref[j * NB + c, :HALF, :].astype(F32)
             stack += [jnp.where(low, q, 0.0), jnp.where(low, swap(q), 0.0)]
-        query_ref[j, :128, :] = jnp.concatenate(stack, axis=0).T.astype(BF)
+        pair, lanes = j // 2, slice(j % 2 * QT, j % 2 * QT + QT)
+        query_ref[pair, :128, lanes] = jnp.concatenate(stack, axis=0).T.astype(BF)
         pos = lane_q + (j * row_tok + column * QT)
         own = jnp.where(pos < first_len, 0, jnp.where(pos < LEN_ALL, 1, 2))
-        query_ref[j, 128:144, :] = jnp.where(row_q == own, 1.0, 0.0).astype(BF)
-        query_ref[j, 144:, :] = jnp.zeros((112, QT), BF)
+        query_ref[pair, 128:144, lanes] = jnp.where(row_q == own, 1.0, 0.0).astype(BF)
+        query_ref[pair, 144:, lanes] = jnp.zeros((112, QT), BF)
     top_ref[...] = jnp.full_like(top_ref, FLOOR)
     acc_ref[...] = jnp.zeros_like(acc_ref)
 
@@ -113,45 +122,58 @@
         stop = jnp.minimum(stop, LEN_ALL)
         return start < first_len, (stop > first_len) & (start < stop)
 
+    def absorb(j, t, lanes):
+        scores = jnp.dot(key_ref[j], query_ref[t, :, lanes], preferred_element_type=F32)
+        old = top_ref[t, :1, lanes]
+        new = jnp.maximum(jnp.max(scores, axis=0, keepdims=True), old)
+        weights = jnp.exp(scores - new).astype(BF)
+        acc_ref[t, :, lanes] = acc_ref[t, :, lanes] * jnp.exp(old - new) + jnp.dot(
+            val_ref[j], weights, preferred_element_type=F32
+        )
+        top_ref[t, :, lanes] = jnp.broadcast_to(new, (8, new.shape[1]))
+
     def visit(number, carry):
-        j, t = number // NY, number % NY
-        start = t * row_tok + column * QT
-        q_first, q_second = holds(start, start + QT)
-        k_first, k_second = holds(j * row_tok, (j + 1) * row_tok)
-
-        @pl.when((q_first & k_first) | (q_second & k_second))
-        def _():
-            scores = jnp.dot(key_ref[j], query_ref[t], preferred_element_type=F32)
-            old = top_ref[t, :1, :]
-            new = jnp.maximum(jnp.max(scores, axis=0, keepdims=True), old)
-            weights = jnp.exp(scores - new).astype(BF)
-            acc_ref[t] = acc_ref[t] * jnp.exp(old - new) + jnp.dot(
-                val_ref[j], weights, preferred_element_type=F32
-            )
-            top_ref[t] = jnp.broadcast_to(new, (8, QT))
-
+        j, t = number // 2, number % 2
+        k_first, k_second = holds(j * (2 * KC), (j + 1) * (2 * KC))
+
+        def needed(row):
+            start = row * row_tok + column * QT
+            q_first, q_second = holds(start, start + QT)
+            return (q_first & k_first) | (q_second & k_second)
+
+        left, right = needed(2 * t), needed(2 * t + 1)
+        pl.when(left & right)(lambda: absorb(j, t, slice(0, QP)))
+        pl.when(left & jnp.logical_not(right))(lambda: absorb(j, t, slice(0, QT)))
+        pl.when(right & jnp.logical_not(left))(lambda: absorb(j, t, slice(QT, QP)))
         return carry
 
-    lax.fori_loop(0, NY * NY, visit, 0)
+    lax.fori_loop(0, NY * KT // KC * 2, visit, 0)
 
     row8 = lax.broadcasted_iota(jnp.int32, (8, QT), 0)
+    lane_m = lax.broadcasted_iota(jnp.int32, (KEPT, 128), 1)
     for t in range(NY):
-        sums = acc_ref[t, HD : HD + 1, :]
+        pair, lanes = t // 2, slice(t % 2 * QT, t % 2 * QT + QT)
+        sums = acc_ref[pair, HD : HD + 1, lanes]
         stats = jnp.zeros((8, QT), F32)
-        for number, piece in enumerate(pieces(top_ref[t, :1, :]) + pieces(sums)):
+        for number, piece in enumerate(pieces(top_ref[pair, :1, lanes]) + pieces(sums)):
             stats = jnp.where(row8 == number, piece, stats)
         whole = jnp.concatenate(
-            [acc_ref[t, :HD, :] * (1.0 / jnp.where(sums > 0.0, sums, 1.0)), stats], axis=0
+            [acc_ref[pair, :HD, lanes] * (1.0 / jnp.where(sums > 0.0, sums, 1.0)), stats], axis=0
         )
         for c in range(NB):
             moved = pltpu.roll(whole, QT - c * TOK, 1) if c else whole
-            out_ref[t * NB + c] = moved[:, :128].astype(BF)
+            moved = moved[:, :128]
+            rest = moved[KEPT:HD]
+            thirds = [pltpu.roll(rest, (TOK - 32 * k) % 128, 1) for k in range(3)]
+            kept = jnp.where(lane_m < TOK, moved[:KEPT], jnp.concatenate(thirds, axis=0))
+            out_ref[t * NB + c] = jnp.concatenate([kept, moved[HD:]], axis=0).astype(BF)
 
 
 def merge_kernel(part_ref, w_ref, out_ref, att_ref, copy_ref, sem):
     copy = pltpu.make_async_copy(w_ref, copy_ref, sem)
     copy.start()
-    stat = part_ref[:, HD:, :].astype(F32)
+    lane_r = lax.broadcasted_iota(jnp.int32, (HD - KEPT, 128), 1)
+    stat = part_ref[:, KEPT:, :].astype(F32)
     tops = stat[:, 0] + stat[:, 1] + stat[:, 2]
     sums = stat[:, 3] + stat[:, 4] + stat[:, 5]
     for h in range(6):
@@ -163,7 +185,15 @@
         shares = scaled / jnp.where(total > 0.0, total, 1.0)
         mixed = jnp.zeros((HD, 128), F32)
         for i, d in enumerate(own):
-            mixed += shares[i : i + 1] * part_ref[d, :HD, :].astype(F32)
+            part = part_ref[d, :KEPT, :].astype(F32)
+            thirds = [
+                pltpu.roll(part[16 * k : 16 * k + 16], (32 * k + 128 - TOK) % 128, 1)
+                for k in range(3)
+            ]
+            rest = jnp.where(
+                lane_r < 32, thirds[0], jnp.where(lane_r < 64, thirds[1], thirds[2])
+            )
+            mixed += shares[i : i + 1] * jnp.concatenate([part, rest], axis=0)
         att_ref[HD * h : HD * h + HD, :] = mixed
     attended = att_ref[...].T[:TOK].astype(BF)
     copy.wait()
@@ -196,8 +226,9 @@
     x = (hid_ref[...].astype(F32) + per_row(gate) * projected).astype(BF)
     hid_out[...] = x
     xf = x.astype(F32)
+    own_mean = jnp.sum(xf, axis=1, keepdims=True) * (1.0 / 384)
     scaled = jnp.concatenate(
-        [xf * per_row(factor), factor, shift, jnp.zeros((28, 384), F32)], axis=0
+        [(xf - own_mean) * per_row(factor), factor, shift, jnp.zeros((28, 384), F32)], axis=0
     )
     sq_hi, sq_lo = split2(xf * xf)
     ones = jnp.ones((8, 384), BF)
@@ -208,28 +239,48 @@
     high, rest = split2(scaled)
     w = w_ref[...]
     a = turn(w, high) + turn(w, rest)
+    left = pltpu.roll(a - a.astype(BF).astype(F32), 4, 1)
+    lane = lax.broadcasted_iota(jnp.int32, (64, 128), 1)
+    a = jnp.where((lane >= TOK + 4) & (lane < TOK + 8), left, a).astype(BF)
     total = turn(ones, x)
     squares = turn(ones, sq_hi) + turn(ones, sq_lo)
     rows8 = lax.broadcasted_iota(jnp.int32, (8, TOK), 0)
-    tail = jnp.where(rows8 == 0, total, squares)
+    tail = jnp.zeros((8, TOK), F32)
+    for number, piece in enumerate(pieces(total) + pieces(squares)):
+        tail = jnp.where(rows8 == number, piece, tail)
+    tail = jnp.concatenate([tail, jnp.zeros((8, 128 - TOK), F32)], axis=1)
+    message = jnp.concatenate([a.astype(F32), tail], axis=0).astype(BF)
     for j in range(NHEAD):
-        msg_ref[j, :64, :] = a
-        msg_ref[j, 64:, :TOK] = tail
-        msg_ref[j, 64:, TOK:] = jnp.zeros((8, 128 - TOK), F32)
+        msg_ref[j] = message
 
 
 def step_kernel(scal_ref, coef_ref, msg_ref, lat_ref, clean_ref, prev_ref):
     first_len, base = scal_ref[0], scal_ref[4]
-    total = msg_ref[0]
-    for j in range(1, NHEAD):
-        total += msg_ref[j]
     pos = base + lax.broadcasted_iota(jnp.int32, (64, TOK), 1)
     first, live = pos < first_len, pos < LEN_ALL
-    mean = total[64:65, :TOK] * (1.0 / D)
-    var = total[65:66, :TOK] * (1.0 / D) - mean * mean
-    scale_w = jnp.where(first, total[:64, TOK : TOK + 1], total[:64, TOK + 1 : TOK + 2])
-    shift_w = jnp.where(first, total[:64, TOK + 2 : TOK + 3], total[:64, TOK + 3 : TOK + 4])
-    velocity = lax.rsqrt(var + EPSILON) * (total[:64, :TOK] - mean * scale_w) + shift_w
+    parts = [msg_ref[j].astype(F32) for j in range(NHEAD)]
+    sums = [p[64:65, :TOK] + p[65:66, :TOK] + p[66:67, :TOK] for p in parts]
+    squares = [p[67:68, :TOK] + p[68:69, :TOK] + p[69:70, :TOK] for p in parts]
+    mean, square = sums[0], squares[0]
+    for j in range(1, NHEAD):
+        mean, square = mean + sums[j], square + squares[j]
+    mean, square = mean * (1.0 / D), square * (1.0 / D)
+    var = square - mean * mean
+    scaled, shifted = jnp.zeros((64, TOK), F32), jnp.zeros((64, 128), F32)
+    for p, own in zip(parts, sums):
+        scale_w = jnp.where(
+            first,
+            p[:64, TOK : TOK + 1] + p[:64, TOK + 4 : TOK + 5],
+            p[:64, TOK + 1 : TOK + 2] + p[:64, TOK + 5 : TOK + 6],
+        )
+        scaled += p[:64, :TOK] + (own * (1.0 / 384) - mean) * scale_w
+        shifted += p[:64]
+    shift_w = jnp.where(
+        first,
+        shifted[:, TOK + 2 : TOK + 3] + shifted[:, TOK + 6 : TOK + 7],
+        shifted[:, TOK + 3 : TOK + 4] + shifted[:, TOK + 7 : TOK + 8],
+    )
+    velocity = lax.rsqrt(var + EPSILON) * scaled + shift_w
     latent = lat_ref[...]
 
     def row_coef(i):
@@ -277,6 +328,7 @@
     scal = jnp.stack([first_len, column, size, part * size, seq * TOK]).astype(jnp.int32)
     in_smem = pl.BlockSpec(memory_space=SMEM)
     big = pltpu.CompilerParams(vmem_limit_bytes=48 * 1024 * 1024)
+    small = pltpu.CompilerParams(vmem_limit_bytes=8 * 1024 * 1024)
 
     any_vmem = pl.BlockSpec(memory_space=VMEM)
 
@@ -287,15 +339,15 @@
     keyvals = lax.all_gather(mine[:, HALF:].reshape(NG * HALF, 128), "a", axis=0, tiled=True)
     partial = pl.pallas_call(
         attend_kernel,
-        out_shape=jax.ShapeDtypeStruct((NG, HD + 8, 128), BF),
+        out_shape=jax.ShapeDtypeStruct((NG, KEPT + 8, 128), BF),
         in_specs=[in_smem, any_vmem, any_vmem],
         out_specs=any_vmem,
         scratch_shapes=[
-            VMEM((NY, KT, 256), BF),
-            VMEM((NY, ROWS, KT), BF),
-            VMEM((NY, 256, QT), BF),
-            VMEM((NY, 8, QT), F32),
-            VMEM((NY, ROWS, QT), F32),
+            VMEM((NY * KT // KC, KC, 256), BF),
+            VMEM((NY * KT // KC, ROWS, KC), BF),
+            VMEM((2, 256, QP), BF),
+            VMEM((2, 8, QP), F32),
+            VMEM((2, ROWS, QP), F32),
         ],
         compiler_params=big,
         name="attend",
@@ -315,9 +367,10 @@
         stream_kernel,
         out_shape=(
             jax.ShapeDtypeStruct((TOK, 384), BF),
-            jax.ShapeDtypeStruct((NHEAD, 72, 128), F32),
+            jax.ShapeDtypeStruct((NHEAD, 72, 128), BF),
         ),
         in_specs=[in_smem] + [any_vmem] * 6,
+        compiler_params=small,
         name="stream",
     )(scal, terms, hidden, gate_mod, shift_mod, scale_mod, proj_weight.T)
     message = lax.all_to_all(message, ("x", "core"), 0, 0, tiled=True)
@@ -336,6 +389,7 @@
         step_kernel,
         out_shape=(jax.ShapeDtypeStruct((64, TOK), F32),) * 2,
         in_specs=[in_smem, in_smem, any_vmem, any_vmem],
+        compiler_params=small,
         name="ddim",
     )(scal, coef, message, latent.T)
     pairs = []

time: 132 us -> 125 us (0.947)
  blocking collectives: 41.7 us -> 55.5 us
  waiting for transfers between devices: 35.1 us -> 25.6 us
  starting transfers between devices: 30.7 us -> 23.8 us
  Pallas kernels: 18.3 us -> 15.9 us
  local copies, waits for them, and re-layouts: 3.57 us -> 2.05 us
    all_to_all x0 -> x1, blocking collectives: none -> 14.2 us  [shards(): parts = lax.all_to_all(partial, ('y', 'c'), 0, 0, tiled=True)]
    all_to_all x1 -> x0, waiting for transfers between devices: 8.58 us -> none  [shards(): parts = lax.all_to_all(partial, ('y', 'c'), 0, 0, tiled=True)]
    all_to_all x1 -> x0, starting transfers between devices: 7.97 us -> none  [shards(): parts = lax.all_to_all(partial, ('y', 'c'), 0, 0, tiled=True)]
    pallas_call x1, Pallas kernels: 10.6 us -> 8.62 us  [shards(): pl.pallas_call(attend_kernel, out_shape=jax.ShapeDtypeStruct((NG, KEPT +...]
    unnamed x14 -> x20, local copies, waits for them, and re-layouts: 1.57 us -> 0.05 us
  transfers between devices with their start and end apart: 5 -> 4, of which waited for: 5 -> 4; matrix products, arithmetic and copies ran while one was open for 2% -> 2% of each run, Pallas kernels for 0% -> 0%
where the time goes in v4:
time: 125 us
  blocking collectives  55.5 us (44%)
  waiting for transfers between devices  25.6 us (20%)
  starting transfers between devices  23.8 us (19%)
  Pallas kernels  15.9 us (13%)
  local copies, waits for them, and re-layouts  2.05 us (2%)
    all_gather x1, blocking collectives, shards(): lax.all_gather(mine[:, HALF:].reshape(NG * HALF, 128), 'a', axis=0, tiled...  36.6 us
    all_to_all x1, blocking collectives, shards(): parts = lax.all_to_all(partial, ('y', 'c'), 0, 0, tiled=True)  14.2 us
    all_to_all x1, waiting for transfers between devices, shards(): mine = lax.all_to_all(packed, ('y', 'c'), 0, 0, tiled=True)  10.2 us
    all_to_all x1, waiting for transfers between devices, shards(): terms = lax.all_to_all(term, ('x', 'core'), 0, 0, tiled=True)  8.89 us
    pallas_call x1, Pallas kernels, shards(): pl.pallas_call(attend_kernel, out_shape=jax.ShapeDtypeStruct((NG, KEPT +...  8.62 us
    all_to_all x1, starting transfers between devices, shards(): mine = lax.all_to_all(packed, ('y', 'c'), 0, 0, tiled=True)  8.21 us
    all_to_all x1, starting transfers between devices, shards(): terms = lax.all_to_all(term, ('x', 'core'), 0, 0, tiled=True)  7.02 us
    all_to_all x1, waiting for transfers between devices, shards(): message = lax.all_to_all(message, ('x', 'core'), 0, 0, tiled=True)  5.26 us
  transfers between devices with their start and end apart: 4, of which 4 were waited for; matrix products, arithmetic and copies ran while one was open for 2% of the time, Pallas kernels for 0%

profile of v4, /device:TPU:25, one launch (start us, length us, event | category | flops | bytes accessed | tf_op | source)
XLA Modules:
  0.0 124.6 jit_solution(5314279964278303700)
XLA Ops:
  0.6 0.0 copy-start
  0.6 2.0 %pack.1 = bf16[16,96,128]{2,1,0:T(8,128)(2,1)} custom-call(bf16[96,384]{1,0:T(8,128)(2,1)} %q_ref.1, bf16[96,384]{1,0:T(8,128)(2,1)} %k_ref.1, bf16[96,384]{1,0:T(8,128)(2,1)} %v_ref.1), custom_call_target="tpu_custom_call" | custom-call | tf_op jit(solution)/shard_map/pack/pallas_call | solution.py:335
  2.6 8.2 %all-to-all-start = ((bf16[16,96,128]{2,1,0:T(8,128)(2,1)}), bf16[16,96,128]{2,1,0:T(8,128)(2,1)S(1)}, u32[]{:S(2)}, u32[]{:S(2)}) async-start(bf16[16,96,128]{2,1,0:T(8,128)(2,1)} %pack.1), calls=%async_computation | async-start | bytes 786432 | tf_op jit(solution)/shard_map/all_to_all | solution.py:338
  10.8 0.7 stack.19.scal_ref
  11.6 10.2 %all-to-all-done.q_ref = bf16[16,96,128]{2,1,0:T(8,128)(2,1)S(1)} async-done(((bf16[16,96,128]{2,1,0:T(8,128)(2,1)}), bf16[16,96,128]{2,1,0:T(8,128)(2,1)S(1)}, u32[]{:S(2)}, u32[]{:S(2)}) %all-to-all-start) | async-done | bytes 393248 | tf_op jit(solution)/shard_map/all_to_all | solution.py:338
  21.7 36.6 %all_gather.9.kv_ref = bf16[3072,128]{1,0:T(8,128)(2,1)S(1)} all-gather(bf16[768,128]{1,0:T(8,128)(2,1)S(1)} %bitcast.24), channel_id=1, replica_groups=mesh['y'=4,'a'=4,'c'=4,'x'=4,'core'=2] {'a'}, dimensions={0}, use_global_device_ids=true | all-gather | bytes 983040 | tf_op jit(solution)/shard_map/all_gather | solution.py:339
  58.3 8.6 %attend.1 = bf16[16,56,128]{2,1,0:T(8,128)(2,1)S(1)} custom-call(s32[5]{0:T(128)S(1)} %stack.19.scal_ref, bf16[16,96,128]{2,1,0:T(8,128)(2,1)S(1)} %all-to-all-done.q_ref, bf16[3072,128]{1,0:T(8,128)(2,1)S(1)} %all_gather.9.kv_ref), custom_call_target="tpu_custom_call" | custom-call | tf_op jit(solution)/shard_map/attend/pallas_call | solution.py:340
  66.9 0.0 copy-start.9
  66.9 0.0 copy-start.7
  67.0 14.2 %all_to_all.20.part_ref = bf16[16,56,128]{2,1,0:T(8,128)(2,1)S(1)} all-to-all(bf16[16,56,128]{2,1,0:T(8,128)(2,1)S(1)} %attend.1), channel_id=1, replica_groups=mesh['y'=4,'a'=4,'c'=4,'x'=4,'core'=2] {'y','c'}, dimensions={0} | all-to-all | bytes 458752 | tf_op jit(solution)/shard_map/all_to_all | solution.py:355
  81.1 0.0 copy-done
  81.1 0.0 copy-start.1
  81.1 0.0 copy-start.2
  81.1 0.0 copy-start.4
  81.2 0.0 copy-start.5
  81.2 0.0 copy-start.6
  81.2 1.8 %merge.1 = bf16[8,96,384]{2,1,0:T(8,128)(2,1)} custom-call(bf16[16,56,128]{2,1,0:T(8,128)(2,1)S(1)} %all_to_all.20.part_ref, bf16[384,3072]{1,0:T(8,128)(2,1)S(1)} %copy-done), custom_call_target="tpu_custom_call" | custom-call | tf_op jit(solution)/shard_map/merge/pallas_call | solution.py:356
  83.0 0.0 copy-start.8
  83.0 0.0 copy-start.3
  83.0 7.0 %all-to-all-start.2 = ((bf16[8,96,384]{2,1,0:T(8,128)(2,1)}), bf16[8,96,384]{2,1,0:T(8,128)(2,1)S(1)}, u32[]{:S(2)}, u32[]{:S(2)}) async-start(bf16[8,96,384]{2,1,0:T(8,128)(2,1)} %merge.1), calls=%async_computation.2 | async-start | bytes 1179648 | tf_op jit(solution)/shard_map/all_to_all | solution.py:365
  90.0 0.0 copy-done.9
  90.0 0.0 copy-done.7
  90.1 0.6 gather_fusion
  90.7 0.6 gather_fusion.1
  91.3 8.9 %all-to-all-done.2.term_ref = bf16[8,96,384]{2,1,0:T(8,128)(2,1)S(1)} async-done(((bf16[8,96,384]{2,1,0:T(8,128)(2,1)}), bf16[8,96,384]{2,1,0:T(8,128)(2,1)S(1)}, u32[]{:S(2)}, u32[]{:S(2)}) %all-to-all-start.2) | async-done | bytes 589856 | tf_op jit(solution)/shard_map/all_to_all | solution.py:365
  100.2 0.0 copy-done.1
  100.2 0.0 copy-done.2
  100.2 0.0 copy-done.4
  100.2 0.0 copy-done.5
  100.2 0.0 copy-done.6
  100.2 1.7 %stream.1 = (bf16[96,384]{1,0:T(8,128)(2,1)}, bf16[8,72,128]{2,1,0:T(8,128)(2,1)}) custom-call(s32[5]{0:T(128)S(1)} %stack.19.scal_ref, bf16[8,96,384]{2,1,0:T(8,128)(2,1)S(1)} %all-to-all-done.2.term_ref, bf16[96,384]{1,0:T(8,128)(2,1)S(1)} %copy-done.1, bf16[2,384]{1,0:T(2,128)(2,1)S(1)} %copy-done.4, bf16[2,384]{1,0:T(2,128)(2,1)S(1)} %copy-done.5, ...), custom_call_target="tpu_custom_call" | custom-call | tf_op jit(solution)/shard_map/stream/pallas_call | solution.py:366
  101.9 4.2 %all-to-all-start.3 = ((bf16[8,72,128]{2,1,0:T(8,128)(2,1)}), bf16[8,72,128]{2,1,0:T(8,128)(2,1)S(1)}, u32[]{:S(2)}, u32[]{:S(2)}) async-start(bf16[8,72,128]{2,1,0:T(8,128)(2,1)} %get-tuple-element.9), calls=%async_computation.3 | async-start | bytes 294912 | tf_op jit(solution)/shard_map/all_to_all | solution.py:376
  106.1 0.0 copy-done.8
  106.2 0.1 pad_maximum_fusion.coef_ref
  106.2 5.3 %all-to-all-done.3.msg_ref = bf16[8,72,128]{2,1,0:T(8,128)(2,1)S(1)} async-done(((bf16[8,72,128]{2,1,0:T(8,128)(2,1)}), bf16[8,72,128]{2,1,0:T(8,128)(2,1)S(1)}, u32[]{:S(2)}, u32[]{:S(2)}) %all-to-all-start.3) | async-done | bytes 147488 | tf_op jit(solution)/shard_map/all_to_all | solution.py:376
  111.5 0.0 copy-done.3
  111.5 1.9 %ddim.1 = (f32[64,96]{1,0:T(8,128)}, f32[64,96]{1,0:T(8,128)}) custom-call(s32[5]{0:T(128)S(1)} %stack.19.scal_ref, f32[8]{0:T(128)S(1)} %pad_maximum_fusion.coef_ref, bf16[8,72,128]{2,1,0:T(8,128)(2,1)S(1)} %all-to-all-done.3.msg_ref, f32[64,96]{1,0:T(8,128)S(1)} %bitcast.23), custom_call_target="tpu_custom_call" | custom-call | tf_op jit(solution)/shard_map/ddim/pallas_call | solution.py:388
  113.3 4.4 %collective-permute-start = (f32[64,96]{1,0:T(8,128)}, f32[64,96]{1,0:T(8,128)S(1)}, u32[]{:S(2)}, u32[]{:S(2)}) collective-permute-start(f32[64,96]{1,0:T(8,128)} %get-tuple-element.11), channel_id=1, source_target_pairs={{0,8},{2,10},{4,12},{6,14},{8,16},{9,1},{10,18},{11,3},{12,20},{13... | collective-permute-start | bytes 73736 | tf_op jit(solution)/shard_map/ppermute | solution.py:403
  117.8 1.3 %collective-permute-done = f32[64,96]{1,0:T(8,128)S(1)} collective-permute-done((f32[64,96]{1,0:T(8,128)}, f32[64,96]{1,0:T(8,128)S(1)}, u32[]{:S(2)}, u32[]{:S(2)}) %collective-permute-start) | collective-permute-done | bytes 24608 | tf_op jit(solution)/shard_map/ppermute | solution.py:403
  119.1 4.7 %all-gather = f32[128,96]{1,0:T(8,128)S(1)} all-gather(f32[64,96]{1,0:T(8,128)S(1)} %collective-permute-done), channel_id=2, replica_groups=mesh['y'=4,'a'=4,'c'=4,'x'=4,'core'=2] {'core'}, dimensions={0}, use_global_device_ids=true | all-gather | bytes 73728 | tf_op jit(solution)/shard_map/all_gather | solution.py:404
  123.8 0.1 fusion.1
  123.9 0.7 maximum_bitcast_fusion
  (6 shorter events, 0.1 us)
Async XLA Ops:
  0.6 80.5 %copy-start = (bf16[384,3072]{1,0:T(8,128)(2,1)S(1)}, bf16[384,3072]{1,0:T(8,128)(2,1)}, u32[]{:S(2)}) copy-start(bf16[384,3072]{1,0:T(8,128)(2,1)} %w_ref.1) | copy-start | bytes 7077892
  2.6 19.1 %all-to-all-start = ((bf16[16,96,128]{2,1,0:T(8,128)(2,1)}), bf16[16,96,128]{2,1,0:T(8,128)(2,1)S(1)}, u32[]{:S(2)}, u32[]{:S(2)}) async-start(bf16[16,96,128]{2,1,0:T(8,128)(2,1)} %pack.1), calls=%async_computation | async-start | bytes 786432 | tf_op jit(solution)/shard_map/all_to_all | solution.py:338
  66.9 23.1 %copy-start.9 = (s32[2]{0:T(128)S(1)}, s32[2]{0:T(128)}, u32[]{:S(2)}) copy-start(s32[2]{0:T(128)} %param.14) | copy-start | bytes 28
  66.9 23.1 %copy-start.7 = (f32[1000]{0:T(1024)S(1)}, f32[1000]{0:T(1024)}, u32[]{:S(2)}) copy-start(f32[1000]{0:T(1024)} %constant.73.clone) | copy-start | bytes 12004
  81.1 19.1 %copy-start.1 = (bf16[96,384]{1,0:T(8,128)(2,1)S(1)}, bf16[96,384]{1,0:T(8,128)(2,1)}, u32[]{:S(2)}) copy-start(bf16[96,384]{1,0:T(8,128)(2,1)} %hid_ref.1) | copy-start | bytes 221188
  81.1 19.1 %copy-start.2 = (bf16[384,64]{0,1:T(8,128)(2,1)S(1)}, bf16[384,64]{0,1:T(8,128)(2,1)}, u32[]{:S(2)}) copy-start(bf16[384,64]{0,1:T(8,128)(2,1)} %param.23) | copy-start | bytes 147460
  81.1 19.1 %copy-start.4 = (bf16[2,384]{1,0:T(2,128)(2,1)S(1)}, bf16[2,384]{1,0:T(2,128)(2,1)}, u32[]{:S(2)}) copy-start(bf16[2,384]{1,0:T(2,128)(2,1)} %gate_ref.1) | copy-start | bytes 4612
  81.2 19.1 %copy-start.5 = (bf16[2,384]{1,0:T(2,128)(2,1)S(1)}, bf16[2,384]{1,0:T(2,128)(2,1)}, u32[]{:S(2)}) copy-start(bf16[2,384]{1,0:T(2,128)(2,1)} %shift_ref.1) | copy-start | bytes 4612
  81.2 19.1 %copy-start.6 = (bf16[2,384]{1,0:T(2,128)(2,1)S(1)}, bf16[2,384]{1,0:T(2,128)(2,1)}, u32[]{:S(2)}) copy-start(bf16[2,384]{1,0:T(2,128)(2,1)} %scale_ref.1) | copy-start | bytes 4612
  83.0 23.1 %copy-start.8 = (s32[2]{0:T(128)S(1)}, s32[2]{0:T(128)}, u32[]{:S(2)}) copy-start(s32[2]{0:T(128)} %param.13) | copy-start | bytes 28
  83.0 28.5 %copy-start.3 = (f32[96,64]{0,1:T(8,128)S(1)}, f32[96,64]{0,1:T(8,128)}, u32[]{:S(2)}) copy-start(f32[96,64]{0,1:T(8,128)} %param.24) | copy-start | bytes 73732
  83.0 17.2 %all-to-all-start.2 = ((bf16[8,96,384]{2,1,0:T(8,128)(2,1)}), bf16[8,96,384]{2,1,0:T(8,128)(2,1)S(1)}, u32[]{:S(2)}, u32[]{:S(2)}) async-start(bf16[8,96,384]{2,1,0:T(8,128)(2,1)} %merge.1), calls=%async_computation.2 | async-start | bytes 1179648 | tf_op jit(solution)/shard_map/all_to_all | solution.py:365
  101.9 9.6 %all-to-all-start.3 = ((bf16[8,72,128]{2,1,0:T(8,128)(2,1)}), bf16[8,72,128]{2,1,0:T(8,128)(2,1)S(1)}, u32[]{:S(2)}, u32[]{:S(2)}) async-start(bf16[8,72,128]{2,1,0:T(8,128)(2,1)} %get-tuple-element.9), calls=%async_computation.3 | async-start | bytes 294912 | tf_op jit(solution)/shard_map/all_to_all | solution.py:376
  113.3 5.8 %collective-permute-start = (f32[64,96]{1,0:T(8,128)}, f32[64,96]{1,0:T(8,128)S(1)}, u32[]{:S(2)}, u32[]{:S(2)}) collective-permute-start(f32[64,96]{1,0:T(8,128)} %get-tuple-element.11), channel_id=1, source_target_pairs={{0,8},{2,10},{4,12},{6,14},{8,16},{9,1},{10,18},{11,3},{12,20},{13... | collective-permute-start | bytes 73736 | tf_op jit(solution)/shard_map/ppermute | solution.py:403

commit v5 on v4

--- a/solution.py
+++ b/solution.py
@@ -72,7 +72,7 @@
 QT = NB * TOK
 QP = 2 * QT
 KT = NA * NB * HALF
-KC = 384
+KC = 768
 ROWS = 80
 KEPT = 48
 
@@ -82,16 +82,16 @@
     row_tok = NA * NB * TOK
     lane3 = lax.broadcasted_iota(jnp.int32, (NA * NB, HALF, 128), 2)
     slot = lax.broadcasted_iota(jnp.int32, (NA * NB, HALF, 128), 1)
-    block = lax.broadcasted_iota(jnp.int32, (NA * NB, HALF, 128), 0) * TOK + slot
+    block = lax.broadcasted_iota(jnp.int32, (NA * NB, HALF, 128), 0) * TOK + slot + offset
+    block = jnp.where(slot < size, block, NY * row_tok)
     low = low_lanes(HALF)
     lane_q = lax.broadcasted_iota(jnp.int32, (16, QT), 1)
     row_q = lax.broadcasted_iota(jnp.int32, (16, QT), 0)
     part = NB * HALF
     ones = (lax.broadcasted_iota(jnp.int32, (ROWS - HD, KC), 0) == 0).astype(F32)
     for j in range(NY):
-        pos = jnp.where(slot < size, block + (j * row_tok + offset), LEN_ALL)
-        own = jnp.where(pos < first_len, 0, jnp.where(pos < LEN_ALL, 1, -1))
-        extra = jnp.where((lane3 < 3) & (lane3 != own), MASKED, 0.0)
+        own = jnp.where(block < first_len - j * row_tok, 0, jnp.where(block < LEN_ALL - j * row_tok, 1, 2))
+        extra = jnp.where(lane3 == own, 1.0, 0.0)
         extra = extra.reshape(KT, 128).astype(BF)
         keyvals = jnp.concatenate(
             [kv_ref[(i * NY + j) * part : (i * NY + j + 1) * part, :] for i in range(NA)], axis=0
@@ -113,7 +113,7 @@
         query_ref[pair, :128, lanes] = jnp.concatenate(stack, axis=0).T.astype(BF)
         pos = lane_q + (j * row_tok + column * QT)
         own = jnp.where(pos < first_len, 0, jnp.where(pos < LEN_ALL, 1, 2))
-        query_ref[pair, 128:144, lanes] = jnp.where(row_q == own, 1.0, 0.0).astype(BF)
+        query_ref[pair, 128:144, lanes] = jnp.where((row_q < 3) & ((row_q != own) | (own == 2)), MASKED, 0.0).astype(BF)
         query_ref[pair, 144:, lanes] = jnp.zeros((112, QT), BF)
     top_ref[...] = jnp.full_like(top_ref, FLOOR)
     acc_ref[...] = jnp.zeros_like(acc_ref)
@@ -327,7 +327,7 @@
     part = jnp.where(member < 12, member % 3, member % 2)
     scal = jnp.stack([first_len, column, size, part * size, seq * TOK]).astype(jnp.int32)
     in_smem = pl.BlockSpec(memory_space=SMEM)
-    big = pltpu.CompilerParams(vmem_limit_bytes=48 * 1024 * 1024)
+    big = pltpu.CompilerParams(vmem_limit_bytes=24 * 1024 * 1024)
     small = pltpu.CompilerParams(vmem_limit_bytes=8 * 1024 * 1024)
 
     any_vmem = pl.BlockSpec(memory_space=VMEM)

time: 125 us -> 124 us (level)
  no operation moved by 1% of the time
where the time goes in v5:
time: 124 us
  blocking collectives  56 us (45%)
  waiting for transfers between devices  25.6 us (21%)
  starting transfers between devices  23.2 us (19%)
  Pallas kernels  14.9 us (12%)
  local copies, waits for them, and re-layouts  2.05 us (2%)
    all_gather x1, blocking collectives, shards(): lax.all_gather(mine[:, HALF:].reshape(NG * HALF, 128), 'a', axis=0, tiled...  36.6 us
    all_to_all x1, blocking collectives, shards(): parts = lax.all_to_all(partial, ('y', 'c'), 0, 0, tiled=True)  14.2 us
    all_to_all x1, waiting for transfers between devices, shards(): mine = lax.all_to_all(packed, ('y', 'c'), 0, 0, tiled=True)  10.2 us
    all_to_all x1, waiting for transfers between devices, shards(): terms = lax.all_to_all(term, ('x', 'core'), 0, 0, tiled=True)  8.89 us
    all_to_all x1, starting transfers between devices, shards(): mine = lax.all_to_all(packed, ('y', 'c'), 0, 0, tiled=True)  8.21 us
    pallas_call x1, Pallas kernels, shards(): pl.pallas_call(attend_kernel, out_shape=jax.ShapeDtypeStruct((NG, KEPT +...  7.66 us
    all_to_all x1, starting transfers between devices, shards(): terms = lax.all_to_all(term, ('x', 'core'), 0, 0, tiled=True)  7 us
    all_gather x1, blocking collectives, shards(): both = lax.all_gather(got, 'core')  5.29 us
  transfers between devices with their start and end apart: 4, of which 4 were waited for; matrix products, arithmetic and copies ran while one was open for 2% of the time, Pallas kernels for 0%

profile of v5, /device:TPU:25, one launch (start us, length us, event | category | flops | bytes accessed | tf_op | source)
XLA Modules:
  0.0 123.6 jit_solution(629309729014076519)
XLA Ops:
  0.6 0.0 copy-start
  0.6 2.0 %pack.1 = bf16[16,96,128]{2,1,0:T(8,128)(2,1)} custom-call(bf16[96,384]{1,0:T(8,128)(2,1)} %q_ref.1, bf16[96,384]{1,0:T(8,128)(2,1)} %k_ref.1, bf16[96,384]{1,0:T(8,128)(2,1)} %v_ref.1), custom_call_target="tpu_custom_call" | custom-call | tf_op jit(solution)/shard_map/pack/pallas_call | solution.py:335
  2.6 8.2 %all-to-all-start = ((bf16[16,96,128]{2,1,0:T(8,128)(2,1)}), bf16[16,96,128]{2,1,0:T(8,128)(2,1)S(1)}, u32[]{:S(2)}, u32[]{:S(2)}) async-start(bf16[16,96,128]{2,1,0:T(8,128)(2,1)} %pack.1), calls=%async_computation | async-start | bytes 786432 | tf_op jit(solution)/shard_map/all_to_all | solution.py:338
  10.8 0.7 stack.19.scal_ref
  11.6 10.2 %all-to-all-done.q_ref = bf16[16,96,128]{2,1,0:T(8,128)(2,1)S(1)} async-done(((bf16[16,96,128]{2,1,0:T(8,128)(2,1)}), bf16[16,96,128]{2,1,0:T(8,128)(2,1)S(1)}, u32[]{:S(2)}, u32[]{:S(2)}) %all-to-all-start) | async-done | bytes 393248 | tf_op jit(solution)/shard_map/all_to_all | solution.py:338
  21.7 36.6 %all_gather.9.kv_ref = bf16[3072,128]{1,0:T(8,128)(2,1)S(1)} all-gather(bf16[768,128]{1,0:T(8,128)(2,1)S(1)} %bitcast.24), channel_id=1, replica_groups=mesh['y'=4,'a'=4,'c'=4,'x'=4,'core'=2] {'a'}, dimensions={0}, use_global_device_ids=true | all-gather | bytes 983040 | tf_op jit(solution)/shard_map/all_gather | solution.py:339
  58.3 7.7 %attend.1 = bf16[16,56,128]{2,1,0:T(8,128)(2,1)S(1)} custom-call(s32[5]{0:T(128)S(1)} %stack.19.scal_ref, bf16[16,96,128]{2,1,0:T(8,128)(2,1)S(1)} %all-to-all-done.q_ref, bf16[3072,128]{1,0:T(8,128)(2,1)S(1)} %all_gather.9.kv_ref), custom_call_target="tpu_custom_call" | custom-call | tf_op jit(solution)/shard_map/attend/pallas_call | solution.py:340
  66.0 0.0 copy-start.9
  66.0 0.0 copy-start.7
  66.0 14.2 %all_to_all.20.part_ref = bf16[16,56,128]{2,1,0:T(8,128)(2,1)S(1)} all-to-all(bf16[16,56,128]{2,1,0:T(8,128)(2,1)S(1)} %attend.1), channel_id=1, replica_groups=mesh['y'=4,'a'=4,'c'=4,'x'=4,'core'=2] {'y','c'}, dimensions={0} | all-to-all | bytes 458752 | tf_op jit(solution)/shard_map/all_to_all | solution.py:355
  80.2 0.0 copy-done
  80.2 0.0 copy-start.1
  80.2 0.0 copy-start.2
  80.2 0.0 copy-start.4
  80.2 0.0 copy-start.5
  80.2 0.0 copy-start.6
  80.2 1.8 %merge.1 = bf16[8,96,384]{2,1,0:T(8,128)(2,1)} custom-call(bf16[16,56,128]{2,1,0:T(8,128)(2,1)S(1)} %all_to_all.20.part_ref, bf16[384,3072]{1,0:T(8,128)(2,1)S(1)} %copy-done), custom_call_target="tpu_custom_call" | custom-call | tf_op jit(solution)/shard_map/merge/pallas_call | solution.py:356
  82.0 0.0 copy-start.8
  82.0 0.0 copy-start.3
  82.0 7.0 %all-to-all-start.2 = ((bf16[8,96,384]{2,1,0:T(8,128)(2,1)}), bf16[8,96,384]{2,1,0:T(8,128)(2,1)S(1)}, u32[]{:S(2)}, u32[]{:S(2)}) async-start(bf16[8,96,384]{2,1,0:T(8,128)(2,1)} %merge.1), calls=%async_computation.2 | async-start | bytes 1179648 | tf_op jit(solution)/shard_map/all_to_all | solution.py:365
  89.0 0.0 copy-done.9
  89.1 0.0 copy-done.7
  89.1 0.6 gather_fusion
  89.7 0.6 gather_fusion.1
  90.3 8.9 %all-to-all-done.2.term_ref = bf16[8,96,384]{2,1,0:T(8,128)(2,1)S(1)} async-done(((bf16[8,96,384]{2,1,0:T(8,128)(2,1)}), bf16[8,96,384]{2,1,0:T(8,128)(2,1)S(1)}, u32[]{:S(2)}, u32[]{:S(2)}) %all-to-all-start.2) | async-done | bytes 589856 | tf_op jit(solution)/shard_map/all_to_all | solution.py:365
  99.2 0.0 copy-done.1
  99.2 0.0 copy-done.2
  99.2 0.0 copy-done.4
  99.2 0.0 copy-done.5
  99.3 0.0 copy-done.6
  99.3 1.7 %stream.1 = (bf16[96,384]{1,0:T(8,128)(2,1)}, bf16[8,72,128]{2,1,0:T(8,128)(2,1)}) custom-call(s32[5]{0:T(128)S(1)} %stack.19.scal_ref, bf16[8,96,384]{2,1,0:T(8,128)(2,1)S(1)} %all-to-all-done.2.term_ref, bf16[96,384]{1,0:T(8,128)(2,1)S(1)} %copy-done.1, bf16[2,384]{1,0:T(2,128)(2,1)S(1)} %copy-done.4, bf16[2,384]{1,0:T(2,128)(2,1)S(1)} %copy-done.5, ...), custom_call_target="tpu_custom_call" | custom-call | tf_op jit(solution)/shard_map/stream/pallas_call | solution.py:366
  100.9 4.1 %all-to-all-start.3 = ((bf16[8,72,128]{2,1,0:T(8,128)(2,1)}), bf16[8,72,128]{2,1,0:T(8,128)(2,1)S(1)}, u32[]{:S(2)}, u32[]{:S(2)}) async-start(bf16[8,72,128]{2,1,0:T(8,128)(2,1)} %get-tuple-element.9), calls=%async_computation.3 | async-start | bytes 294912 | tf_op jit(solution)/shard_map/all_to_all | solution.py:376
  105.1 0.0 copy-done.8
  105.2 0.1 pad_maximum_fusion.coef_ref
  105.3 5.3 %all-to-all-done.3.msg_ref = bf16[8,72,128]{2,1,0:T(8,128)(2,1)S(1)} async-done(((bf16[8,72,128]{2,1,0:T(8,128)(2,1)}), bf16[8,72,128]{2,1,0:T(8,128)(2,1)S(1)}, u32[]{:S(2)}, u32[]{:S(2)}) %all-to-all-start.3) | async-done | bytes 147488 | tf_op jit(solution)/shard_map/all_to_all | solution.py:376
  110.5 0.0 copy-done.3
  110.5 1.9 %ddim.1 = (f32[64,96]{1,0:T(8,128)}, f32[64,96]{1,0:T(8,128)}) custom-call(s32[5]{0:T(128)S(1)} %stack.19.scal_ref, f32[8]{0:T(128)S(1)} %pad_maximum_fusion.coef_ref, bf16[8,72,128]{2,1,0:T(8,128)(2,1)S(1)} %all-to-all-done.3.msg_ref, f32[64,96]{1,0:T(8,128)S(1)} %bitcast.23), custom_call_target="tpu_custom_call" | custom-call | tf_op jit(solution)/shard_map/ddim/pallas_call | solution.py:388
  112.4 3.9 %collective-permute-start = (f32[64,96]{1,0:T(8,128)}, f32[64,96]{1,0:T(8,128)S(1)}, u32[]{:S(2)}, u32[]{:S(2)}) collective-permute-start(f32[64,96]{1,0:T(8,128)} %get-tuple-element.11), channel_id=1, source_target_pairs={{0,8},{2,10},{4,12},{6,14},{8,16},{9,1},{10,18},{11,3},{12,20},{13... | collective-permute-start | bytes 73736 | tf_op jit(solution)/shard_map/ppermute | solution.py:403
  116.3 1.3 %collective-permute-done = f32[64,96]{1,0:T(8,128)S(1)} collective-permute-done((f32[64,96]{1,0:T(8,128)}, f32[64,96]{1,0:T(8,128)S(1)}, u32[]{:S(2)}, u32[]{:S(2)}) %collective-permute-start) | collective-permute-done | bytes 24608 | tf_op jit(solution)/shard_map/ppermute | solution.py:403
  117.6 5.3 %all-gather = f32[128,96]{1,0:T(8,128)S(1)} all-gather(f32[64,96]{1,0:T(8,128)S(1)} %collective-permute-done), channel_id=2, replica_groups=mesh['y'=4,'a'=4,'c'=4,'x'=4,'core'=2] {'core'}, dimensions={0}, use_global_device_ids=true | all-gather | bytes 73728 | tf_op jit(solution)/shard_map/all_gather | solution.py:404
  122.9 0.1 fusion.1
  122.9 0.7 maximum_bitcast_fusion
  (6 shorter events, 0.1 us)
Async XLA Ops:
  0.6 79.6 %copy-start = (bf16[384,3072]{1,0:T(8,128)(2,1)S(1)}, bf16[384,3072]{1,0:T(8,128)(2,1)}, u32[]{:S(2)}) copy-start(bf16[384,3072]{1,0:T(8,128)(2,1)} %w_ref.1) | copy-start | bytes 7077892
  2.6 19.1 %all-to-all-start = ((bf16[16,96,128]{2,1,0:T(8,128)(2,1)}), bf16[16,96,128]{2,1,0:T(8,128)(2,1)S(1)}, u32[]{:S(2)}, u32[]{:S(2)}) async-start(bf16[16,96,128]{2,1,0:T(8,128)(2,1)} %pack.1), calls=%async_computation | async-start | bytes 786432 | tf_op jit(solution)/shard_map/all_to_all | solution.py:338
  66.0 23.1 %copy-start.9 = (s32[2]{0:T(128)S(1)}, s32[2]{0:T(128)}, u32[]{:S(2)}) copy-start(s32[2]{0:T(128)} %param.14) | copy-start | bytes 28
  66.0 23.1 %copy-start.7 = (f32[1000]{0:T(1024)S(1)}, f32[1000]{0:T(1024)}, u32[]{:S(2)}) copy-start(f32[1000]{0:T(1024)} %constant.73.clone) | copy-start | bytes 12004
  80.2 19.1 %copy-start.1 = (bf16[96,384]{1,0:T(8,128)(2,1)S(1)}, bf16[96,384]{1,0:T(8,128)(2,1)}, u32[]{:S(2)}) copy-start(bf16[96,384]{1,0:T(8,128)(2,1)} %hid_ref.1) | copy-start | bytes 221188
  80.2 19.1 %copy-start.2 = (bf16[384,64]{0,1:T(8,128)(2,1)S(1)}, bf16[384,64]{0,1:T(8,128)(2,1)}, u32[]{:S(2)}) copy-start(bf16[384,64]{0,1:T(8,128)(2,1)} %param.23) | copy-start | bytes 147460
  80.2 19.1 %copy-start.4 = (bf16[2,384]{1,0:T(2,128)(2,1)S(1)}, bf16[2,384]{1,0:T(2,128)(2,1)}, u32[]{:S(2)}) copy-start(bf16[2,384]{1,0:T(2,128)(2,1)} %gate_ref.1) | copy-start | bytes 4612
  80.2 19.1 %copy-start.5 = (bf16[2,384]{1,0:T(2,128)(2,1)S(1)}, bf16[2,384]{1,0:T(2,128)(2,1)}, u32[]{:S(2)}) copy-start(bf16[2,384]{1,0:T(2,128)(2,1)} %shift_ref.1) | copy-start | bytes 4612
  80.2 19.0 %copy-start.6 = (bf16[2,384]{1,0:T(2,128)(2,1)S(1)}, bf16[2,384]{1,0:T(2,128)(2,1)}, u32[]{:S(2)}) copy-start(bf16[2,384]{1,0:T(2,128)(2,1)} %scale_ref.1) | copy-start | bytes 4612
  82.0 23.1 %copy-start.8 = (s32[2]{0:T(128)S(1)}, s32[2]{0:T(128)}, u32[]{:S(2)}) copy-start(s32[2]{0:T(128)} %param.13) | copy-start | bytes 28
  82.0 28.5 %copy-start.3 = (f32[96,64]{0,1:T(8,128)S(1)}, f32[96,64]{0,1:T(8,128)}, u32[]{:S(2)}) copy-start(f32[96,64]{0,1:T(8,128)} %param.24) | copy-start | bytes 73732
  82.0 17.2 %all-to-all-start.2 = ((bf16[8,96,384]{2,1,0:T(8,128)(2,1)}), bf16[8,96,384]{2,1,0:T(8,128)(2,1)S(1)}, u32[]{:S(2)}, u32[]{:S(2)}) async-start(bf16[8,96,384]{2,1,0:T(8,128)(2,1)} %merge.1), calls=%async_computation.2 | async-start | bytes 1179648 | tf_op jit(solution)/shard_map/all_to_all | solution.py:365
  100.9 9.6 %all-to-all-start.3 = ((bf16[8,72,128]{2,1,0:T(8,128)(2,1)}), bf16[8,72,128]{2,1,0:T(8,128)(2,1)S(1)}, u32[]{:S(2)}, u32[]{:S(2)}) async-start(bf16[8,72,128]{2,1,0:T(8,128)(2,1)} %get-tuple-element.9), calls=%async_computation.3 | async-start | bytes 294912 | tf_op jit(solution)/shard_map/all_to_all | solution.py:376
  112.4 5.2 %collective-permute-start = (f32[64,96]{1,0:T(8,128)}, f32[64,96]{1,0:T(8,128)S(1)}, u32[]{:S(2)}, u32[]{:S(2)}) collective-permute-start(f32[64,96]{1,0:T(8,128)} %get-tuple-element.11), channel_id=1, source_target_pairs={{0,8},{2,10},{4,12},{6,14},{8,16},{9,1},{10,18},{11,3},{12,20},{13... | collective-permute-start | bytes 73736 | tf_op jit(solution)/shard_map/ppermute | solution.py:403

commit v6 on v5

--- a/solution.py
+++ b/solution.py
@@ -16,7 +16,7 @@
 TRAIN_STEPS = 1000
 STEP_GAP = 20
 NY, NA, NB, NX, NC = 4, 4, 4, 4, 2
-NG = NY * NB
+NG = NA * NB
 NHEAD = 8
 EPSILON = 1e-06
 MASKED = -1e30
@@ -72,13 +72,13 @@
 QT = NB * TOK
 QP = 2 * QT
 KT = NA * NB * HALF
-KC = 768
+KC = KT // 2
 ROWS = 80
 KEPT = 48
 
 
 def attend_kernel(scal_ref, q_ref, kv_ref, out_ref, key_ref, val_ref, query_ref, top_ref, acc_ref):
-    first_len, column, size, offset = scal_ref[0], scal_ref[1], scal_ref[2], scal_ref[3]
+    first_len, row, size, offset = scal_ref[0], scal_ref[1], scal_ref[2], scal_ref[3]
     row_tok = NA * NB * TOK
     lane3 = lax.broadcasted_iota(jnp.int32, (NA * NB, HALF, 128), 2)
     slot = lax.broadcasted_iota(jnp.int32, (NA * NB, HALF, 128), 1)
@@ -87,23 +87,16 @@
     low = low_lanes(HALF)
     lane_q = lax.broadcasted_iota(jnp.int32, (16, QT), 1)
     row_q = lax.broadcasted_iota(jnp.int32, (16, QT), 0)
-    part = NB * HALF
-    ones = (lax.broadcasted_iota(jnp.int32, (ROWS - HD, KC), 0) == 0).astype(F32)
+    ones = (lax.broadcasted_iota(jnp.int32, (ROWS - HD, KT), 0) == 0).astype(F32)
     for j in range(NY):
         own = jnp.where(block < first_len - j * row_tok, 0, jnp.where(block < LEN_ALL - j * row_tok, 1, 2))
         extra = jnp.where(lane3 == own, 1.0, 0.0)
         extra = extra.reshape(KT, 128).astype(BF)
-        keyvals = jnp.concatenate(
-            [kv_ref[(i * NY + j) * part : (i * NY + j + 1) * part, :] for i in range(NA)], axis=0
-        )
+        keyvals = kv_ref[j * KT : (j + 1) * KT, :]
         turned = keyvals.astype(F32).T
-        for i in range(KT // KC):
-            rows = slice(i * KC, (i + 1) * KC)
-            key_ref[j * (KT // KC) + i, :, :128] = keyvals[rows]
-            key_ref[j * (KT // KC) + i, :, 128:] = extra[rows]
-            val_ref[j * (KT // KC) + i] = jnp.concatenate(
-                [turned[HD:, i * KC : (i + 1) * KC], ones], axis=0
-            ).astype(BF)
+        key_ref[j * KT : (j + 1) * KT, :128] = keyvals
+        key_ref[j * KT : (j + 1) * KT, 128:] = extra
+        val_ref[j] = jnp.concatenate([turned[HD:], ones], axis=0).astype(BF)
 
         stack = []
         for c in range(NB):
@@ -111,7 +104,7 @@
             stack += [jnp.where(low, q, 0.0), jnp.where(low, swap(q), 0.0)]
         pair, lanes = j // 2, slice(j % 2 * QT, j % 2 * QT + QT)
         query_ref[pair, :128, lanes] = jnp.concatenate(stack, axis=0).T.astype(BF)
-        pos = lane_q + (j * row_tok + column * QT)
+        pos = lane_q + (row * row_tok + j * QT)
         own = jnp.where(pos < first_len, 0, jnp.where(pos < LEN_ALL, 1, 2))
         query_ref[pair, 128:144, lanes] = jnp.where((row_q < 3) & ((row_q != own) | (own == 2)), MASKED, 0.0).astype(BF)
         query_ref[pair, 144:, lanes] = jnp.zeros((112, QT), BF)
@@ -122,32 +115,51 @@
         stop = jnp.minimum(stop, LEN_ALL)
         return start < first_len, (stop > first_len) & (start < stop)
 
-    def absorb(j, t, lanes):
-        scores = jnp.dot(key_ref[j], query_ref[t, :, lanes], preferred_element_type=F32)
+    def absorb(keys, values, t, lanes):
+        scores = jnp.dot(keys, query_ref[t, :, lanes], preferred_element_type=F32)
         old = top_ref[t, :1, lanes]
         new = jnp.maximum(jnp.max(scores, axis=0, keepdims=True), old)
         weights = jnp.exp(scores - new).astype(BF)
         acc_ref[t, :, lanes] = acc_ref[t, :, lanes] * jnp.exp(old - new) + jnp.dot(
-            val_ref[j], weights, preferred_element_type=F32
+            values, weights, preferred_element_type=F32
         )
         top_ref[t, :, lanes] = jnp.broadcast_to(new, (8, new.shape[1]))
 
     def visit(number, carry):
         j, t = number // 2, number % 2
-        k_first, k_second = holds(j * (2 * KC), (j + 1) * (2 * KC))
-
-        def needed(row):
-            start = row * row_tok + column * QT
+
+        def needed(half, side):
+            start = row * row_tok + (2 * t + side) * QT
             q_first, q_second = holds(start, start + QT)
+            begin = j * row_tok + half * (row_tok // 2)
+            k_first, k_second = holds(begin, begin + row_tok // 2)
             return (q_first & k_first) | (q_second & k_second)
 
-        left, right = needed(2 * t), needed(2 * t + 1)
-        pl.when(left & right)(lambda: absorb(j, t, slice(0, QP)))
-        pl.when(left & jnp.logical_not(right))(lambda: absorb(j, t, slice(0, QT)))
-        pl.when(right & jnp.logical_not(left))(lambda: absorb(j, t, slice(QT, QP)))
+        need = [[needed(half, side) for side in range(2)] for half in range(2)]
+        every = need[0][0] & need[0][1] & need[1][0] & need[1][1]
+
+        @pl.when(every)
+        def _():
+            rows = pl.ds(pl.multiple_of(j * KT, KT), KT)
+            absorb(key_ref[rows, :], val_ref[j], t, slice(0, QP))
+
+        @pl.when(jnp.logical_not(every))
+        def _():
+            for half in range(2):
+                left, right = need[half]
+
+                def take(lanes):
+                    rows = pl.ds(pl.multiple_of(j * KT + half * KC, KC), KC)
+                    values = val_ref[j, :, half * KC : (half + 1) * KC]
+                    absorb(key_ref[rows, :], values, t, lanes)
+
+                pl.when(left & right)(lambda: take(slice(0, QP)))
+                pl.when(left & jnp.logical_not(right))(lambda: take(slice(0, QT)))
+                pl.when(right & jnp.logical_not(left))(lambda: take(slice(QT, QP)))
+
         return carry
 
-    lax.fori_loop(0, NY * KT // KC * 2, visit, 0)
+    lax.fori_loop(0, NY * 2, visit, 0)
 
     row8 = lax.broadcasted_iota(jnp.int32, (8, QT), 0)
     lane_m = lax.broadcasted_iota(jnp.int32, (KEPT, 128), 1)
@@ -319,13 +331,12 @@
     proj_weight,
     latent,
 ):
-    y, column, c = lax.axis_index("y"), lax.axis_index("a"), lax.axis_index("c")
-    seq = (y * NA + column) * NB + c
-    member = y * NB + c
+    row, member = lax.axis_index("y"), lax.axis_index(("a", "c"))
+    seq = row * (NA * NB) + member
     first_len = lengths[0]
     size = jnp.where(member < 12, 32, 48)
     part = jnp.where(member < 12, member % 3, member % 2)
-    scal = jnp.stack([first_len, column, size, part * size, seq * TOK]).astype(jnp.int32)
+    scal = jnp.stack([first_len, row, size, part * size, seq * TOK]).astype(jnp.int32)
     in_smem = pl.BlockSpec(memory_space=SMEM)
     big = pltpu.CompilerParams(vmem_limit_bytes=24 * 1024 * 1024)
     small = pltpu.CompilerParams(vmem_limit_bytes=8 * 1024 * 1024)
@@ -335,16 +346,16 @@
     packed = pl.pallas_call(
         pack_kernel, out_shape=jax.ShapeDtypeStruct((NG, TOK, 128), BF), name="pack"
     )(query_act, key_act, value_act)
-    mine = lax.all_to_all(packed, ("y", "c"), 0, 0, tiled=True)
-    keyvals = lax.all_gather(mine[:, HALF:].reshape(NG * HALF, 128), "a", axis=0, tiled=True)
+    mine = lax.all_to_all(packed, ("a", "c"), 0, 0, tiled=True)
+    keyvals = lax.all_gather(mine[:, HALF:].reshape(NG * HALF, 128), "y", axis=0, tiled=True)
     partial = pl.pallas_call(
         attend_kernel,
         out_shape=jax.ShapeDtypeStruct((NG, KEPT + 8, 128), BF),
         in_specs=[in_smem, any_vmem, any_vmem],
         out_specs=any_vmem,
         scratch_shapes=[
-            VMEM((NY * KT // KC, KC, 256), BF),
-            VMEM((NY * KT // KC, ROWS, KC), BF),
+            VMEM((NY * KT, 256), BF),
+            VMEM((NY, ROWS, KT), BF),
             VMEM((2, 256, QP), BF),
             VMEM((2, 8, QP), F32),
             VMEM((2, ROWS, QP), F32),
@@ -352,7 +363,7 @@
         compiler_params=big,
         name="attend",
     )(scal, mine, keyvals)
-    parts = lax.all_to_all(partial, ("y", "c"), 0, 0, tiled=True)
+    parts = lax.all_to_all(partial, ("a", "c"), 0, 0, tiled=True)
     term = pl.pallas_call(
         merge_kernel,
         out_shape=jax.ShapeDtypeStruct((NHEAD, TOK, 384), BF),

time: 124 us -> 127 us (1.024); the launches traced: 124 us -> 125 us
  blocking collectives: 56 us -> 38.8 us
  starting transfers between devices: 23.2 us -> 34.4 us
  waiting for transfers between devices: 25.6 us -> 32.6 us
    all_gather x1, blocking collectives: 36.6 us -> 10.7 us  [shards(): lax.all_gather(mine[:, HALF:].reshape(NG * HALF, 128), 'y', axis=0, tiled...]
    all_to_all x1, blocking collectives: 14.2 us -> 23.6 us  [shards(): parts = lax.all_to_all(partial, ('a', 'c'), 0, 0, tiled=True)]
    all_to_all x1, waiting for transfers between devices: 10.2 us -> 17.2 us  [shards(): mine = lax.all_to_all(packed, ('a', 'c'), 0, 0, tiled=True)]
    all_to_all x1, starting transfers between devices: 8.21 us -> 14.9 us  [shards(): mine = lax.all_to_all(packed, ('a', 'c'), 0, 0, tiled=True)]
    all_to_all x1, starting transfers between devices: 7 us -> 10.7 us  [shards(): terms = lax.all_to_all(term, ('x', 'core'), 0, 0, tiled=True)]
where the time goes in v6:
time: 127 us; the launch traced here: 125 us
  blocking collectives  38.8 us (31%)
  starting transfers between devices  34.4 us (27%)
  waiting for transfers between devices  32.6 us (26%)
  Pallas kernels  15.3 us (12%)
  local copies, waits for them, and re-layouts  2.05 us (2%)
    all_to_all x1, blocking collectives, shards(): parts = lax.all_to_all(partial, ('a', 'c'), 0, 0, tiled=True)  23.6 us
    all_to_all x1, waiting for transfers between devices, shards(): mine = lax.all_to_all(packed, ('a', 'c'), 0, 0, tiled=True)  17.2 us
    all_to_all x1, starting transfers between devices, shards(): mine = lax.all_to_all(packed, ('a', 'c'), 0, 0, tiled=True)  14.9 us
    all_gather x1, blocking collectives, shards(): lax.all_gather(mine[:, HALF:].reshape(NG * HALF, 128), 'y', axis=0, tiled...  10.7 us
    all_to_all x1, starting transfers between devices, shards(): terms = lax.all_to_all(term, ('x', 'core'), 0, 0, tiled=True)  10.7 us
    all_to_all x1, waiting for transfers between devices, shards(): terms = lax.all_to_all(term, ('x', 'core'), 0, 0, tiled=True)  8.89 us
    pallas_call x1, Pallas kernels, shards(): pl.pallas_call(attend_kernel, out_shape=jax.ShapeDtypeStruct((NG, KEPT +...  8.05 us
    all_to_all x1, waiting for transfers between devices, shards(): message = lax.all_to_all(message, ('x', 'core'), 0, 0, tiled=True)  5.26 us
  transfers between devices with their start and end apart: 4, of which 4 were waited for; matrix products, arithmetic and copies ran while one was open for 2% of the time, Pallas kernels for 0%

profile of v6, /device:TPU:25, one launch (start us, length us, event | category | flops | bytes accessed | tf_op | source)
XLA Modules:
  0.0 125.1 jit_solution(802526461589473207)
XLA Ops:
  0.6 0.0 copy-start
  0.6 2.0 %pack.1 = bf16[16,96,128]{2,1,0:T(8,128)(2,1)} custom-call(bf16[96,384]{1,0:T(8,128)(2,1)} %q_ref.1, bf16[96,384]{1,0:T(8,128)(2,1)} %k_ref.1, bf16[96,384]{1,0:T(8,128)(2,1)} %v_ref.1), custom_call_target="tpu_custom_call" | custom-call | tf_op jit(solution)/shard_map/pack/pallas_call | solution.py:346
  2.6 14.9 %all-to-all-start = ((bf16[16,96,128]{2,1,0:T(8,128)(2,1)}), bf16[16,96,128]{2,1,0:T(8,128)(2,1)S(1)}, u32[]{:S(2)}, u32[]{:S(2)}) async-start(bf16[16,96,128]{2,1,0:T(8,128)(2,1)} %pack.1), calls=%async_computation | async-start | bytes 786432 | tf_op jit(solution)/shard_map/all_to_all | solution.py:349
  17.6 0.7 stack.19.scal_ref
  18.3 17.2 %all-to-all-done.q_ref = bf16[16,96,128]{2,1,0:T(8,128)(2,1)S(1)} async-done(((bf16[16,96,128]{2,1,0:T(8,128)(2,1)}), bf16[16,96,128]{2,1,0:T(8,128)(2,1)S(1)}, u32[]{:S(2)}, u32[]{:S(2)}) %all-to-all-start) | async-done | bytes 393248 | tf_op jit(solution)/shard_map/all_to_all | solution.py:349
  35.6 10.7 %all_gather.9.kv_ref = bf16[3072,128]{1,0:T(8,128)(2,1)S(1)} all-gather(bf16[768,128]{1,0:T(8,128)(2,1)S(1)} %bitcast.24), channel_id=1, replica_groups=mesh['y'=4,'a'=4,'c'=4,'x'=4,'core'=2] {'y'}, dimensions={0}, use_global_device_ids=true | all-gather | bytes 983040 | tf_op jit(solution)/shard_map/all_gather | solution.py:350
  46.3 8.1 %attend.1 = bf16[16,56,128]{2,1,0:T(8,128)(2,1)S(1)} custom-call(s32[5]{0:T(128)S(1)} %stack.19.scal_ref, bf16[16,96,128]{2,1,0:T(8,128)(2,1)S(1)} %all-to-all-done.q_ref, bf16[3072,128]{1,0:T(8,128)(2,1)S(1)} %all_gather.9.kv_ref), custom_call_target="tpu_custom_call" | custom-call | tf_op jit(solution)/shard_map/attend/pallas_call | solution.py:351
  54.3 0.0 copy-start.9
  54.4 0.0 copy-start.7
  54.4 23.6 %all_to_all.20.part_ref = bf16[16,56,128]{2,1,0:T(8,128)(2,1)S(1)} all-to-all(bf16[16,56,128]{2,1,0:T(8,128)(2,1)S(1)} %attend.1), channel_id=1, replica_groups=mesh['y'=4,'a'=4,'c'=4,'x'=4,'core'=2] {'a','c'}, dimensions={0} | all-to-all | bytes 458752 | tf_op jit(solution)/shard_map/all_to_all | solution.py:366
  78.0 0.0 copy-done
  78.0 0.0 copy-start.1
  78.0 0.0 copy-start.2
  78.0 0.0 copy-start.4
  78.0 0.0 copy-start.5
  78.0 0.0 copy-start.6
  78.0 1.8 %merge.1 = bf16[8,96,384]{2,1,0:T(8,128)(2,1)} custom-call(bf16[16,56,128]{2,1,0:T(8,128)(2,1)S(1)} %all_to_all.20.part_ref, bf16[384,3072]{1,0:T(8,128)(2,1)S(1)} %copy-done), custom_call_target="tpu_custom_call" | custom-call | tf_op jit(solution)/shard_map/merge/pallas_call | solution.py:367
  79.8 0.0 copy-start.8
  79.9 0.0 copy-start.3
  79.9 10.7 %all-to-all-start.2 = ((bf16[8,96,384]{2,1,0:T(8,128)(2,1)}), bf16[8,96,384]{2,1,0:T(8,128)(2,1)S(1)}, u32[]{:S(2)}, u32[]{:S(2)}) async-start(bf16[8,96,384]{2,1,0:T(8,128)(2,1)} %merge.1), calls=%async_computation.2 | async-start | bytes 1179648 | tf_op jit(solution)/shard_map/all_to_all | solution.py:376
  90.5 0.0 copy-done.9
  90.6 0.0 copy-done.7
  90.6 0.6 gather_fusion
  91.2 0.6 gather_fusion.1
  91.8 8.9 %all-to-all-done.2.term_ref = bf16[8,96,384]{2,1,0:T(8,128)(2,1)S(1)} async-done(((bf16[8,96,384]{2,1,0:T(8,128)(2,1)}), bf16[8,96,384]{2,1,0:T(8,128)(2,1)S(1)}, u32[]{:S(2)}, u32[]{:S(2)}) %all-to-all-start.2) | async-done | bytes 589856 | tf_op jit(solution)/shard_map/all_to_all | solution.py:376
  100.7 0.0 copy-done.1
  100.7 0.0 copy-done.2
  100.7 0.0 copy-done.4
  100.7 0.0 copy-done.5
  100.7 0.0 copy-done.6
  100.8 1.7 %stream.1 = (bf16[96,384]{1,0:T(8,128)(2,1)}, bf16[8,72,128]{2,1,0:T(8,128)(2,1)}) custom-call(s32[5]{0:T(128)S(1)} %stack.19.scal_ref, bf16[8,96,384]{2,1,0:T(8,128)(2,1)S(1)} %all-to-all-done.2.term_ref, bf16[96,384]{1,0:T(8,128)(2,1)S(1)} %copy-done.1, bf16[2,384]{1,0:T(2,128)(2,1)S(1)} %copy-done.4, bf16[2,384]{1,0:T(2,128)(2,1)S(1)} %copy-done.5, ...), custom_call_target="tpu_custom_call" | custom-call | tf_op jit(solution)/shard_map/stream/pallas_call | solution.py:377
  102.4 4.1 %all-to-all-start.3 = ((bf16[8,72,128]{2,1,0:T(8,128)(2,1)}), bf16[8,72,128]{2,1,0:T(8,128)(2,1)S(1)}, u32[]{:S(2)}, u32[]{:S(2)}) async-start(bf16[8,72,128]{2,1,0:T(8,128)(2,1)} %get-tuple-element.9), calls=%async_computation.3 | async-start | bytes 294912 | tf_op jit(solution)/shard_map/all_to_all | solution.py:387
  106.6 0.0 copy-done.8
  106.7 0.1 pad_maximum_fusion.coef_ref
  106.8 5.3 %all-to-all-done.3.msg_ref = bf16[8,72,128]{2,1,0:T(8,128)(2,1)S(1)} async-done(((bf16[8,72,128]{2,1,0:T(8,128)(2,1)}), bf16[8,72,128]{2,1,0:T(8,128)(2,1)S(1)}, u32[]{:S(2)}, u32[]{:S(2)}) %all-to-all-start.3) | async-done | bytes 147488 | tf_op jit(solution)/shard_map/all_to_all | solution.py:387
  112.0 0.0 copy-done.3
  112.0 1.9 %ddim.1 = (f32[64,96]{1,0:T(8,128)}, f32[64,96]{1,0:T(8,128)}) custom-call(s32[5]{0:T(128)S(1)} %stack.19.scal_ref, f32[8]{0:T(128)S(1)} %pad_maximum_fusion.coef_ref, bf16[8,72,128]{2,1,0:T(8,128)(2,1)S(1)} %all-to-all-done.3.msg_ref, f32[64,96]{1,0:T(8,128)S(1)} %bitcast.23), custom_call_target="tpu_custom_call" | custom-call | tf_op jit(solution)/shard_map/ddim/pallas_call | solution.py:399
  113.9 4.7 %collective-permute-start = (f32[64,96]{1,0:T(8,128)}, f32[64,96]{1,0:T(8,128)S(1)}, u32[]{:S(2)}, u32[]{:S(2)}) collective-permute-start(f32[64,96]{1,0:T(8,128)} %get-tuple-element.11), channel_id=1, source_target_pairs={{0,8},{2,10},{4,12},{6,14},{8,16},{9,1},{10,18},{11,3},{12,20},{13... | collective-permute-start | bytes 73736 | tf_op jit(solution)/shard_map/ppermute | solution.py:414
  118.6 1.3 %collective-permute-done = f32[64,96]{1,0:T(8,128)S(1)} collective-permute-done((f32[64,96]{1,0:T(8,128)}, f32[64,96]{1,0:T(8,128)S(1)}, u32[]{:S(2)}, u32[]{:S(2)}) %collective-permute-start) | collective-permute-done | bytes 24608 | tf_op jit(solution)/shard_map/ppermute | solution.py:414
  119.9 4.5 %all-gather = f32[128,96]{1,0:T(8,128)S(1)} all-gather(f32[64,96]{1,0:T(8,128)S(1)} %collective-permute-done), channel_id=2, replica_groups=mesh['y'=4,'a'=4,'c'=4,'x'=4,'core'=2] {'core'}, dimensions={0}, use_global_device_ids=true | all-gather | bytes 73728 | tf_op jit(solution)/shard_map/all_gather | solution.py:415
  124.4 0.1 fusion.1
  124.4 0.7 maximum_bitcast_fusion
  (6 shorter events, 0.1 us)
Async XLA Ops:
  0.6 77.4 %copy-start = (bf16[384,3072]{1,0:T(8,128)(2,1)S(1)}, bf16[384,3072]{1,0:T(8,128)(2,1)}, u32[]{:S(2)}) copy-start(bf16[384,3072]{1,0:T(8,128)(2,1)} %w_ref.1) | copy-start | bytes 7077892
  2.6 32.9 %all-to-all-start = ((bf16[16,96,128]{2,1,0:T(8,128)(2,1)}), bf16[16,96,128]{2,1,0:T(8,128)(2,1)S(1)}, u32[]{:S(2)}, u32[]{:S(2)}) async-start(bf16[16,96,128]{2,1,0:T(8,128)(2,1)} %pack.1), calls=%async_computation | async-start | bytes 786432 | tf_op jit(solution)/shard_map/all_to_all | solution.py:349
  54.3 36.2 %copy-start.9 = (s32[2]{0:T(128)S(1)}, s32[2]{0:T(128)}, u32[]{:S(2)}) copy-start(s32[2]{0:T(128)} %param.14) | copy-start | bytes 28
  54.4 36.2 %copy-start.7 = (f32[1000]{0:T(1024)S(1)}, f32[1000]{0:T(1024)}, u32[]{:S(2)}) copy-start(f32[1000]{0:T(1024)} %constant.75.clone) | copy-start | bytes 12004
  78.0 22.7 %copy-start.1 = (bf16[96,384]{1,0:T(8,128)(2,1)S(1)}, bf16[96,384]{1,0:T(8,128)(2,1)}, u32[]{:S(2)}) copy-start(bf16[96,384]{1,0:T(8,128)(2,1)} %hid_ref.1) | copy-start | bytes 221188
  78.0 22.7 %copy-start.2 = (bf16[384,64]{0,1:T(8,128)(2,1)S(1)}, bf16[384,64]{0,1:T(8,128)(2,1)}, u32[]{:S(2)}) copy-start(bf16[384,64]{0,1:T(8,128)(2,1)} %param.23) | copy-start | bytes 147460
  78.0 22.7 %copy-start.4 = (bf16[2,384]{1,0:T(2,128)(2,1)S(1)}, bf16[2,384]{1,0:T(2,128)(2,1)}, u32[]{:S(2)}) copy-start(bf16[2,384]{1,0:T(2,128)(2,1)} %gate_ref.1) | copy-start | bytes 4612
  78.0 22.7 %copy-start.5 = (bf16[2,384]{1,0:T(2,128)(2,1)S(1)}, bf16[2,384]{1,0:T(2,128)(2,1)}, u32[]{:S(2)}) copy-start(bf16[2,384]{1,0:T(2,128)(2,1)} %shift_ref.1) | copy-start | bytes 4612
  78.0 22.7 %copy-start.6 = (bf16[2,384]{1,0:T(2,128)(2,1)S(1)}, bf16[2,384]{1,0:T(2,128)(2,1)}, u32[]{:S(2)}) copy-start(bf16[2,384]{1,0:T(2,128)(2,1)} %scale_ref.1) | copy-start | bytes 4612
  79.8 26.7 %copy-start.8 = (s32[2]{0:T(128)S(1)}, s32[2]{0:T(128)}, u32[]{:S(2)}) copy-start(s32[2]{0:T(128)} %param.13) | copy-start | bytes 28
  79.9 32.2 %copy-start.3 = (f32[96,64]{0,1:T(8,128)S(1)}, f32[96,64]{0,1:T(8,128)}, u32[]{:S(2)}) copy-start(f32[96,64]{0,1:T(8,128)} %param.24) | copy-start | bytes 73732
  79.9 20.9 %all-to-all-start.2 = ((bf16[8,96,384]{2,1,0:T(8,128)(2,1)}), bf16[8,96,384]{2,1,0:T(8,128)(2,1)S(1)}, u32[]{:S(2)}, u32[]{:S(2)}) async-start(bf16[8,96,384]{2,1,0:T(8,128)(2,1)} %merge.1), calls=%async_computation.2 | async-start | bytes 1179648 | tf_op jit(solution)/shard_map/all_to_all | solution.py:376
  102.4 9.6 %all-to-all-start.3 = ((bf16[8,72,128]{2,1,0:T(8,128)(2,1)}), bf16[8,72,128]{2,1,0:T(8,128)(2,1)S(1)}, u32[]{:S(2)}, u32[]{:S(2)}) async-start(bf16[8,72,128]{2,1,0:T(8,128)(2,1)} %get-tuple-element.9), calls=%async_computation.3 | async-start | bytes 294912 | tf_op jit(solution)/shard_map/all_to_all | solution.py:387
  113.9 6.0 %collective-permute-start = (f32[64,96]{1,0:T(8,128)}, f32[64,96]{1,0:T(8,128)S(1)}, u32[]{:S(2)}, u32[]{:S(2)}) collective-permute-start(f32[64,96]{1,0:T(8,128)} %get-tuple-element.11), channel_id=1, source_target_pairs={{0,8},{2,10},{4,12},{6,14},{8,16},{9,1},{10,18},{11,3},{12,20},{13... | collective-permute-start | bytes 73736 | tf_op jit(solution)/shard_map/ppermute | solution.py:414

commit v7 on v6

--- a/solution.py
+++ b/solution.py
@@ -74,11 +74,13 @@
 KT = NA * NB * HALF
 KC = KT // 2
 ROWS = 80
+PART = KT // NA
 KEPT = 48
 
 
 def attend_kernel(scal_ref, q_ref, kv_ref, out_ref, key_ref, val_ref, query_ref, top_ref, acc_ref):
-    first_len, row, size, offset = scal_ref[0], scal_ref[1], scal_ref[2], scal_ref[3]
+    first_len, size, offset = scal_ref[0], scal_ref[1], scal_ref[2]
+    base, stride, by_row, by_part = scal_ref[4], scal_ref[5], scal_ref[6], scal_ref[7]
     row_tok = NA * NB * TOK
     lane3 = lax.broadcasted_iota(jnp.int32, (NA * NB, HALF, 128), 2)
     slot = lax.broadcasted_iota(jnp.int32, (NA * NB, HALF, 128), 1)
@@ -92,7 +94,13 @@
         own = jnp.where(block < first_len - j * row_tok, 0, jnp.where(block < LEN_ALL - j * row_tok, 1, 2))
         extra = jnp.where(lane3 == own, 1.0, 0.0)
         extra = extra.reshape(KT, 128).astype(BF)
-        keyvals = kv_ref[j * KT : (j + 1) * KT, :]
+        keyvals = jnp.concatenate(
+            [
+                kv_ref[pl.ds(pl.multiple_of((j * by_row + i * by_part) * PART, PART), PART), :]
+                for i in range(NA)
+            ],
+            axis=0,
+        )
         turned = keyvals.astype(F32).T
         key_ref[j * KT : (j + 1) * KT, :128] = keyvals
         key_ref[j * KT : (j + 1) * KT, 128:] = extra
@@ -104,7 +112,7 @@
             stack += [jnp.where(low, q, 0.0), jnp.where(low, swap(q), 0.0)]
         pair, lanes = j // 2, slice(j % 2 * QT, j % 2 * QT + QT)
         query_ref[pair, :128, lanes] = jnp.concatenate(stack, axis=0).T.astype(BF)
-        pos = lane_q + (row * row_tok + j * QT)
+        pos = lane_q + (base + j * stride)
         own = jnp.where(pos < first_len, 0, jnp.where(pos < LEN_ALL, 1, 2))
         query_ref[pair, 128:144, lanes] = jnp.where((row_q < 3) & ((row_q != own) | (own == 2)), MASKED, 0.0).astype(BF)
         query_ref[pair, 144:, lanes] = jnp.zeros((112, QT), BF)
@@ -129,7 +137,7 @@
         j, t = number // 2, number % 2
 
         def needed(half, side):
-            start = row * row_tok + (2 * t + side) * QT
+            start = base + (2 * t + side) * stride
             q_first, q_second = holds(start, start + QT)
             begin = j * row_tok + half * (row_tok // 2)
             k_first, k_second = holds(begin, begin + row_tok // 2)
@@ -223,7 +231,7 @@
 def stream_kernel(
     scal_ref, term_ref, hid_ref, gate_ref, shift_ref, scale_ref, w_ref, hid_out, msg_ref
 ):
-    first_len, base = scal_ref[0], scal_ref[4]
+    first_len, base = scal_ref[0], scal_ref[3]
     projected = term_ref[0].astype(F32)
     for j in range(1, NHEAD):
         projected += term_ref[j].astype(F32)
@@ -267,7 +275,7 @@
 
 
 def step_kernel(scal_ref, coef_ref, msg_ref, lat_ref, clean_ref, prev_ref):
-    first_len, base = scal_ref[0], scal_ref[4]
+    first_len, base = scal_ref[0], scal_ref[3]
     pos = base + lax.broadcasted_iota(jnp.int32, (64, TOK), 1)
     first, live = pos < first_len, pos < LEN_ALL
     parts = [msg_ref[j].astype(F32) for j in range(NHEAD)]
@@ -311,6 +319,25 @@
     return np.cumprod(1.0 - betas).astype(np.float32)
 
 
+TOKEN_AXES = ("y", "a", "c", "core")
+NEAR_Z = 1
+
+
+def core_groups():
+    def index(y, a, c, core):
+        return ((y * NA + a) * NB + c) * NC + core
+
+    near, far = [], []
+    for core in range(NC):
+        if core == NEAR_Z:
+            near += [[index(y, a, c, core) for a in range(NA) for c in range(NB)] for y in range(NY)]
+            far += [[index(y, a, c, core) for y in range(NY)] for a in range(NA) for c in range(NB)]
+        else:
+            near += [[index(y, a, c, core) for y in range(NY) for c in range(NB)] for a in range(NA)]
+            far += [[index(y, a, c, core) for a in range(NA)] for y in range(NY) for c in range(NB)]
+    return near, far
+
+
 def request_of(position, first_len):
     return jnp.where(
         position < 0, -1, jnp.where(position < first_len, 0, jnp.where(position < LEN_ALL, 1, 2))
@@ -331,12 +358,27 @@
     proj_weight,
     latent,
 ):
-    row, member = lax.axis_index("y"), lax.axis_index(("a", "c"))
-    seq = row * (NA * NB) + member
+    y, a, c = lax.axis_index("y"), lax.axis_index("a"), lax.axis_index("c")
+    near_z = lax.axis_index("core") == NEAR_Z
+    seq = (y * NA + a) * NB + c
+    member = jnp.where(near_z, a, y) * NB + c
     first_len = lengths[0]
     size = jnp.where(member < 12, 32, 48)
     part = jnp.where(member < 12, member % 3, member % 2)
-    scal = jnp.stack([first_len, row, size, part * size, seq * TOK]).astype(jnp.int32)
+    row_tok, tile_tok = NA * NB * TOK, NB * TOK
+    scal = jnp.stack(
+        [
+            first_len,
+            size,
+            part * size,
+            seq * TOK,
+            jnp.where(near_z, y * row_tok, a * tile_tok),
+            jnp.where(near_z, tile_tok, row_tok),
+            jnp.where(near_z, NA, 1),
+            jnp.where(near_z, 1, NA),
+        ]
+    ).astype(jnp.int32)
+    near, far = core_groups()
     in_smem = pl.BlockSpec(memory_space=SMEM)
     big = pltpu.CompilerParams(vmem_limit_bytes=24 * 1024 * 1024)
     small = pltpu.CompilerParams(vmem_limit_bytes=8 * 1024 * 1024)
@@ -346,8 +388,14 @@
     packed = pl.pallas_call(
         pack_kernel, out_shape=jax.ShapeDtypeStruct((NG, TOK, 128), BF), name="pack"
     )(query_act, key_act, value_act)
-    mine = lax.all_to_all(packed, ("a", "c"), 0, 0, tiled=True)
-    keyvals = lax.all_gather(mine[:, HALF:].reshape(NG * HALF, 128), "y", axis=0, tiled=True)
+    mine = lax.all_to_all(packed, TOKEN_AXES, 0, 0, tiled=True, axis_index_groups=near)
+    keyvals = lax.all_gather(
+        mine[:, HALF:].reshape(NG * HALF, 128),
+        TOKEN_AXES,
+        axis=0,
+        tiled=True,
+        axis_index_groups=far,
+    )
     partial = pl.pallas_call(
         attend_kernel,
         out_shape=jax.ShapeDtypeStruct((NG, KEPT + 8, 128), BF),
@@ -363,7 +411,7 @@
         compiler_params=big,
         name="attend",
     )(scal, mine, keyvals)
-    parts = lax.all_to_all(partial, ("a", "c"), 0, 0, tiled=True)
+    parts = lax.all_to_all(partial, TOKEN_AXES, 0, 0, tiled=True, axis_index_groups=near)
     term = pl.pallas_call(
         merge_kernel,
         out_shape=jax.ShapeDtypeStruct((NHEAD, TOK, 384), BF),

time: 127 us -> 119 us (0.937)
  blocking collectives: 38.8 us -> 33.3 us
    all_to_all x1, blocking collectives: 23.6 us -> 18.6 us  [shards(): lax.all_to_all(partial, TOKEN_AXES, 0, 0, tiled=True, axis_index_groups=n...]
    all_to_all x1, starting transfers between devices: 10.7 us -> 9 us  [shards(): terms = lax.all_to_all(term, ('x', 'core'), 0, 0, tiled=True)]
where the time goes in v7:
time: 119 us; the launch traced here: 118 us
  starting transfers between devices  33.5 us (28%)
  blocking collectives  33.3 us (28%)
  waiting for transfers between devices  31.7 us (27%)
  Pallas kernels  15.3 us (13%)
  local copies, waits for them, and re-layouts  2.05 us (2%)
    all_to_all x1, blocking collectives, shards(): lax.all_to_all(partial, TOKEN_AXES, 0, 0, tiled=True, axis_index_groups=n...  18.6 us
    all_to_all x1, waiting for transfers between devices, shards(): lax.all_to_all(packed, TOKEN_AXES, 0, 0, tiled=True, axis_index_groups=near)  16.3 us
    all_to_all x1, starting transfers between devices, shards(): lax.all_to_all(packed, TOKEN_AXES, 0, 0, tiled=True, axis_index_groups=near)  14.9 us
    all_gather x1, blocking collectives, shards(): lax.all_gather(mine[:, HALF:].reshape(NG * HALF, 128), TOKEN_AXES, axis=0...  11 us
    all_to_all x1, starting transfers between devices, shards(): terms = lax.all_to_all(term, ('x', 'core'), 0, 0, tiled=True)  9 us
    all_to_all x1, waiting for transfers between devices, shards(): terms = lax.all_to_all(term, ('x', 'core'), 0, 0, tiled=True)  8.89 us
    pallas_call x1, Pallas kernels, shards(): pl.pallas_call(attend_kernel, out_shape=jax.ShapeDtypeStruct((NG, KEPT +...  8.02 us
    ppermute x1, starting transfers between devices, shards(): got = lax.ppermute(stepped, ('y', 'a', 'c', 'x', 'core'), pairs)  5.46 us
  transfers between devices with their start and end apart: 4, of which 4 were waited for; matrix products, arithmetic and copies ran while one was open for 2% of the time, Pallas kernels for 0%

profile of v7, /device:TPU:25, one launch (start us, length us, event | category | flops | bytes accessed | tf_op | source)
XLA Modules:
  0.0 117.8 jit_solution(16294978683623364923)
XLA Ops:
  0.6 0.0 copy-start
  0.6 2.0 %pack.1 = bf16[16,96,128]{2,1,0:T(8,128)(2,1)} custom-call(bf16[96,384]{1,0:T(8,128)(2,1)} %q_ref.1, bf16[96,384]{1,0:T(8,128)(2,1)} %k_ref.1, bf16[96,384]{1,0:T(8,128)(2,1)} %v_ref.1), custom_call_target="tpu_custom_call" | custom-call | tf_op jit(solution)/shard_map/pack/pallas_call | solution.py:388
  2.6 14.9 %all-to-all-start = ((bf16[16,96,128]{2,1,0:T(8,128)(2,1)}), bf16[16,96,128]{2,1,0:T(8,128)(2,1)S(1)}, u32[]{:S(2)}, u32[]{:S(2)}) async-start(bf16[16,96,128]{2,1,0:T(8,128)(2,1)} %pack.1), calls=%async_computation | async-start | bytes 786432 | tf_op jit(solution)/shard_map/all_to_all | solution.py:391
  17.6 0.7 stack.31.scal_ref
  18.3 16.3 %all-to-all-done.q_ref = bf16[16,96,128]{2,1,0:T(8,128)(2,1)S(1)} async-done(((bf16[16,96,128]{2,1,0:T(8,128)(2,1)}), bf16[16,96,128]{2,1,0:T(8,128)(2,1)S(1)}, u32[]{:S(2)}, u32[]{:S(2)}) %all-to-all-start) | async-done | bytes 393248 | tf_op jit(solution)/shard_map/all_to_all | solution.py:391
  34.6 11.0 %all_gather.9.kv_ref = bf16[3072,128]{1,0:T(8,128)(2,1)S(1)} all-gather(bf16[768,128]{1,0:T(8,128)(2,1)S(1)} %bitcast.27), channel_id=1, replica_groups={{0,32,64,96},{8,40,72,104},{16,48,80,112},{24,56,88,120},{128,160,192,2..., dimensions={0}, use_global_device_ids=true | all-gather | bytes 983040 | tf_op jit(solution)/shard_map/all_gather | solution.py:392
  45.6 8.0 %attend.1 = bf16[16,56,128]{2,1,0:T(8,128)(2,1)S(1)} custom-call(s32[8]{0:T(128)S(1)} %stack.31.scal_ref, bf16[16,96,128]{2,1,0:T(8,128)(2,1)S(1)} %all-to-all-done.q_ref, bf16[3072,128]{1,0:T(8,128)(2,1)S(1)} %all_gather.9.kv_ref), custom_call_target="tpu_custom_call" | custom-call | tf_op jit(solution)/shard_map/attend/pallas_call | solution.py:399
  53.7 0.0 copy-start.9
  53.7 0.0 copy-start.7
  53.7 18.6 %all_to_all.20.part_ref = bf16[16,56,128]{2,1,0:T(8,128)(2,1)S(1)} all-to-all(bf16[16,56,128]{2,1,0:T(8,128)(2,1)S(1)} %attend.1), channel_id=1, replica_groups={{0,8,16,24,128,136,144,152,256,264,272,280,384,392,400,408},{32,40,48,5..., dimensions={0} | all-to-all | bytes 458752 | tf_op jit(solution)/shard_map/all_to_all | solution.py:414
  72.3 0.0 copy-done
  72.3 0.0 copy-start.1
  72.3 0.0 copy-start.2
  72.3 0.0 copy-start.4
  72.3 0.0 copy-start.5
  72.3 0.0 copy-start.6
  72.3 1.8 %merge.1 = bf16[8,96,384]{2,1,0:T(8,128)(2,1)} custom-call(bf16[16,56,128]{2,1,0:T(8,128)(2,1)S(1)} %all_to_all.20.part_ref, bf16[384,3072]{1,0:T(8,128)(2,1)S(1)} %copy-done), custom_call_target="tpu_custom_call" | custom-call | tf_op jit(solution)/shard_map/merge/pallas_call | solution.py:415
  74.1 0.0 copy-start.8
  74.1 0.0 copy-start.3
  74.2 9.0 %all-to-all-start.2 = ((bf16[8,96,384]{2,1,0:T(8,128)(2,1)}), bf16[8,96,384]{2,1,0:T(8,128)(2,1)S(1)}, u32[]{:S(2)}, u32[]{:S(2)}) async-start(bf16[8,96,384]{2,1,0:T(8,128)(2,1)} %merge.1), calls=%async_computation.2 | async-start | bytes 1179648 | tf_op jit(solution)/shard_map/all_to_all | solution.py:424
  83.2 0.0 copy-done.9
  83.2 0.0 copy-done.7
  83.2 0.6 gather_fusion
  83.8 0.6 gather_fusion.1
  84.5 8.9 %all-to-all-done.2.term_ref = bf16[8,96,384]{2,1,0:T(8,128)(2,1)S(1)} async-done(((bf16[8,96,384]{2,1,0:T(8,128)(2,1)}), bf16[8,96,384]{2,1,0:T(8,128)(2,1)S(1)}, u32[]{:S(2)}, u32[]{:S(2)}) %all-to-all-start.2) | async-done | bytes 589856 | tf_op jit(solution)/shard_map/all_to_all | solution.py:424
  93.3 0.0 copy-done.1
  93.3 0.0 copy-done.2
  93.4 0.0 copy-done.4
  93.4 0.0 copy-done.5
  93.4 0.0 copy-done.6
  93.4 1.7 %stream.1 = (bf16[96,384]{1,0:T(8,128)(2,1)}, bf16[8,72,128]{2,1,0:T(8,128)(2,1)}) custom-call(s32[8]{0:T(128)S(1)} %stack.31.scal_ref, bf16[8,96,384]{2,1,0:T(8,128)(2,1)S(1)} %all-to-all-done.2.term_ref, bf16[96,384]{1,0:T(8,128)(2,1)S(1)} %copy-done.1, bf16[2,384]{1,0:T(2,128)(2,1)S(1)} %copy-done.4, bf16[2,384]{1,0:T(2,128)(2,1)S(1)} %copy-done.5, ...), custom_call_target="tpu_custom_call" | custom-call | tf_op jit(solution)/shard_map/stream/pallas_call | solution.py:425
  95.0 4.1 %all-to-all-start.3 = ((bf16[8,72,128]{2,1,0:T(8,128)(2,1)}), bf16[8,72,128]{2,1,0:T(8,128)(2,1)S(1)}, u32[]{:S(2)}, u32[]{:S(2)}) async-start(bf16[8,72,128]{2,1,0:T(8,128)(2,1)} %get-tuple-element.9), calls=%async_computation.3 | async-start | bytes 294912 | tf_op jit(solution)/shard_map/all_to_all | solution.py:435
  99.2 0.0 copy-done.8
  99.3 0.1 pad_maximum_fusion.coef_ref
  99.4 5.3 %all-to-all-done.3.msg_ref = bf16[8,72,128]{2,1,0:T(8,128)(2,1)S(1)} async-done(((bf16[8,72,128]{2,1,0:T(8,128)(2,1)}), bf16[8,72,128]{2,1,0:T(8,128)(2,1)S(1)}, u32[]{:S(2)}, u32[]{:S(2)}) %all-to-all-start.3) | async-done | bytes 147488 | tf_op jit(solution)/shard_map/all_to_all | solution.py:435
  104.6 0.0 copy-done.3
  104.6 1.9 %ddim.1 = (f32[64,96]{1,0:T(8,128)}, f32[64,96]{1,0:T(8,128)}) custom-call(s32[8]{0:T(128)S(1)} %stack.31.scal_ref, f32[8]{0:T(128)S(1)} %pad_maximum_fusion.coef_ref, bf16[8,72,128]{2,1,0:T(8,128)(2,1)S(1)} %all-to-all-done.3.msg_ref, f32[64,96]{1,0:T(8,128)S(1)} %bitcast.26), custom_call_target="tpu_custom_call" | custom-call | tf_op jit(solution)/shard_map/ddim/pallas_call | solution.py:447
  106.5 5.5 %collective-permute-start = (f32[64,96]{1,0:T(8,128)}, f32[64,96]{1,0:T(8,128)S(1)}, u32[]{:S(2)}, u32[]{:S(2)}) collective-permute-start(f32[64,96]{1,0:T(8,128)} %get-tuple-element.11), channel_id=1, source_target_pairs={{0,8},{2,10},{4,12},{6,14},{8,16},{9,1},{10,18},{11,3},{12,20},{13... | collective-permute-start | bytes 73736 | tf_op jit(solution)/shard_map/ppermute | solution.py:462
  112.0 1.3 %collective-permute-done = f32[64,96]{1,0:T(8,128)S(1)} collective-permute-done((f32[64,96]{1,0:T(8,128)}, f32[64,96]{1,0:T(8,128)S(1)}, u32[]{:S(2)}, u32[]{:S(2)}) %collective-permute-start) | collective-permute-done | bytes 24608 | tf_op jit(solution)/shard_map/ppermute | solution.py:462
  113.3 3.7 %all-gather = f32[128,96]{1,0:T(8,128)S(1)} all-gather(f32[64,96]{1,0:T(8,128)S(1)} %collective-permute-done), channel_id=2, replica_groups=mesh['y'=4,'a'=4,'c'=4,'x'=4,'core'=2] {'core'}, dimensions={0}, use_global_device_ids=true | all-gather | bytes 73728 | tf_op jit(solution)/shard_map/all_gather | solution.py:463
  117.0 0.1 fusion.1
  117.1 0.7 maximum_bitcast_fusion
  (6 shorter events, 0.1 us)
Async XLA Ops:
  0.6 71.7 %copy-start = (bf16[384,3072]{1,0:T(8,128)(2,1)S(1)}, bf16[384,3072]{1,0:T(8,128)(2,1)}, u32[]{:S(2)}) copy-start(bf16[384,3072]{1,0:T(8,128)(2,1)} %w_ref.1) | copy-start | bytes 7077892
  2.6 32.0 %all-to-all-start = ((bf16[16,96,128]{2,1,0:T(8,128)(2,1)}), bf16[16,96,128]{2,1,0:T(8,128)(2,1)S(1)}, u32[]{:S(2)}, u32[]{:S(2)}) async-start(bf16[16,96,128]{2,1,0:T(8,128)(2,1)} %pack.1), calls=%async_computation | async-start | bytes 786432 | tf_op jit(solution)/shard_map/all_to_all | solution.py:391
  53.7 29.5 %copy-start.9 = (s32[2]{0:T(128)S(1)}, s32[2]{0:T(128)}, u32[]{:S(2)}) copy-start(s32[2]{0:T(128)} %param.14) | copy-start | bytes 28
  53.7 29.5 %copy-start.7 = (f32[1000]{0:T(1024)S(1)}, f32[1000]{0:T(1024)}, u32[]{:S(2)}) copy-start(f32[1000]{0:T(1024)} %constant.81.clone) | copy-start | bytes 12004
  72.3 21.0 %copy-start.1 = (bf16[96,384]{1,0:T(8,128)(2,1)S(1)}, bf16[96,384]{1,0:T(8,128)(2,1)}, u32[]{:S(2)}) copy-start(bf16[96,384]{1,0:T(8,128)(2,1)} %hid_ref.1) | copy-start | bytes 221188
  72.3 21.0 %copy-start.2 = (bf16[384,64]{0,1:T(8,128)(2,1)S(1)}, bf16[384,64]{0,1:T(8,128)(2,1)}, u32[]{:S(2)}) copy-start(bf16[384,64]{0,1:T(8,128)(2,1)} %param.23) | copy-start | bytes 147460
  72.3 21.0 %copy-start.4 = (bf16[2,384]{1,0:T(2,128)(2,1)S(1)}, bf16[2,384]{1,0:T(2,128)(2,1)}, u32[]{:S(2)}) copy-start(bf16[2,384]{1,0:T(2,128)(2,1)} %gate_ref.1) | copy-start | bytes 4612
  72.3 21.0 %copy-start.5 = (bf16[2,384]{1,0:T(2,128)(2,1)S(1)}, bf16[2,384]{1,0:T(2,128)(2,1)}, u32[]{:S(2)}) copy-start(bf16[2,384]{1,0:T(2,128)(2,1)} %shift_ref.1) | copy-start | bytes 4612
  72.3 21.0 %copy-start.6 = (bf16[2,384]{1,0:T(2,128)(2,1)S(1)}, bf16[2,384]{1,0:T(2,128)(2,1)}, u32[]{:S(2)}) copy-start(bf16[2,384]{1,0:T(2,128)(2,1)} %scale_ref.1) | copy-start | bytes 4612
  74.1 25.1 %copy-start.8 = (s32[2]{0:T(128)S(1)}, s32[2]{0:T(128)}, u32[]{:S(2)}) copy-start(s32[2]{0:T(128)} %param.13) | copy-start | bytes 28
  74.1 30.5 %copy-start.3 = (f32[96,64]{0,1:T(8,128)S(1)}, f32[96,64]{0,1:T(8,128)}, u32[]{:S(2)}) copy-start(f32[96,64]{0,1:T(8,128)} %param.24) | copy-start | bytes 73732
  74.2 19.2 %all-to-all-start.2 = ((bf16[8,96,384]{2,1,0:T(8,128)(2,1)}), bf16[8,96,384]{2,1,0:T(8,128)(2,1)S(1)}, u32[]{:S(2)}, u32[]{:S(2)}) async-start(bf16[8,96,384]{2,1,0:T(8,128)(2,1)} %merge.1), calls=%async_computation.2 | async-start | bytes 1179648 | tf_op jit(solution)/shard_map/all_to_all | solution.py:424
  95.0 9.6 %all-to-all-start.3 = ((bf16[8,72,128]{2,1,0:T(8,128)(2,1)}), bf16[8,72,128]{2,1,0:T(8,128)(2,1)S(1)}, u32[]{:S(2)}, u32[]{:S(2)}) async-start(bf16[8,72,128]{2,1,0:T(8,128)(2,1)} %get-tuple-element.9), calls=%async_computation.3 | async-start | bytes 294912 | tf_op jit(solution)/shard_map/all_to_all | solution.py:435
  106.5 6.8 %collective-permute-start = (f32[64,96]{1,0:T(8,128)}, f32[64,96]{1,0:T(8,128)S(1)}, u32[]{:S(2)}, u32[]{:S(2)}) collective-permute-start(f32[64,96]{1,0:T(8,128)} %get-tuple-element.11), channel_id=1, source_target_pairs={{0,8},{2,10},{4,12},{6,14},{8,16},{9,1},{10,18},{11,3},{12,20},{13... | collective-permute-start | bytes 73736 | tf_op jit(solution)/shard_map/ppermute | solution.py:462

commit v8 on v7

--- a/solution.py
+++ b/solution.py
@@ -144,14 +144,20 @@
             return (q_first & k_first) | (q_second & k_second)
 
         need = [[needed(half, side) for side in range(2)] for half in range(2)]
-        every = need[0][0] & need[0][1] & need[1][0] & need[1][1]
-
-        @pl.when(every)
-        def _():
-            rows = pl.ds(pl.multiple_of(j * KT, KT), KT)
-            absorb(key_ref[rows, :], val_ref[j], t, slice(0, QP))
-
-        @pl.when(jnp.logical_not(every))
+        lefts, rights = need[0][0] & need[1][0], need[0][1] & need[1][1]
+        no_left = jnp.logical_not(need[0][0] | need[1][0])
+        no_right = jnp.logical_not(need[0][1] | need[1][1])
+        rows = pl.ds(pl.multiple_of(j * KT, KT), KT)
+
+        def whole_chunk(lanes):
+            absorb(key_ref[rows, :], val_ref[j], t, lanes)
+
+        pl.when(lefts & rights)(lambda: whole_chunk(slice(0, QP)))
+        pl.when(lefts & no_right)(lambda: whole_chunk(slice(0, QT)))
+        pl.when(rights & no_left)(lambda: whole_chunk(slice(QT, QP)))
+        done = (lefts & rights) | (lefts & no_right) | (rights & no_left)
+
+        @pl.when(jnp.logical_not(done))
         def _():
             for half in range(2):
                 left, right = need[half]
@@ -181,7 +187,10 @@
             [acc_ref[pair, :HD, lanes] * (1.0 / jnp.where(sums > 0.0, sums, 1.0)), stats], axis=0
         )
         for c in range(NB):
-            moved = pltpu.roll(whole, QT - c * TOK, 1) if c else whole
+            skip = c * TOK // 128 * 128
+            moved = whole[:, skip : min(skip + 256, QT)]
+            if c:
+                moved = pltpu.roll(moved, moved.shape[1] - (c * TOK - skip), 1)
             moved = moved[:, :128]
             rest = moved[KEPT:HD]
             thirds = [pltpu.roll(rest, (TOK - 32 * k) % 128, 1) for k in range(3)]
@@ -189,9 +198,7 @@
             out_ref[t * NB + c] = jnp.concatenate([kept, moved[HD:]], axis=0).astype(BF)
 
 
-def merge_kernel(part_ref, w_ref, out_ref, att_ref, copy_ref, sem):
-    copy = pltpu.make_async_copy(w_ref, copy_ref, sem)
-    copy.start()
+def merge_kernel(part_ref, w_ref, out_ref, att_ref):
     lane_r = lax.broadcasted_iota(jnp.int32, (HD - KEPT, 128), 1)
     stat = part_ref[:, KEPT:, :].astype(F32)
     tops = stat[:, 0] + stat[:, 1] + stat[:, 2]
@@ -216,10 +223,9 @@
             mixed += shares[i : i + 1] * jnp.concatenate([part, rest], axis=0)
         att_ref[HD * h : HD * h + HD, :] = mixed
     attended = att_ref[...].T[:TOK].astype(BF)
-    copy.wait()
     for j in range(NHEAD):
         out_ref[j] = jnp.dot(
-            attended, copy_ref[:, 384 * j : 384 * j + 384], preferred_element_type=F32
+            attended, w_ref[:, 384 * j : 384 * j + 384], preferred_element_type=F32
         ).astype(BF)
 
 
@@ -415,9 +421,9 @@
     term = pl.pallas_call(
         merge_kernel,
         out_shape=jax.ShapeDtypeStruct((NHEAD, TOK, 384), BF),
-        in_specs=[any_vmem, pl.BlockSpec(memory_space=pl.ANY)],
+        in_specs=[any_vmem, any_vmem],
         out_specs=any_vmem,
-        scratch_shapes=[VMEM((384, 128), F32), VMEM((384, D), BF), pltpu.SemaphoreType.DMA],
+        scratch_shapes=[VMEM((384, 128), F32)],
         compiler_params=big,
         name="merge",
     )(parts, attn_weight)

time: 119 us -> 119 us (level)
  no operation moved by 1% of the time
where the time goes in v8:
time: 119 us; the launch traced here: 117 us
  blocking collectives  33.7 us (28%)
  starting transfers between devices  33 us (28%)
  waiting for transfers between devices  31.7 us (27%)
  Pallas kernels  15.2 us (13%)
  local copies, waits for them, and re-layouts  2.05 us (2%)
    all_to_all x1, blocking collectives, shards(): lax.all_to_all(partial, TOKEN_AXES, 0, 0, tiled=True, axis_index_groups=n...  18.6 us
    all_to_all x1, waiting for transfers between devices, shards(): lax.all_to_all(packed, TOKEN_AXES, 0, 0, tiled=True, axis_index_groups=near)  16.3 us
    all_to_all x1, starting transfers between devices, shards(): lax.all_to_all(packed, TOKEN_AXES, 0, 0, tiled=True, axis_index_groups=near)  14.9 us
    all_gather x1, blocking collectives, shards(): lax.all_gather(mine[:, HALF:].reshape(NG * HALF, 128), TOKEN_AXES, axis=0...  11 us
    all_to_all x1, starting transfers between devices, shards(): terms = lax.all_to_all(term, ('x', 'core'), 0, 0, tiled=True)  8.9 us
    all_to_all x1, waiting for transfers between devices, shards(): terms = lax.all_to_all(term, ('x', 'core'), 0, 0, tiled=True)  8.89 us
    pallas_call x1, Pallas kernels, shards(): pl.pallas_call(attend_kernel, out_shape=jax.ShapeDtypeStruct((NG, KEPT +...  8.12 us
    all_to_all x1, waiting for transfers between devices, shards(): message = lax.all_to_all(message, ('x', 'core'), 0, 0, tiled=True)  5.26 us
  transfers between devices with their start and end apart: 4, of which 4 were waited for; matrix products, arithmetic and copies ran while one was open for 2% of the time, Pallas kernels for 0%

profile of v8, /device:TPU:25, one launch (start us, length us, event | category | flops | bytes accessed | tf_op | source)
XLA Modules:
  0.0 117.5 jit_solution(16574523551134457448)
XLA Ops:
  0.6 0.0 copy-start
  0.6 2.0 %pack.1 = bf16[16,96,128]{2,1,0:T(8,128)(2,1)} custom-call(bf16[96,384]{1,0:T(8,128)(2,1)} %q_ref.1, bf16[96,384]{1,0:T(8,128)(2,1)} %k_ref.1, bf16[96,384]{1,0:T(8,128)(2,1)} %v_ref.1), custom_call_target="tpu_custom_call" | custom-call | tf_op jit(solution)/shard_map/pack/pallas_call | solution.py:394
  2.6 14.9 %all-to-all-start = ((bf16[16,96,128]{2,1,0:T(8,128)(2,1)}), bf16[16,96,128]{2,1,0:T(8,128)(2,1)S(1)}, u32[]{:S(2)}, u32[]{:S(2)}) async-start(bf16[16,96,128]{2,1,0:T(8,128)(2,1)} %pack.1), calls=%async_computation | async-start | bytes 786432 | tf_op jit(solution)/shard_map/all_to_all | solution.py:397
  17.6 0.7 stack.31.scal_ref
  18.3 16.3 %all-to-all-done.q_ref = bf16[16,96,128]{2,1,0:T(8,128)(2,1)S(1)} async-done(((bf16[16,96,128]{2,1,0:T(8,128)(2,1)}), bf16[16,96,128]{2,1,0:T(8,128)(2,1)S(1)}, u32[]{:S(2)}, u32[]{:S(2)}) %all-to-all-start) | async-done | bytes 393248 | tf_op jit(solution)/shard_map/all_to_all | solution.py:397
  34.6 11.0 %all_gather.9.kv_ref = bf16[3072,128]{1,0:T(8,128)(2,1)S(1)} all-gather(bf16[768,128]{1,0:T(8,128)(2,1)S(1)} %bitcast.27), channel_id=1, replica_groups={{0,32,64,96},{8,40,72,104},{16,48,80,112},{24,56,88,120},{128,160,192,2..., dimensions={0}, use_global_device_ids=true | all-gather | bytes 983040 | tf_op jit(solution)/shard_map/all_gather | solution.py:398
  45.6 8.1 %attend.1 = bf16[16,56,128]{2,1,0:T(8,128)(2,1)S(1)} custom-call(s32[8]{0:T(128)S(1)} %stack.31.scal_ref, bf16[16,96,128]{2,1,0:T(8,128)(2,1)S(1)} %all-to-all-done.q_ref, bf16[3072,128]{1,0:T(8,128)(2,1)S(1)} %all_gather.9.kv_ref), custom_call_target="tpu_custom_call" | custom-call | tf_op jit(solution)/shard_map/attend/pallas_call | solution.py:405
  53.8 0.0 copy-start.9
  53.8 0.0 copy-start.7
  53.8 18.6 %all_to_all.20.part_ref = bf16[16,56,128]{2,1,0:T(8,128)(2,1)S(1)} all-to-all(bf16[16,56,128]{2,1,0:T(8,128)(2,1)S(1)} %attend.1), channel_id=1, replica_groups={{0,8,16,24,128,136,144,152,256,264,272,280,384,392,400,408},{32,40,48,5..., dimensions={0} | all-to-all | bytes 458752 | tf_op jit(solution)/shard_map/all_to_all | solution.py:420
  72.4 0.0 copy-done
  72.4 0.0 copy-start.1
  72.4 0.0 copy-start.2
  72.4 0.0 copy-start.4
  72.4 0.0 copy-start.5
  72.4 0.0 copy-start.6
  72.4 1.6 %merge.1 = bf16[8,96,384]{2,1,0:T(8,128)(2,1)} custom-call(bf16[16,56,128]{2,1,0:T(8,128)(2,1)S(1)} %all_to_all.20.part_ref, bf16[384,3072]{1,0:T(8,128)(2,1)S(1)} %copy-done), custom_call_target="tpu_custom_call" | custom-call | tf_op jit(solution)/shard_map/merge/pallas_call | solution.py:421
  74.0 0.0 copy-start.8
  74.0 0.0 copy-start.3
  74.0 8.9 %all-to-all-start.2 = ((bf16[8,96,384]{2,1,0:T(8,128)(2,1)}), bf16[8,96,384]{2,1,0:T(8,128)(2,1)S(1)}, u32[]{:S(2)}, u32[]{:S(2)}) async-start(bf16[8,96,384]{2,1,0:T(8,128)(2,1)} %merge.1), calls=%async_computation.2 | async-start | bytes 1179648 | tf_op jit(solution)/shard_map/all_to_all | solution.py:430
  82.9 0.0 copy-done.9
  82.9 0.0 copy-done.7
  82.9 0.6 gather_fusion
  83.6 0.6 gather_fusion.1
  84.2 8.9 %all-to-all-done.2.term_ref = bf16[8,96,384]{2,1,0:T(8,128)(2,1)S(1)} async-done(((bf16[8,96,384]{2,1,0:T(8,128)(2,1)}), bf16[8,96,384]{2,1,0:T(8,128)(2,1)S(1)}, u32[]{:S(2)}, u32[]{:S(2)}) %all-to-all-start.2) | async-done | bytes 589856 | tf_op jit(solution)/shard_map/all_to_all | solution.py:430
  93.1 0.0 copy-done.1
  93.1 0.0 copy-done.2
  93.1 0.0 copy-done.4
  93.1 0.0 copy-done.5
  93.1 0.0 copy-done.6
  93.1 1.7 %stream.1 = (bf16[96,384]{1,0:T(8,128)(2,1)}, bf16[8,72,128]{2,1,0:T(8,128)(2,1)}) custom-call(s32[8]{0:T(128)S(1)} %stack.31.scal_ref, bf16[8,96,384]{2,1,0:T(8,128)(2,1)S(1)} %all-to-all-done.2.term_ref, bf16[96,384]{1,0:T(8,128)(2,1)S(1)} %copy-done.1, bf16[2,384]{1,0:T(2,128)(2,1)S(1)} %copy-done.4, bf16[2,384]{1,0:T(2,128)(2,1)S(1)} %copy-done.5, ...), custom_call_target="tpu_custom_call" | custom-call | tf_op jit(solution)/shard_map/stream/pallas_call | solution.py:431
  94.8 4.1 %all-to-all-start.3 = ((bf16[8,72,128]{2,1,0:T(8,128)(2,1)}), bf16[8,72,128]{2,1,0:T(8,128)(2,1)S(1)}, u32[]{:S(2)}, u32[]{:S(2)}) async-start(bf16[8,72,128]{2,1,0:T(8,128)(2,1)} %get-tuple-element.9), calls=%async_computation.3 | async-start | bytes 294912 | tf_op jit(solution)/shard_map/all_to_all | solution.py:441
  98.9 0.0 copy-done.8
  99.0 0.1 pad_maximum_fusion.coef_ref
  99.1 5.3 %all-to-all-done.3.msg_ref = bf16[8,72,128]{2,1,0:T(8,128)(2,1)S(1)} async-done(((bf16[8,72,128]{2,1,0:T(8,128)(2,1)}), bf16[8,72,128]{2,1,0:T(8,128)(2,1)S(1)}, u32[]{:S(2)}, u32[]{:S(2)}) %all-to-all-start.3) | async-done | bytes 147488 | tf_op jit(solution)/shard_map/all_to_all | solution.py:441
  104.4 0.0 copy-done.3
  104.4 1.9 %ddim.1 = (f32[64,96]{1,0:T(8,128)}, f32[64,96]{1,0:T(8,128)}) custom-call(s32[8]{0:T(128)S(1)} %stack.31.scal_ref, f32[8]{0:T(128)S(1)} %pad_maximum_fusion.coef_ref, bf16[8,72,128]{2,1,0:T(8,128)(2,1)S(1)} %all-to-all-done.3.msg_ref, f32[64,96]{1,0:T(8,128)S(1)} %bitcast.26), custom_call_target="tpu_custom_call" | custom-call | tf_op jit(solution)/shard_map/ddim/pallas_call | solution.py:453
  106.2 5.1 %collective-permute-start = (f32[64,96]{1,0:T(8,128)}, f32[64,96]{1,0:T(8,128)S(1)}, u32[]{:S(2)}, u32[]{:S(2)}) collective-permute-start(f32[64,96]{1,0:T(8,128)} %get-tuple-element.11), channel_id=1, source_target_pairs={{0,8},{2,10},{4,12},{6,14},{8,16},{9,1},{10,18},{11,3},{12,20},{13... | collective-permute-start | bytes 73736 | tf_op jit(solution)/shard_map/ppermute | solution.py:468
  111.3 1.3 %collective-permute-done = f32[64,96]{1,0:T(8,128)S(1)} collective-permute-done((f32[64,96]{1,0:T(8,128)}, f32[64,96]{1,0:T(8,128)S(1)}, u32[]{:S(2)}, u32[]{:S(2)}) %collective-permute-start) | collective-permute-done | bytes 24608 | tf_op jit(solution)/shard_map/ppermute | solution.py:468
  112.6 4.1 %all-gather = f32[128,96]{1,0:T(8,128)S(1)} all-gather(f32[64,96]{1,0:T(8,128)S(1)} %collective-permute-done), channel_id=2, replica_groups=mesh['y'=4,'a'=4,'c'=4,'x'=4,'core'=2] {'core'}, dimensions={0}, use_global_device_ids=true | all-gather | bytes 73728 | tf_op jit(solution)/shard_map/all_gather | solution.py:469
  116.7 0.1 fusion.1
  116.8 0.7 maximum_bitcast_fusion
  (6 shorter events, 0.1 us)
Async XLA Ops:
  0.6 71.8 %copy-start = (bf16[384,3072]{1,0:T(8,128)(2,1)S(1)}, bf16[384,3072]{1,0:T(8,128)(2,1)}, u32[]{:S(2)}) copy-start(bf16[384,3072]{1,0:T(8,128)(2,1)} %w_ref.1) | copy-start | bytes 7077892
  2.6 32.0 %all-to-all-start = ((bf16[16,96,128]{2,1,0:T(8,128)(2,1)}), bf16[16,96,128]{2,1,0:T(8,128)(2,1)S(1)}, u32[]{:S(2)}, u32[]{:S(2)}) async-start(bf16[16,96,128]{2,1,0:T(8,128)(2,1)} %pack.1), calls=%async_computation | async-start | bytes 786432 | tf_op jit(solution)/shard_map/all_to_all | solution.py:397
  53.8 29.1 %copy-start.9 = (s32[2]{0:T(128)S(1)}, s32[2]{0:T(128)}, u32[]{:S(2)}) copy-start(s32[2]{0:T(128)} %param.14) | copy-start | bytes 28
  53.8 29.2 %copy-start.7 = (f32[1000]{0:T(1024)S(1)}, f32[1000]{0:T(1024)}, u32[]{:S(2)}) copy-start(f32[1000]{0:T(1024)} %constant.81.clone) | copy-start | bytes 12004
  72.4 20.7 %copy-start.1 = (bf16[96,384]{1,0:T(8,128)(2,1)S(1)}, bf16[96,384]{1,0:T(8,128)(2,1)}, u32[]{:S(2)}) copy-start(bf16[96,384]{1,0:T(8,128)(2,1)} %hid_ref.1) | copy-start | bytes 221188
  72.4 20.7 %copy-start.2 = (bf16[384,64]{0,1:T(8,128)(2,1)S(1)}, bf16[384,64]{0,1:T(8,128)(2,1)}, u32[]{:S(2)}) copy-start(bf16[384,64]{0,1:T(8,128)(2,1)} %param.23) | copy-start | bytes 147460
  72.4 20.7 %copy-start.4 = (bf16[2,384]{1,0:T(2,128)(2,1)S(1)}, bf16[2,384]{1,0:T(2,128)(2,1)}, u32[]{:S(2)}) copy-start(bf16[2,384]{1,0:T(2,128)(2,1)} %gate_ref.1) | copy-start | bytes 4612
  72.4 20.7 %copy-start.5 = (bf16[2,384]{1,0:T(2,128)(2,1)S(1)}, bf16[2,384]{1,0:T(2,128)(2,1)}, u32[]{:S(2)}) copy-start(bf16[2,384]{1,0:T(2,128)(2,1)} %shift_ref.1) | copy-start | bytes 4612
  72.4 20.7 %copy-start.6 = (bf16[2,384]{1,0:T(2,128)(2,1)S(1)}, bf16[2,384]{1,0:T(2,128)(2,1)}, u32[]{:S(2)}) copy-start(bf16[2,384]{1,0:T(2,128)(2,1)} %scale_ref.1) | copy-start | bytes 4612
  74.0 24.9 %copy-start.8 = (s32[2]{0:T(128)S(1)}, s32[2]{0:T(128)}, u32[]{:S(2)}) copy-start(s32[2]{0:T(128)} %param.13) | copy-start | bytes 28
  74.0 30.4 %copy-start.3 = (f32[96,64]{0,1:T(8,128)S(1)}, f32[96,64]{0,1:T(8,128)}, u32[]{:S(2)}) copy-start(f32[96,64]{0,1:T(8,128)} %param.24) | copy-start | bytes 73732
  74.0 19.1 %all-to-all-start.2 = ((bf16[8,96,384]{2,1,0:T(8,128)(2,1)}), bf16[8,96,384]{2,1,0:T(8,128)(2,1)S(1)}, u32[]{:S(2)}, u32[]{:S(2)}) async-start(bf16[8,96,384]{2,1,0:T(8,128)(2,1)} %merge.1), calls=%async_computation.2 | async-start | bytes 1179648 | tf_op jit(solution)/shard_map/all_to_all | solution.py:430
  94.8 9.6 %all-to-all-start.3 = ((bf16[8,72,128]{2,1,0:T(8,128)(2,1)}), bf16[8,72,128]{2,1,0:T(8,128)(2,1)S(1)}, u32[]{:S(2)}, u32[]{:S(2)}) async-start(bf16[8,72,128]{2,1,0:T(8,128)(2,1)} %get-tuple-element.9), calls=%async_computation.3 | async-start | bytes 294912 | tf_op jit(solution)/shard_map/all_to_all | solution.py:441
  106.2 6.4 %collective-permute-start = (f32[64,96]{1,0:T(8,128)}, f32[64,96]{1,0:T(8,128)S(1)}, u32[]{:S(2)}, u32[]{:S(2)}) collective-permute-start(f32[64,96]{1,0:T(8,128)} %get-tuple-element.11), channel_id=1, source_target_pairs={{0,8},{2,10},{4,12},{6,14},{8,16},{9,1},{10,18},{11,3},{12,20},{13... | collective-permute-start | bytes 73736 | tf_op jit(solution)/shard_map/ppermute | solution.py:468

commit v9 on v8

--- a/solution.py
+++ b/solution.py
@@ -391,10 +391,22 @@
 
     any_vmem = pl.BlockSpec(memory_space=VMEM)
 
+    table = jnp.asarray(alpha_table())
+    alpha_now = table[step_index]
+    alpha_prev = table[step_index - STEP_GAP]
+    coef = jnp.concatenate(
+        [
+            jnp.sqrt(alpha_now),
+            jnp.sqrt(1.0 - alpha_now),
+            jnp.sqrt(alpha_prev),
+            jnp.sqrt(1.0 - alpha_prev),
+        ]
+    )
     packed = pl.pallas_call(
         pack_kernel, out_shape=jax.ShapeDtypeStruct((NG, TOK, 128), BF), name="pack"
     )(query_act, key_act, value_act)
     mine = lax.all_to_all(packed, TOKEN_AXES, 0, 0, tiled=True, axis_index_groups=near)
+    mine, coef = lax.optimization_barrier((mine, coef))
     keyvals = lax.all_gather(
         mine[:, HALF:].reshape(NG * HALF, 128),
         TOKEN_AXES,
@@ -439,17 +451,6 @@
         name="stream",
     )(scal, terms, hidden, gate_mod, shift_mod, scale_mod, proj_weight.T)
     message = lax.all_to_all(message, ("x", "core"), 0, 0, tiled=True)
-    table = jnp.asarray(alpha_table())
-    alpha_now = table[step_index]
-    alpha_prev = table[step_index - STEP_GAP]
-    coef = jnp.concatenate(
-        [
-            jnp.sqrt(alpha_now),
-            jnp.sqrt(1.0 - alpha_now),
-            jnp.sqrt(alpha_prev),
-            jnp.sqrt(1.0 - alpha_prev),
-        ]
-    )
     clean, stepped = pl.pallas_call(
         step_kernel,
         out_shape=(jax.ShapeDtypeStruct((64, TOK), F32),) * 2,

time: 119 us -> 118 us (level); the launches traced: 117 us -> 118 us
  blocking collectives: 33.7 us -> 57 us
  starting transfers between devices: 33 us -> 21.2 us
  waiting for transfers between devices: 31.7 us -> 21.9 us
  Pallas kernels: 15.2 us -> 12.9 us
    all_to_all x0 -> x1, blocking collectives: none -> 21.6 us  [shards(): terms = lax.all_to_all(term, ('x', 'core'), 0, 0, tiled=True)]
    all_to_all x1 -> x0, starting transfers between devices: 8.9 us -> none  [shards(): terms = lax.all_to_all(term, ('x', 'core'), 0, 0, tiled=True)]
    all_to_all x1 -> x0, waiting for transfers between devices: 8.89 us -> none  [shards(): terms = lax.all_to_all(term, ('x', 'core'), 0, 0, tiled=True)]
    ppermute x1, starting transfers between devices: 5.06 us -> 2.22 us  [shards(): got = lax.ppermute(stepped, ('y', 'a', 'c', 'x', 'core'), pairs)]
    all_to_all x1, waiting for transfers between devices: 16.3 us -> 14 us  [shards(): lax.all_to_all(packed, TOKEN_AXES, 0, 0, tiled=True, axis_index_groups=near)]
    all_gather x1, blocking collectives: 4.11 us -> 5.64 us  [shards(): both = lax.all_gather(got, 'core')]
    ppermute x1, waiting for transfers between devices: 1.27 us -> 2.57 us  [shards(): got = lax.ppermute(stepped, ('y', 'a', 'c', 'x', 'core'), pairs)]
    pallas_call x1, Pallas kernels: 8.12 us -> 6.83 us  [shards(): pl.pallas_call(attend_kernel, out_shape=jax.ShapeDtypeStruct((NG, KEPT +...]
  transfers between devices with their start and end apart: 4 -> 3, of which waited for: 4 -> 3; matrix products, arithmetic and copies ran while one was open for 2% -> 3% of each run, Pallas kernels for 0% -> 0%
where the time goes in v9:
time: 118 us
  blocking collectives  57 us (48%)
  waiting for transfers between devices  21.9 us (19%)
  starting transfers between devices  21.2 us (18%)
  Pallas kernels  12.9 us (11%)
  local copies, waits for them, and re-layouts  2.13 us (2%)
  other arithmetic  1.73 us (1%)
    all_to_all x1, blocking collectives, shards(): terms = lax.all_to_all(term, ('x', 'core'), 0, 0, tiled=True)  21.6 us
    all_to_all x1, blocking collectives, shards(): lax.all_to_all(partial, TOKEN_AXES, 0, 0, tiled=True, axis_index_groups=n...  18.8 us
    all_to_all x1, starting transfers between devices, shards(): lax.all_to_all(packed, TOKEN_AXES, 0, 0, tiled=True, axis_index_groups=near)  14.9 us
    all_to_all x1, waiting for transfers between devices, shards(): lax.all_to_all(packed, TOKEN_AXES, 0, 0, tiled=True, axis_index_groups=near)  14 us
    all_gather x1, blocking collectives, shards(): lax.all_gather(mine[:, HALF:].reshape(NG * HALF, 128), TOKEN_AXES, axis=0...  11 us
    pallas_call x1, Pallas kernels, shards(): pl.pallas_call(attend_kernel, out_shape=jax.ShapeDtypeStruct((NG, KEPT +...  6.83 us
    all_gather x1, blocking collectives, shards(): both = lax.all_gather(got, 'core')  5.64 us
    all_to_all x1, waiting for transfers between devices, shards(): message = lax.all_to_all(message, ('x', 'core'), 0, 0, tiled=True)  5.35 us
  transfers between devices with their start and end apart: 3, of which 3 were waited for; matrix products, arithmetic and copies ran while one was open for 3% of the time, Pallas kernels for 0%

profile of v9, /device:TPU:25, one launch (start us, length us, event | category | flops | bytes accessed | tf_op | source)
XLA Modules:
  0.0 117.8 jit_solution(5944219854372253385)
XLA Ops:
  0.6 0.0 copy-start.7
  0.6 0.0 copy-start.8
  0.7 1.8 %pack.1 = bf16[16,96,128]{2,1,0:T(8,128)(2,1)} custom-call(bf16[96,384]{1,0:T(8,128)(2,1)} %q_ref.1, bf16[96,384]{1,0:T(8,128)(2,1)} %k_ref.1, bf16[96,384]{1,0:T(8,128)(2,1)} %v_ref.1), custom_call_target="tpu_custom_call" | custom-call | tf_op jit(solution)/shard_map/pack/pallas_call | solution.py:405
  2.5 14.9 %all-to-all-start = ((bf16[16,96,128]{2,1,0:T(8,128)(2,1)}), bf16[16,96,128]{2,1,0:T(8,128)(2,1)S(1)}, u32[]{:S(2)}, u32[]{:S(2)}) async-start(bf16[16,96,128]{2,1,0:T(8,128)(2,1)} %pack.1), calls=%async_computation | async-start | bytes 786432 | tf_op jit(solution)/shard_map/all_to_all | solution.py:408
  17.4 0.0 copy-start
  17.5 0.8 compare_select_fusion.1
  18.3 1.3 %gather_fusion = f32[2]{0:T(128)S(1)} fusion(f32[1000]{0:T(1024)} %constant.81.clone, s32[1024]{0:T(1024)S(1)} %get-tuple-element.25), kind=kCustom, calls=%fused_computation | custom fusion | bytes 24 | tf_op jit(solution)/shard_map/gather | solution.py:395
  19.6 0.0 copy-done.7
  19.6 0.6 gather_fusion.1
  20.2 0.0 copy-done.8
  20.2 0.1 stack.31.scal_ref
  20.4 0.1 pad_maximum_fusion.coef_ref
  20.5 14.0 %all-to-all-done.q_ref = bf16[16,96,128]{2,1,0:T(8,128)(2,1)S(1)} async-done(((bf16[16,96,128]{2,1,0:T(8,128)(2,1)}), bf16[16,96,128]{2,1,0:T(8,128)(2,1)S(1)}, u32[]{:S(2)}, u32[]{:S(2)}) %all-to-all-start) | async-done | bytes 393248 | tf_op jit(solution)/shard_map/all_to_all | solution.py:408
  34.5 11.0 %all_gather.9.kv_ref = bf16[3072,128]{1,0:T(8,128)(2,1)S(1)} all-gather(bf16[768,128]{1,0:T(8,128)(2,1)S(1)} %bitcast.27), channel_id=1, replica_groups={{0,32,64,96},{8,40,72,104},{16,48,80,112},{24,56,88,120},{128,160,192,2..., dimensions={0}, use_global_device_ids=true | all-gather | bytes 983040 | tf_op jit(solution)/shard_map/all_gather | solution.py:410
  45.5 6.8 %attend.1 = bf16[16,56,128]{2,1,0:T(8,128)(2,1)S(1)} custom-call(s32[8]{0:T(128)S(1)} %stack.31.scal_ref, bf16[16,96,128]{2,1,0:T(8,128)(2,1)S(1)} %all-to-all-done.q_ref, bf16[3072,128]{1,0:T(8,128)(2,1)S(1)} %all_gather.9.kv_ref), custom_call_target="tpu_custom_call" | custom-call | tf_op jit(solution)/shard_map/attend/pallas_call | solution.py:417
  52.3 0.0 copy-start.1
  52.4 0.0 copy-start.2
  52.4 0.0 copy-start.4
  52.4 0.0 copy-start.5
  52.4 0.0 copy-start.6
  52.4 18.8 %all_to_all.20.part_ref = bf16[16,56,128]{2,1,0:T(8,128)(2,1)S(1)} all-to-all(bf16[16,56,128]{2,1,0:T(8,128)(2,1)S(1)} %attend.1), channel_id=1, replica_groups={{0,8,16,24,128,136,144,152,256,264,272,280,384,392,400,408},{32,40,48,5..., dimensions={0} | all-to-all | bytes 458752 | tf_op jit(solution)/shard_map/all_to_all | solution.py:432
  71.2 0.0 copy-done
  71.2 0.0 copy-start.3
  71.2 0.7 merge.1
  71.9 21.6 %all_to_all.21.term_ref = bf16[8,96,384]{2,1,0:T(8,128)(2,1)S(1)} all-to-all(bf16[8,96,384]{2,1,0:T(8,128)(2,1)S(1)} %merge.1), channel_id=1, replica_groups=mesh['y'=4,'a'=4,'c'=4,'x'=4,'core'=2] {'x','core'}, dimensions={0} | all-to-all | bytes 1179648 | tf_op jit(solution)/shard_map/all_to_all | solution.py:442
  93.5 0.0 copy-done.1
  93.5 0.0 copy-done.2
  93.5 0.0 copy-done.4
  93.5 0.0 copy-done.5
  93.5 0.0 copy-done.6
  93.5 1.7 %stream.1 = (bf16[96,384]{1,0:T(8,128)(2,1)}, bf16[8,72,128]{2,1,0:T(8,128)(2,1)}) custom-call(s32[8]{0:T(128)S(1)} %stack.31.scal_ref, bf16[8,96,384]{2,1,0:T(8,128)(2,1)S(1)} %all_to_all.21.term_ref, bf16[96,384]{1,0:T(8,128)(2,1)S(1)} %copy-done.1, bf16[2,384]{1,0:T(2,128)(2,1)S(1)} %copy-done.4, bf16[2,384]{1,0:T(2,128)(2,1)S(1)} %copy-done.5, ...), custom_call_target="tpu_custom_call" | custom-call | tf_op jit(solution)/shard_map/stream/pallas_call | solution.py:443
  95.2 4.0 %all-to-all-start.3 = ((bf16[8,72,128]{2,1,0:T(8,128)(2,1)}), bf16[8,72,128]{2,1,0:T(8,128)(2,1)S(1)}, u32[]{:S(2)}, u32[]{:S(2)}) async-start(bf16[8,72,128]{2,1,0:T(8,128)(2,1)} %get-tuple-element.13), calls=%async_computation.3 | async-start | bytes 294912 | tf_op jit(solution)/shard_map/all_to_all | solution.py:453
  99.3 5.4 %all-to-all-done.3.msg_ref = bf16[8,72,128]{2,1,0:T(8,128)(2,1)S(1)} async-done(((bf16[8,72,128]{2,1,0:T(8,128)(2,1)}), bf16[8,72,128]{2,1,0:T(8,128)(2,1)S(1)}, u32[]{:S(2)}, u32[]{:S(2)}) %all-to-all-start.3) | async-done | bytes 147488 | tf_op jit(solution)/shard_map/all_to_all | solution.py:453
  104.6 0.0 copy-done.3
  104.6 1.9 %ddim.1 = (f32[64,96]{1,0:T(8,128)}, f32[64,96]{1,0:T(8,128)}) custom-call(s32[8]{0:T(128)S(1)} %stack.31.scal_ref, f32[8]{0:T(128)S(1)} %pad_maximum_fusion.coef_ref, bf16[8,72,128]{2,1,0:T(8,128)(2,1)S(1)} %all-to-all-done.3.msg_ref, f32[64,96]{1,0:T(8,128)S(1)} %bitcast.26), custom_call_target="tpu_custom_call" | custom-call | tf_op jit(solution)/shard_map/ddim/pallas_call | solution.py:454
  106.5 2.2 %collective-permute-start = (f32[64,96]{1,0:T(8,128)}, f32[64,96]{1,0:T(8,128)S(1)}, u32[]{:S(2)}, u32[]{:S(2)}) collective-permute-start(f32[64,96]{1,0:T(8,128)} %get-tuple-element.15), channel_id=1, source_target_pairs={{0,8},{2,10},{4,12},{6,14},{8,16},{9,1},{10,18},{11,3},{12,20},{13... | collective-permute-start | bytes 73736 | tf_op jit(solution)/shard_map/ppermute | solution.py:469
  108.8 2.6 %collective-permute-done = f32[64,96]{1,0:T(8,128)S(1)} collective-permute-done((f32[64,96]{1,0:T(8,128)}, f32[64,96]{1,0:T(8,128)S(1)}, u32[]{:S(2)}, u32[]{:S(2)}) %collective-permute-start) | collective-permute-done | bytes 24608 | tf_op jit(solution)/shard_map/ppermute | solution.py:469
  111.4 5.6 %all-gather = f32[128,96]{1,0:T(8,128)S(1)} all-gather(f32[64,96]{1,0:T(8,128)S(1)} %collective-permute-done), channel_id=2, replica_groups=mesh['y'=4,'a'=4,'c'=4,'x'=4,'core'=2] {'core'}, dimensions={0}, use_global_device_ids=true | all-gather | bytes 73728 | tf_op jit(solution)/shard_map/all_gather | solution.py:470
  117.0 0.1 fusion.1
  117.1 0.7 maximum_bitcast_fusion
  (5 shorter events, 0.1 us)
Async XLA Ops:
  0.6 19.0 %copy-start.7 = (f32[1000]{0:T(1024)S(1)}, f32[1000]{0:T(1024)}, u32[]{:S(2)}) copy-start(f32[1000]{0:T(1024)} %constant.81.clone) | copy-start | bytes 12004
  0.6 19.6 %copy-start.8 = (s32[2]{0:T(128)S(1)}, s32[2]{0:T(128)}, u32[]{:S(2)}) copy-start(s32[2]{0:T(128)} %param.13) | copy-start | bytes 28
  2.5 32.0 %all-to-all-start = ((bf16[16,96,128]{2,1,0:T(8,128)(2,1)}), bf16[16,96,128]{2,1,0:T(8,128)(2,1)S(1)}, u32[]{:S(2)}, u32[]{:S(2)}) async-start(bf16[16,96,128]{2,1,0:T(8,128)(2,1)} %pack.1), calls=%async_computation | async-start | bytes 786432 | tf_op jit(solution)/shard_map/all_to_all | solution.py:408
  17.4 53.7 %copy-start = (bf16[384,3072]{1,0:T(8,128)(2,1)S(1)}, bf16[384,3072]{1,0:T(8,128)(2,1)}, u32[]{:S(2)}) copy-start(bf16[384,3072]{1,0:T(8,128)(2,1)} %w_ref.1) | copy-start | bytes 7077892
  52.3 41.1 %copy-start.1 = (bf16[96,384]{1,0:T(8,128)(2,1)S(1)}, bf16[96,384]{1,0:T(8,128)(2,1)}, u32[]{:S(2)}) copy-start(bf16[96,384]{1,0:T(8,128)(2,1)} %hid_ref.1) | copy-start | bytes 221188
  52.4 41.1 %copy-start.2 = (bf16[384,64]{0,1:T(8,128)(2,1)S(1)}, bf16[384,64]{0,1:T(8,128)(2,1)}, u32[]{:S(2)}) copy-start(bf16[384,64]{0,1:T(8,128)(2,1)} %param.23) | copy-start | bytes 147460
  52.4 41.1 %copy-start.4 = (bf16[2,384]{1,0:T(2,128)(2,1)S(1)}, bf16[2,384]{1,0:T(2,128)(2,1)}, u32[]{:S(2)}) copy-start(bf16[2,384]{1,0:T(2,128)(2,1)} %gate_ref.1) | copy-start | bytes 4612
  52.4 41.1 %copy-start.5 = (bf16[2,384]{1,0:T(2,128)(2,1)S(1)}, bf16[2,384]{1,0:T(2,128)(2,1)}, u32[]{:S(2)}) copy-start(bf16[2,384]{1,0:T(2,128)(2,1)} %shift_ref.1) | copy-start | bytes 4612
  52.4 41.1 %copy-start.6 = (bf16[2,384]{1,0:T(2,128)(2,1)S(1)}, bf16[2,384]{1,0:T(2,128)(2,1)}, u32[]{:S(2)}) copy-start(bf16[2,384]{1,0:T(2,128)(2,1)} %scale_ref.1) | copy-start | bytes 4612
  71.2 33.5 %copy-start.3 = (f32[96,64]{0,1:T(8,128)S(1)}, f32[96,64]{0,1:T(8,128)}, u32[]{:S(2)}) copy-start(f32[96,64]{0,1:T(8,128)} %param.24) | copy-start | bytes 73732
  95.2 9.5 %all-to-all-start.3 = ((bf16[8,72,128]{2,1,0:T(8,128)(2,1)}), bf16[8,72,128]{2,1,0:T(8,128)(2,1)S(1)}, u32[]{:S(2)}, u32[]{:S(2)}) async-start(bf16[8,72,128]{2,1,0:T(8,128)(2,1)} %get-tuple-element.13), calls=%async_computation.3 | async-start | bytes 294912 | tf_op jit(solution)/shard_map/all_to_all | solution.py:453
  106.5 4.9 %collective-permute-start = (f32[64,96]{1,0:T(8,128)}, f32[64,96]{1,0:T(8,128)S(1)}, u32[]{:S(2)}, u32[]{:S(2)}) collective-permute-start(f32[64,96]{1,0:T(8,128)} %get-tuple-element.15), channel_id=1, source_target_pairs={{0,8},{2,10},{4,12},{6,14},{8,16},{9,1},{10,18},{11,3},{12,20},{13... | collective-permute-start | bytes 73736 | tf_op jit(solution)/shard_map/ppermute | solution.py:469
